TPU v7x, 32 devices: a whole 2x2x4 slice. The times are simulated.
32 devices in a mesh: row: 4 (over y, x), col: 8 (over z, core).
Axes of the slice: x: 2, y: 2, z: 4, core: 2. Of those that a mesh axis runs over, the one named last changes fastest.
Arguments:
- snapshots: float32 [4, 256, 1024], P('row', 'col'), may hold values from -6 to 6
- operator: float32 [65536, 1024], P('row', 'col'), may hold values from -0.1875 to 0.1875
Outputs:
- reduced: float32 [4, 256, 65536], P(None, 'col', 'row')
All inputs are finite; a program needn't handle non-finite values.
Results may differ from a plain program's by a relative error of at most 0.00007.
Values sent between devices are 32-bit elements; how exact they have to be, the bound alone decides.
No kernel may reach another device: no remote copies, remote signals or barrier semaphores. Data moves between devices by JAX's collectives and lax.ppermute only.
A program may use at most 192 MiB of HBM per device.

v0:
```python
import jax
import jax.numpy as jnp
from jax import lax
from jax.sharding import PartitionSpec as P


def contract(left, right):
    return lax.dot_general(
        left,
        right,
        (((1,), (1,)), ((), ())),
        precision=lax.Precision.HIGHEST,
        preferred_element_type=jnp.float32,
    )


def shards(snapshots, operator):
    modes_local = operator.shape[0]
    turned = lax.all_to_all(snapshots, "row", split_axis=2, concat_axis=0, tiled=True)
    gathered = lax.all_gather(turned, "row", axis=2, tiled=True)
    groups, times, width = gathered.shape
    snapshot_rows = gathered.reshape(groups * times, width)
    running = contract(snapshot_rows, lax.all_gather(operator, "col", axis=1, tiled=True))
    return running.reshape(groups, times, modes_local)


def solution(mesh):
    placed = (P("row", "col", None), P("row", "col"))
    return jax.shard_map(
        shards, mesh=mesh, in_specs=placed, out_specs=P(None, "col", "row"), check_vma=False
    )
```

profile of v0, /device:TPU:0, one launch (start us, length us, event | category | flops | bytes accessed | tf_op | source)
XLA Modules:
  0.0 660.8 jit_solution(17097389520366919560)
XLA Ops:
  6.5 0.0 all-gather.3.cloned.1.call-start
  6.5 0.7 all-gather.3.cloned.1.call-update
  7.3 1.1 copy.4
  8.4 0.5 broadcast
  8.9 1.9 reduce
  10.9 0.3 reshape.6
  11.1 10.0 %all_to_all.18 = f32[4,1,8192]{2,1,0:T(1,128)S(1)} all-to-all(f32[4,1,8192]{2,1,0:T(1,128)S(1)} %reshape.6), channel_id=1, replica_groups=mesh['row'=4,'col'=8] {'row'}, dimensions={0} | all-to-all | bytes 262144 | tf_op jit(solution)/shard_map/all_to_all | solution.py:19
  21.1 1.0 reduce.1
  22.1 0.8 reshape.7
  22.9 0.2 copy.6
  23.1 10.1 %all-gather = f32[4,1,32,1024]{3,2,0,1:T(8,128)S(1)} all-gather(f32[4,1,32,256]{3,2,0,1:T(8,128)S(1)} %bitcast.12), channel_id=2, replica_groups=mesh['row'=4,'col'=8] {'row'}, dimensions={3}, use_global_device_ids=true | all-gather | bytes 655360 | tf_op jit(solution)/shard_map/all_gather | solution.py:20
  33.2 546.5 %all-gather.3.cloned.1.call-done = f32[16384,1024]{1,0:T(8,128)} async-done(((f32[16384,128]{1,0:T(8,128)}), f32[16384,1024]{1,0:T(8,128)}) %all-gather.3.cloned.1.call-update) | async-done | bytes 67108880 | tf_op jit(solution)/shard_map/all_gather | solution.py:23
  579.8 74.2 %fusion = f32[4,32,16384]{2,1,0:T(8,128)} fusion(f32[16384,1024]{1,0:T(8,128)} %all-gather.3.cloned.1.call-done, f32[4,1,32,1024]{3,2,0,1:T(8,128)S(1)} %all-gather), kind=kOutput, calls=%fused_computation | convolution fusion | flops 25769803776 | bytes 76021760 | tf_op jit(solution)/shard_map/dot_general | solution.py:8
Async XLA Ops:
  6.5 573.2 %all-gather.3.cloned.1.call-start = ((), (), s32[]{:S(2)}) async-start(), calls=%async_computation.1 | async-start | bytes 75497472 | tf_op jit(solution)/shard_map/all_gather | solution.py:23
Sparse Core Ops, SparseCore 0:
  9.0 570.7 all-gather.2
where the time goes:
time: 663 us; the launch traced here: 661 us
  waiting for transfers between devices  547 us (83%)
  matrix products  74.2 us (11%)
  blocking collectives  20.1 us (3%)
  between operations  13.4 us (2%)
    all_gather x1, waiting for transfers between devices, shards(): lax.all_gather(operator, 'col', axis=1, tiled=True)  547 us
    dot_general x1, matrix products, contract(): lax.dot_general(left, right, (((1,), (1,)), ((), ())), precision=lax.Prec...  74.2 us
  transfers between devices with their start and end apart: 1, of which 1 were waited for; matrix products, arithmetic and copies ran while one was open for 1% of the time, Pallas kernels for 0%

commit v1 on v0

v1 whole, which is shorter than its diff:
```python
import functools

import jax
import jax.numpy as jnp
from jax import lax
from jax.experimental import pallas as pl
from jax.experimental.pallas import tpu as pltpu
from jax.sharding import PartitionSpec as P

CORES = 2
PARTS = 4
BLOCK = 512


def split(x):
    high = x.astype(jnp.bfloat16)
    low = (x - high.astype(jnp.float32)).astype(jnp.bfloat16)
    return high, low


def dot(left, right):
    return lax.dot_general(
        left, right, (((1,), (1,)), ((), ())), preferred_element_type=jnp.float32
    )


def product_kernel(rows_ref, *refs):
    pieces, out_ref, high_ref, low_ref = refs[:-3], refs[-3], refs[-2], refs[-1]

    @pl.when(pl.program_id(0) == 0)
    def _():
        high, low = split(rows_ref[...])
        high_ref[...] = high
        low_ref[...] = low

    modes = [piece[...] for piece in pieces]
    high, low = split(modes[0] if len(modes) == 1 else jnp.concatenate(modes, axis=1))
    row_high = high_ref[...]
    out_ref[...] = dot(row_high, high) + (dot(row_high, low) + dot(low_ref[...], high))


def product(rows, pieces):
    if pieces[0].shape[1] % 128:
        pieces = [jnp.concatenate(pieces, axis=1)]
    height, depth = rows.shape
    modes = pieces[0].shape[0]
    block = min(BLOCK, modes)
    return pl.pallas_call(
        product_kernel,
        grid=(modes // block,),
        in_specs=[pl.BlockSpec((height, depth), lambda i: (0, 0))]
        + [pl.BlockSpec((block, piece.shape[1]), lambda i: (i, 0)) for piece in pieces],
        out_specs=pl.BlockSpec((height, block), lambda i: (0, i)),
        out_shape=jax.ShapeDtypeStruct((height, modes), jnp.float32),
        scratch_shapes=[pltpu.VMEM((height, depth), jnp.bfloat16)] * 2,
        compiler_params=pltpu.CompilerParams(vmem_limit_bytes=48 * 2**20),
        cost_estimate=pl.CostEstimate(
            flops=6 * height * depth * modes,
            bytes_accessed=4 * (height * depth + depth * modes + height * modes),
            transcendentals=0,
        ),
    )(rows, *pieces)


def shards(snapshots, operator):
    chips = lax.axis_size("col") // CORES
    half = chips // 2
    modes, width = operator.shape
    col = lax.axis_index("col")
    chip, core = col // CORES, col % CORES
    side = (chip >= half).astype(jnp.int32)
    place = jnp.where(side == 0, half - 1 - chip, chip - half)

    def at(side, place):
        return (half - 1 - place) + side * (2 * place + 1)

    def move(x, routes):
        pairs = [
            (at(a, i) * CORES + c, at(b, j) * CORES + c)
            for (a, i), (b, j) in routes
            for c in range(CORES)
        ]
        return lax.ppermute(x, "col", pairs)

    def inward(x, i):
        return move(x, [((s, i), (s, 0)) for s in range(2)])

    def outward(x, i):
        return move(x, [((s, 0), (s, i)) for s in range(2)])

    def across(x, i=0):
        return move(x, [((s, 0), (1 - s, i)) for s in range(2)])

    def turn(x, i):
        return move(x, [((s, j), (s, (j + i) % half)) for s in range(2) for j in range(half)])

    def swap(x):
        pairs = [(q * CORES + c, q * CORES + 1 - c) for q in range(chips) for c in range(CORES)]
        return lax.ppermute(x, "col", pairs)

    times = snapshots.shape[1]
    flat = lax.all_gather(snapshots, "col", axis=1, tiled=True)
    flat = lax.all_gather(flat, "row", axis=0, tiled=True)
    groups = flat.shape[0]
    height = groups * times

    def rows_of(chip, core):
        block = lax.dynamic_slice_in_dim(flat, (chip * CORES + core) * times, times, axis=1)
        return block.reshape(height, flat.shape[2])

    def columns_of(rows, chip):
        return lax.dynamic_slice_in_dim(rows, (chip * CORES + core) * width, width, axis=1)

    def left_side(row_chips, column_chips):
        rows = jnp.concatenate([rows_of(q, e) for e in (core, 1 - core) for q in row_chips], axis=0)
        return [columns_of(rows, q) for q in column_chips]

    mine = [at(side, (place + i) % half) for i in range(half)]
    others = [at(1 - side, i) for i in range(half)]
    rows_a = left_side(mine, mine + others)
    for i in range(1, half):
        own = (jnp.arange(CORES * half * height) // height) % half == i
        rows_a[i] = jnp.where(own[:, None], 0.0, rows_a[i])
    rows_a = jnp.concatenate(rows_a, axis=1)
    rows_b = left_side(
        [mine[0]] + others, [at(side, (place - i + half) % half) for i in range(half)]
    )
    rows_b = jnp.concatenate(rows_b, axis=1)

    part = modes // PARTS
    count = PARTS - 1
    last = modes - count * part
    chunk = [operator[k * part : (k + 1) * part] for k in range(count)]
    tail = operator[count * part :]

    hub = across(operator[: count * part])
    inner = [[inward(chunk[k], i) for i in range(1, half)] for k in range(count)]
    pieces_b = [tail] + [turn(tail, i) for i in range(1, half)]
    outer = [[across(x) for x in inner[k]] for k in range(count)]

    sums_b = product(rows_b, pieces_b)
    sums_b = sums_b.reshape(CORES, 1 + half, height, last)
    sums_b = sums_b[0] + swap(sums_b[1])
    total_b = sums_b[0]

    out = jnp.zeros((height, modes), jnp.float32)
    for k in range(count):
        pieces = [chunk[k]] + inner[k] + [hub[k * part : (k + 1) * part]] + outer[k]
        sums = product(rows_a, pieces).reshape(CORES, half, height, part)
        sums = sums[0] + swap(sums[1])
        total = sums[0]
        for i in range(1, half):
            total = total + outward(sums[i], i)
        out = lax.dynamic_update_slice(out, total, (0, k * part))

    for i in reversed(range(half)):
        total_b = total_b + across(sums_b[1 + i], i)
    out = lax.dynamic_update_slice(out, total_b, (0, count * part))
    return out.reshape(groups, times, modes)


def solution(mesh):
    placed = (P("row", "col", None), P("row", "col"))
    return jax.shard_map(
        shards, mesh=mesh, in_specs=placed, out_specs=P(None, "col", "row"), check_vma=False
    )
```

time: 663 us -> 516 us (0.78)
  waiting for transfers between devices: 547 us -> 343 us
  matrix products: 74.2 us -> 0 us
  local copies, waits for them, and re-layouts: 2.89 us -> 64.2 us
  Pallas kernels: 0 us -> 47.4 us
  starting transfers between devices: 0.01 us -> 29.4 us
  blocking collectives: 20.1 us -> 0 us
  other arithmetic: 2.94 us -> 16.5 us
    all_gather x1 -> x2, waiting for transfers between devices: 547 us -> 21.6 us  [the longest x1 21.6 us: shards(): flat = lax.all_gather(snapshots, 'col', axis=1, tiled=True)]
    ppermute x0 -> x17, waiting for transfers between devices: none -> 321 us  [the longest x13 321 us: move(): return lax.ppermute(x, 'col', pairs)]
    dot_general x1 -> x0, matrix products: 74.2 us -> none  [contract(): lax.dot_general(left, right, (((1,), (1,)), ((), ())), precision=lax.Prec...]
    slice x0 -> x7, local copies, waits for them, and re-layouts: none -> 49 us  [the longest x3 21.8 us: shards(): sums = sums[0] + swap(sums[1])]
    pallas_call x0 -> x4, Pallas kernels: none -> 47.4 us  [product(): pl.pallas_call(product_kernel, grid=(modes // block,), in_specs=[pl.Block...]
    ppermute x0 -> x17, starting transfers between devices: none -> 29.4 us  [the longest x13 28.4 us: move(): return lax.ppermute(x, 'col', pairs)]
    add x0 -> x5, other arithmetic: none -> 11.8 us  [the longest x3 6.18 us: shards(): sums = sums[0] + swap(sums[1])]
    all_gather x1 -> x0, blocking collectives: 10.1 us -> none  [shards(): gathered = lax.all_gather(turned, 'row', axis=2, tiled=True)]
  transfers between devices with their start and end apart: 1 -> 19, of which waited for: 1 -> 7; matrix products, arithmetic and copies ran while one was open for 1% -> 14% of each run, Pallas kernels for 0% -> 9%
where the time goes in v1:
time: 516 us; the launch traced here: 514 us
  waiting for transfers between devices  343 us (66%)
  local copies, waits for them, and re-layouts  64.2 us (12%)
  Pallas kernels  47.4 us (9%)
  starting transfers between devices  29.4 us (6%)
  other arithmetic  16.5 us (3%)
  between operations  13.8 us (3%)
    ppermute x13, waiting for transfers between devices, move(): return lax.ppermute(x, 'col', pairs)  321 us
    pallas_call x4, Pallas kernels, product(): pl.pallas_call(product_kernel, grid=(modes // block,), in_specs=[pl.Block...  47.4 us
    ppermute x13, starting transfers between devices, move(): return lax.ppermute(x, 'col', pairs)  28.4 us
    slice x3, local copies, waits for them, and re-layouts, shards(): sums = sums[0] + swap(sums[1])  21.8 us
    all_gather x1, waiting for transfers between devices, shards(): flat = lax.all_gather(snapshots, 'col', axis=1, tiled=True)  21.6 us
    slice x1, local copies, waits for them, and re-layouts, shards(): sums_b = sums_b[0] + swap(sums_b[1])  10.7 us
  transfers between devices with their start and end apart: 19, of which 7 were waited for; matrix products, arithmetic and copies ran while one was open for 14% of the time, Pallas kernels for 9%

profile of v1, /device:TPU:0, one launch (start us, length us, event | category | flops | bytes accessed | tf_op | source)
XLA Modules:
  0.0 514.5 jit_solution(1721505213568486624)
XLA Ops:
  6.5 0.7 all-gather.3.cloned.1.call-update
  7.3 4.8 slice.84
  12.1 3.3 collective-permute-start.1
  15.4 21.6 %all-gather.3.cloned.1.call-done = f32[1,256,1024]{2,1,0:T(8,128)} async-done(((f32[1,32,1024]{2,1,0:T(8,128)}), f32[1,256,1024]{2,1,0:T(8,128)}) %all-gather.3.cloned.1.call-update) | async-done | bytes 1048592 | tf_op jit(solution)/shard_map/all_gather | solution.py:102
  37.1 6.0 %fusion.14 = (f32[4096,128]{1,0:T(8,128)}, f32[4096,128]{1,0:T(8,128)}, f32[4096,128]{1,0:T(8,128)S(1)}, f32[4096,128]{1,0:T(8,128)S(1)}) fusion(f32[16384,128]{1,0:T(8,128)} %param.3), kind=kLoop, calls=%fused_computation.53 | loop fusion | bytes 16777216 | tf_op jit(solution)/shard_map/slice | solution.py:134
  43.1 3.7 collective-permute-start
  46.8 1.3 copy-done
  48.1 2.6 collective-permute-start.5
  50.7 2.6 collective-permute-start.9
  53.3 38.0 %collective-permute-done.refs_1_ = f32[4096,128]{1,0:T(8,128)} collective-permute-done((f32[4096,128]{1,0:T(8,128)S(1)}, f32[4096,128]{1,0:T(8,128)}, u32[]{:S(2)}, u32[]{:S(2)}) %collective-permute-start) | collective-permute-done | bytes 2097184 | tf_op jit(solution)/shard_map/ppermute | solution.py:83
  91.4 2.1 collective-permute-start.2
  93.4 3.4 collective-permute-start.13
  96.9 39.5 %collective-permute-done.5.refs_1_ = f32[4096,128]{1,0:T(8,128)} collective-permute-done((f32[4096,128]{1,0:T(8,128)}, f32[4096,128]{1,0:T(8,128)}, u32[]{:S(2)}, u32[]{:S(2)}) %collective-permute-start.5) | collective-permute-done | bytes 2097184 | tf_op jit(solution)/shard_map/ppermute | solution.py:83
  136.4 2.0 collective-permute-start.6
  138.4 42.9 %collective-permute-done.9.refs_1_ = f32[4096,128]{1,0:T(8,128)} collective-permute-done((f32[4096,128]{1,0:T(8,128)S(1)}, f32[4096,128]{1,0:T(8,128)}, u32[]{:S(2)}, u32[]{:S(2)}) %collective-permute-start.9) | collective-permute-done | bytes 2097184 | tf_op jit(solution)/shard_map/ppermute | solution.py:83
  181.2 2.0 collective-permute-start.10
  183.2 5.6 %fusion.18 = (f32[4096,128]{1,0:T(8,128)}, f32[4096,128]{1,0:T(8,128)}, f32[4096,128]{1,0:T(8,128)}) fusion(f32[12288,128]{1,0:T(8,128)} %collective-permute-done.1), kind=kLoop, calls=%fused_computation.57 | loop fusion | bytes 12582912 | tf_op jit(solution)/shard_map/slice | solution.py:148
  188.9 2.7 constant_dynamic-slice_fusion.2
  192.1 1.3 copy-done.1
  193.4 12.0 %shard_map.28 = f32[512,4096]{1,0:T(8,128)} custom-call(f32[512,512]{1,0:T(8,128)S(1)} %pad_maximum_fusion.1.rows_ref, f32[4096,128]{1,0:T(8,128)S(1)} %copy-done.1, f32[4096,128]{1,0:T(8,128)} %collective-permute-done.refs_1_, f32[4096,128]{1,0:T(8,128)} %get-tuple-element.21.refs_2_, f32[4096,128]{1,0:T(8,128)} %collective-permute-done.2.refs_3_), custom_call_target="tpu_custom_call" | custom-call | flops 6442450944 | bytes 17825792 | tf_op jit(solution)/shard_map/pallas_call | solution.py:48
  205.4 7.7 %fusion.17 = (f32[256,4096]{1,0:T(8,128)}, f32[256,4096]{1,0:T(8,128)}) fusion(f32[512,4096]{1,0:T(8,128)} %shard_map.28), kind=kLoop, calls=%fused_computation.56 | loop fusion | bytes 16777216 | tf_op jit(solution)/shard_map/slice | solution.py:150
  213.1 12.4 %shard_map.29 = f32[512,4096]{1,0:T(8,128)} custom-call(f32[512,512]{1,0:T(8,128)S(1)} %pad_maximum_fusion.1.rows_ref, f32[4096,128]{1,0:T(8,128)} %get-tuple-element.8.refs_0_, f32[4096,128]{1,0:T(8,128)} %collective-permute-done.5.refs_1_, f32[4096,128]{1,0:T(8,128)} %get-tuple-element.20.refs_2_, f32[4096,128]{1,0:T(8,128)} %collective-permute-done.6.refs_3_), custom_call_target="tpu_custom_call" | custom-call | flops 6442450944 | bytes 17825792 | tf_op jit(solution)/shard_map/pallas_call | solution.py:48
  225.5 7.7 %fusion.16 = (f32[256,4096]{1,0:T(8,128)}, f32[256,4096]{1,0:T(8,128)}) fusion(f32[512,4096]{1,0:T(8,128)} %shard_map.29), kind=kLoop, calls=%fused_computation.55 | loop fusion | bytes 16777216 | tf_op jit(solution)/shard_map/slice | solution.py:150
  233.2 0.5 collective-permute-start.7
  234.2 11.1 %shard_map.31 = f32[768,4096]{1,0:T(8,128)} custom-call(f32[768,256]{1,0:T(8,128)S(1)} %pad_maximum_fusion.2.rows_ref, f32[4096,128]{1,0:T(8,128)} %get-tuple-element.7.refs_0_, f32[4096,128]{1,0:T(8,128)} %collective-permute-done.13.refs_1_), custom_call_target="tpu_custom_call" | custom-call | flops 4831838208 | bytes 17563648 | tf_op jit(solution)/shard_map/pallas_call | solution.py:48
  245.3 10.7 %fusion.13 = (f32[384,4096]{1,0:T(8,128)}, f32[384,4096]{1,0:T(8,128)}) fusion(f32[768,4096]{1,0:T(8,128)} %shard_map.31), kind=kLoop, calls=%fused_computation.52 | loop fusion | bytes 25165824 | tf_op jit(solution)/shard_map/slice | solution.py:143
  256.0 12.0 %shard_map.30 = f32[512,4096]{1,0:T(8,128)} custom-call(f32[512,512]{1,0:T(8,128)S(1)} %pad_maximum_fusion.1.rows_ref, f32[4096,128]{1,0:T(8,128)S(1)} %get-tuple-element.10.refs_0_, f32[4096,128]{1,0:T(8,128)} %collective-permute-done.9.refs_1_, f32[4096,128]{1,0:T(8,128)} %get-tuple-element.19.refs_2_, f32[4096,128]{1,0:T(8,128)} %collective-permute-done.10.refs_3_), custom_call_target="tpu_custom_call" | custom-call | flops 6442450944 | bytes 17825792 | tf_op jit(solution)/shard_map/pallas_call | solution.py:48
  268.0 6.4 %fusion.15 = (f32[256,4096]{1,0:T(8,128)S(1)}, f32[256,4096]{1,0:T(8,128)}) fusion(f32[512,4096]{1,0:T(8,128)} %shard_map.30), kind=kLoop, calls=%fused_computation.54 | loop fusion | bytes 16777216 | tf_op jit(solution)/shard_map/slice | solution.py:150
  274.9 2.8 add.194
  277.8 1.6 collective-permute-start.4
  279.9 2.8 add.196
  282.6 1.5 slice_bitcast_fusion.5
  284.1 1.7 collective-permute-start.8
  285.9 1.2 copy-done.8
  287.0 0.6 add.198
  287.7 1.5 slice_bitcast_fusion.3
  289.2 1.3 collective-permute-start.12
  290.5 3.8 add.212
  294.8 0.8 collective-permute-start.16
  295.6 1.3 collective-permute-start.15
  296.9 70.4 %collective-permute-done.4 = f32[128,4096]{1,0:T(8,128)} collective-permute-done((f32[128,4096]{1,0:T(8,128)S(1)}, f32[128,4096]{1,0:T(8,128)}, u32[]{:S(2)}, u32[]{:S(2)}) %collective-permute-start.4) | collective-permute-done | bytes 2097184 | tf_op jit(solution)/shard_map/ppermute | solution.py:83
  367.3 1.9 fusion.7
  369.2 0.9 dynamic_update_slice.12
  370.0 87.1 %collective-permute-done.8 = f32[128,4096]{1,0:T(8,128)} collective-permute-done((f32[128,4096]{1,0:T(8,128)}, f32[128,4096]{1,0:T(8,128)}, u32[]{:S(2)}, u32[]{:S(2)}) %collective-permute-start.8) | collective-permute-done | bytes 2097184 | tf_op jit(solution)/shard_map/ppermute | solution.py:83
  457.2 1.9 fusion.6
  459.1 42.9 %collective-permute-done.12 = f32[128,4096]{1,0:T(8,128)} collective-permute-done((f32[128,4096]{1,0:T(8,128)}, f32[128,4096]{1,0:T(8,128)}, u32[]{:S(2)}, u32[]{:S(2)}) %collective-permute-start.12) | collective-permute-done | bytes 2097184 | tf_op jit(solution)/shard_map/ppermute | solution.py:83
  501.9 1.9 fusion.4
  504.3 3.4 copy-done.9
  (54 shorter events, 3.0 us)
Async XLA Ops:
  6.5 30.5 %all-gather.3.cloned.1.call-start = ((), (), s32[]{:S(2)}) async-start(), calls=%async_computation | async-start | bytes 1179648 | tf_op jit(solution)/shard_map/all_gather | solution.py:102
  7.3 181.6 %all-gather.5.cloned.1.call-start = ((), (), s32[]{:S(2)}) async-start(), calls=%async_computation.1 | async-start | bytes 5242880 | tf_op jit(solution)/shard_map/all_gather | solution.py:103
  12.1 171.1 %collective-permute-start.1 = (f32[12288,128]{1,0:T(8,128)}, f32[12288,128]{1,0:T(8,128)}, u32[]{:S(2)}, u32[]{:S(2)}) collective-permute-start(f32[12288,128]{1,0:T(8,128)} %slice.84), channel_id=1, source_target_pairs={{2,4},{3,5},{4,2},{5,3},{10,12},{11,13},{12,10},{13,11},{18,20},{1... | collective-permute-start | bytes 18874376 | tf_op jit(solution)/shard_map/ppermute | solution.py:83
  43.1 48.2 %collective-permute-start = (f32[4096,128]{1,0:T(8,128)S(1)}, f32[4096,128]{1,0:T(8,128)}, u32[]{:S(2)}, u32[]{:S(2)}) collective-permute-start(f32[4096,128]{1,0:T(8,128)S(1)} %get-tuple-element.9.refs_0_), channel_id=1, source_target_pairs={{0,2},{1,3},{6,4},{7,5},{8,10},{9,11},{14,12},{15,13},{16,18},{17,... | collective-permute-start | bytes 6291464 | tf_op jit(solution)/shard_map/ppermute | solution.py:83
  46.8 1.3 copy-start
  48.1 88.3 %collective-permute-start.5 = (f32[4096,128]{1,0:T(8,128)}, f32[4096,128]{1,0:T(8,128)}, u32[]{:S(2)}, u32[]{:S(2)}) collective-permute-start(f32[4096,128]{1,0:T(8,128)} %get-tuple-element.8.refs_0_), channel_id=1, source_target_pairs={{0,2},{1,3},{6,4},{7,5},{8,10},{9,11},{14,12},{15,13},{16,18},{17,... | collective-permute-start | bytes 6291464 | tf_op jit(solution)/shard_map/ppermute | solution.py:83
  50.7 130.5 %collective-permute-start.9 = (f32[4096,128]{1,0:T(8,128)S(1)}, f32[4096,128]{1,0:T(8,128)}, u32[]{:S(2)}, u32[]{:S(2)}) collective-permute-start(f32[4096,128]{1,0:T(8,128)S(1)} %get-tuple-element.10.refs_0_), channel_id=1, source_target_pairs={{0,2},{1,3},{6,4},{7,5},{8,10},{9,11},{14,12},{15,13},{16,18},{17,... | collective-permute-start | bytes 6291464 | tf_op jit(solution)/shard_map/ppermute | solution.py:83
  91.4 100.7 %collective-permute-start.2 = (f32[4096,128]{1,0:T(8,128)}, f32[4096,128]{1,0:T(8,128)}, u32[]{:S(2)}, u32[]{:S(2)}) collective-permute-start(f32[4096,128]{1,0:T(8,128)} %collective-permute-done.refs_1_), channel_id=1, source_target_pairs={{2,4},{3,5},{4,2},{5,3},{10,12},{11,13},{12,10},{13,11},{18,20},{1... | collective-permute-start | bytes 6291464 | tf_op jit(solution)/shard_map/ppermute | solution.py:83
  93.4 140.7 %collective-permute-start.13 = (f32[4096,128]{1,0:T(8,128)}, f32[4096,128]{1,0:T(8,128)}, u32[]{:S(2)}, u32[]{:S(2)}) collective-permute-start(f32[4096,128]{1,0:T(8,128)} %get-tuple-element.7.refs_0_), channel_id=1, source_target_pairs={{2,0},{3,1},{0,2},{1,3},{4,6},{5,7},{6,4},{7,5},{10,8},{11,9},{8,1... | collective-permute-start | bytes 6291464 | tf_op jit(solution)/shard_map/ppermute | solution.py:83
  136.4 76.7 %collective-permute-start.6 = (f32[4096,128]{1,0:T(8,128)}, f32[4096,128]{1,0:T(8,128)}, u32[]{:S(2)}, u32[]{:S(2)}) collective-permute-start(f32[4096,128]{1,0:T(8,128)} %collective-permute-done.5.refs_1_), channel_id=1, source_target_pairs={{2,4},{3,5},{4,2},{5,3},{10,12},{11,13},{12,10},{13,11},{18,20},{1... | collective-permute-start | bytes 6291464 | tf_op jit(solution)/shard_map/ppermute | solution.py:83
  181.2 74.8 %collective-permute-start.10 = (f32[4096,128]{1,0:T(8,128)}, f32[4096,128]{1,0:T(8,128)}, u32[]{:S(2)}, u32[]{:S(2)}) collective-permute-start(f32[4096,128]{1,0:T(8,128)} %collective-permute-done.9.refs_1_), channel_id=1, source_target_pairs={{2,4},{3,5},{4,2},{5,3},{10,12},{11,13},{12,10},{13,11},{18,20},{1... | collective-permute-start | bytes 6291464 | tf_op jit(solution)/shard_map/ppermute | solution.py:83
  191.8 1.6 copy-start.1
  213.1 61.8 %collective-permute-start.3 = (f32[2,128,4096]{2,1,0:T(8,128)}, f32[2,128,4096]{2,1,0:T(8,128)}, u32[]{:S(2)}, u32[]{:S(2)}) collective-permute-start(f32[2,128,4096]{2,1,0:T(8,128)} %bitcast.5), channel_id=1, source_target_pairs={{0,1},{1,0},{2,3},{3,2},{4,5},{5,4},{6,7},{7,6},{8,9},{9,8},{10,11... | collective-permute-start | bytes 12582920 | tf_op jit(solution)/shard_map/ppermute | solution.py:99
  233.2 46.2 %collective-permute-start.7 = (f32[2,128,4096]{2,1,0:T(8,128)}, f32[2,128,4096]{2,1,0:T(8,128)}, u32[]{:S(2)}, u32[]{:S(2)}) collective-permute-start(f32[2,128,4096]{2,1,0:T(8,128)} %bitcast.9), channel_id=1, source_target_pairs={{0,1},{1,0},{2,3},{3,2},{4,5},{5,4},{6,7},{7,6},{8,9},{9,8},{10,11... | collective-permute-start | bytes 12582920 | tf_op jit(solution)/shard_map/ppermute | solution.py:99
  256.0 34.5 %collective-permute-start.14 = (f32[3,128,4096]{2,1,0:T(8,128)}, f32[3,128,4096]{2,1,0:T(8,128)}, u32[]{:S(2)}, u32[]{:S(2)}) collective-permute-start(f32[3,128,4096]{2,1,0:T(8,128)} %bitcast.57), channel_id=1, source_target_pairs={{0,1},{1,0},{2,3},{3,2},{4,5},{5,4},{6,7},{7,6},{8,9},{9,8},{10,11... | collective-permute-start | bytes 18874376 | tf_op jit(solution)/shard_map/ppermute | solution.py:99
  268.0 6.9 %copy-start.6 = (f32[256,4096]{1,0:T(8,128)S(1)}, f32[256,4096]{1,0:T(8,128)}, u32[]{:S(2)}) copy-start(f32[256,4096]{1,0:T(8,128)} %get-tuple-element.16) | copy-start | bytes 12582916
  274.4 11.5 %collective-permute-start.11 = (f32[2,128,4096]{2,1,0:T(8,128)S(1)}, f32[2,128,4096]{2,1,0:T(8,128)S(1)}, u32[]{:S(2)}, u32[]{:S(2)}) collective-permute-start(f32[2,128,4096]{2,1,0:T(8,128)S(1)} %bitcast.62), channel_id=1, source_target_pairs={{0,1},{1,0},{2,3},{3,2},{4,5},{5,4},{6,7},{7,6},{8,9},{9,8},{10,11... | collective-permute-start | bytes 12582920 | tf_op jit(solution)/shard_map/ppermute | solution.py:99
  277.7 2.2 copy-start.7
  277.8 89.5 %collective-permute-start.4 = (f32[128,4096]{1,0:T(8,128)S(1)}, f32[128,4096]{1,0:T(8,128)}, u32[]{:S(2)}, u32[]{:S(2)}) collective-permute-start(f32[128,4096]{1,0:T(8,128)S(1)} %slice_bitcast_fusion.7), channel_id=1, source_target_pairs={{2,0},{3,1},{4,6},{5,7},{10,8},{11,9},{12,14},{13,15},{18,16},{19,... | collective-permute-start | bytes 6291464 | tf_op jit(solution)/shard_map/ppermute | solution.py:83
  282.6 5.1 copy-start.2
  282.6 4.4 copy-start.8
  284.1 173.1 %collective-permute-start.8 = (f32[128,4096]{1,0:T(8,128)}, f32[128,4096]{1,0:T(8,128)}, u32[]{:S(2)}, u32[]{:S(2)}) collective-permute-start(f32[128,4096]{1,0:T(8,128)} %slice_bitcast_fusion.5), channel_id=1, source_target_pairs={{2,0},{3,1},{4,6},{5,7},{10,8},{11,9},{12,14},{13,15},{18,16},{19,... | collective-permute-start | bytes 6291464 | tf_op jit(solution)/shard_map/ppermute | solution.py:83
  285.9 4.7 slice-start
  287.0 3.5 slice-start.1
  287.7 2.8 copy-start.4
  289.2 212.7 %collective-permute-start.12 = (f32[128,4096]{1,0:T(8,128)}, f32[128,4096]{1,0:T(8,128)}, u32[]{:S(2)}, u32[]{:S(2)}) collective-permute-start(f32[128,4096]{1,0:T(8,128)} %slice_bitcast_fusion.3), channel_id=1, source_target_pairs={{2,0},{3,1},{4,6},{5,7},{10,8},{11,9},{12,14},{13,15},{18,16},{19,... | collective-permute-start | bytes 6291464 | tf_op jit(solution)/shard_map/ppermute | solution.py:83
  294.8 209.0 %collective-permute-start.16 = (f32[128,4096]{1,0:T(8,128)S(1)}, f32[128,4096]{1,0:T(8,128)S(1)}, u32[]{:S(2)}, u32[]{:S(2)}) collective-permute-start(f32[128,4096]{1,0:T(8,128)S(1)} %get-tuple-element.18), channel_id=1, source_target_pairs={{2,4},{3,5},{4,2},{5,3},{10,12},{11,13},{12,10},{13,11},{18,20},{1... | collective-permute-start | bytes 6291464 | tf_op jit(solution)/shard_map/ppermute | solution.py:83
  295.6 208.3 %collective-permute-start.15 = (f32[128,4096]{1,0:T(8,128)S(1)}, f32[128,4096]{1,0:T(8,128)S(1)}, u32[]{:S(2)}, u32[]{:S(2)}) collective-permute-start(f32[128,4096]{1,0:T(8,128)S(1)} %get-tuple-element.17), channel_id=1, source_target_pairs={{2,6},{3,7},{4,0},{5,1},{10,14},{11,15},{12,8},{13,9},{18,22},{19,... | collective-permute-start | bytes 6291464 | tf_op jit(solution)/shard_map/ppermute | solution.py:83
  369.1 88.0 %copy-start.3 = (f32[2,128,4096]{2,1,0:T(8,128)S(1)}, f32[2,128,4096]{2,1,0:T(8,128)}, u32[]{:S(2)}) copy-start(f32[2,128,4096]{2,1,0:T(8,128)} %copy-done.2) | copy-start | bytes 12582916
  370.0 131.9 %copy-start.5 = (f32[2,128,4096]{2,1,0:T(8,128)S(1)}, f32[2,128,4096]{2,1,0:T(8,128)}, u32[]{:S(2)}) copy-start(f32[2,128,4096]{2,1,0:T(8,128)} %copy-done.4) | copy-start | bytes 12582916
  504.3 3.4 copy-start.9
Sparse Core Ops, SparseCore 0:
  9.0 28.0 all-gather.2
  38.9 51.7 all-gather.4

commit v2 on v0

v2 whole, which is shorter than its diff:
```python
import math

import jax
import jax.numpy as jnp
from jax import lax
from jax.experimental import pallas as pl
from jax.experimental.pallas import tpu as pltpu
from jax.sharding import PartitionSpec as P

CORES = 2
BLOCK = 512
SIXTEENTHS = (4, 4, 4, 4)


def after(x, *others):
    return lax.optimization_barrier((x, *others))[0]


def split(x):
    high = x.astype(jnp.bfloat16)
    low = (x - high.astype(jnp.float32)).astype(jnp.bfloat16)
    return high, low


def dot(left, right):
    return lax.dot_general(
        left, right, (((1,), (1,)), ((), ())), preferred_element_type=jnp.float32
    )


def arrange(lines, owners, blocks, places, width):
    _, groups, times, depth = lines[0].shape
    step = groups * times
    height = step * len(lines)
    count, slots = places.shape

    def kernel(owners_ref, blocks_ref, places_ref, *refs):
        high_ref, low_ref = refs[-2:]
        row = pl.program_id(0)
        for i, line_ref in enumerate(refs[:-2]):
            span = pl.ds(pl.multiple_of(owners_ref[i] * step, step), step)
            for slot in range(slots):
                at = places_ref[row * slots + slot]
                start = pl.multiple_of(jnp.maximum(at, 0) * width, width)
                part = line_ref[0, :, :, pl.ds(start, width)].reshape(step, width)
                high, low = split(jnp.where(at < 0, 0.0, part))
                high_ref[span, slot * width : (slot + 1) * width] = high
                low_ref[span, slot * width : (slot + 1) * width] = low

    shape = jax.ShapeDtypeStruct((count * height, slots * width), jnp.bfloat16)
    return pl.pallas_call(
        kernel,
        grid_spec=pltpu.PrefetchScalarGridSpec(
            num_scalar_prefetch=3,
            grid=(count,),
            in_specs=[
                pl.BlockSpec(
                    (1, groups, times, depth), lambda i, owners, blocks, places: (blocks[i], 0, 0, 0)
                )
                for _ in lines
            ],
            out_specs=[
                pl.BlockSpec((height, slots * width), lambda i, owners, blocks, places: (i, 0))
            ]
            * 2,
        ),
        out_shape=[shape, shape],
        cost_estimate=pl.CostEstimate(flops=0, bytes_accessed=0, transcendentals=0),
    )(owners, blocks, places.reshape(-1), *lines)


def product(rows, pieces, modes, heights):
    depth = rows[0].shape[1]
    height = sum(heights)
    block = math.gcd(BLOCK, modes, *(start for _, start in pieces))
    count = len(pieces)

    def kernel(high_ref, low_ref, *refs):
        parts = [piece[...] for piece in refs[:count]]
        high, low = split(parts[0] if count == 1 else jnp.concatenate(parts, axis=1))
        at = 0
        for out_ref in refs[count:]:
            span = pl.ds(at, out_ref.shape[0])
            row_high = high_ref[span, :]
            out_ref[...] = dot(row_high, high) + (dot(row_high, low) + dot(low_ref[span, :], high))
            at += out_ref.shape[0]

    return pl.pallas_call(
        kernel,
        grid=(modes // block,),
        in_specs=[pl.BlockSpec((height, depth), lambda i: (0, 0))] * 2
        + [
            pl.BlockSpec((block, x.shape[1]), lambda i, first=start // block: (first + i, 0))
            for x, start in pieces
        ],
        out_specs=[pl.BlockSpec((h, block), lambda i: (0, i)) for h in heights],
        out_shape=[jax.ShapeDtypeStruct((h, modes), jnp.float32) for h in heights],
        compiler_params=pltpu.CompilerParams(vmem_limit_bytes=48 * 2**20),
        cost_estimate=pl.CostEstimate(flops=0, bytes_accessed=0, transcendentals=0),
    )(*rows, *(x for x, _ in pieces))


def put(out, parts, start, modes):
    height, span = parts[0].shape
    block = math.gcd(math.gcd(4 * BLOCK, span), start or span)
    first = start // block
    count = len(parts)

    def kernel(*refs):
        value = refs[0][...]
        for ref in refs[1:count]:
            value = value + ref[...]
        refs[-1][...] = value

    operands = list(parts)
    in_specs = [pl.BlockSpec((height, block), lambda i: (0, i)) for _ in parts]
    if out is not None:
        operands.append(out)
        in_specs.append(pl.BlockSpec(memory_space=pltpu.HBM))
    return pl.pallas_call(
        kernel,
        grid=(span // block,),
        in_specs=in_specs,
        out_specs=pl.BlockSpec((height, block), lambda i: (0, first + i)),
        out_shape=jax.ShapeDtypeStruct((height, modes), jnp.float32),
        input_output_aliases={} if out is None else {count: 0},
        compiler_params=pltpu.CompilerParams(vmem_limit_bytes=48 * 2**20),
        cost_estimate=pl.CostEstimate(flops=0, bytes_accessed=0, transcendentals=0),
    )(*operands)


def shards(snapshots, operator):
    chips = lax.axis_size("col") // CORES
    half = chips // 2
    modes, width = operator.shape
    col = lax.axis_index("col")
    chip, core = lax.div(col, CORES), lax.rem(col, CORES)
    side = (chip >= half).astype(jnp.int32)
    place = jnp.where(side == 0, half - 1 - chip, chip - half)

    def at(side, place):
        return (half - 1 - place) + side * (2 * place + 1)

    def move(x, routes, cross=0):
        pairs = [
            (at(a, i) * CORES + c, at(b, j) * CORES + (c + cross) % CORES)
            for (a, i), (b, j) in routes
            for c in range(CORES)
        ]
        return lax.ppermute(x, "col", pairs)

    def inward(x, i):
        return move(x, [((s, i), (s, 0)) for s in range(2)])

    def outward(x, i, cross=0):
        return move(x, [((s, 0), (s, i)) for s in range(2)], cross)

    def across(x, i=0, cross=0):
        return move(x, [((s, 0), (1 - s, i)) for s in range(2)], cross)

    def far(x, i):
        return move(x, [((s, i), (1 - s, 0)) for s in range(2)])

    def turn(x, i):
        return move(x, [((s, j), (s, (j + i) % half)) for s in range(2) for j in range(half)])

    def swap(x):
        return move(x, [((s, j), (s, j)) for s in range(2) for j in range(half)], 1)

    edges = [0]
    for part in SIXTEENTHS:
        edges.append(edges[-1] + modes * part // sum(SIXTEENTHS))
    count = len(SIXTEENTHS)
    spokes = range(1, half)
    chunk = [operator[edges[k] : edges[k + 1]] for k in range(2)]

    def pair(x):
        if width % 128 == 0:
            return [(x, 0), (swap(x), 0)]
        other = swap(x)
        ends = jnp.where(core == 0, x, other), jnp.where(core == 0, other, x)
        return [(jnp.concatenate(ends, axis=1), 0)]

    def places_of(chips):
        if width % 128 == 0:
            return [q * CORES + e if q is not None else -1 for q in chips for e in (core, 1 - core)]
        return [-1 if q is None else q for q in chips]

    hub = across(chunk[0])
    first = [turn(chunk[1], i) for i in spokes]
    outer = [far(chunk[0], i) for i in spokes]
    rest = after(operator, hub)
    chunk += [rest[edges[k] : edges[k + 1]] for k in range(2, count)]
    if width % 128 == 0:
        other = swap(operator)
        own = [[(operator, edges[k]), (other, edges[k])] for k in range(count)]
    else:
        own = [pair(operator[edges[k] : edges[k + 1]]) for k in range(count)]

    turns = lax.axis_size("row")
    line_row = lax.axis_index("row")
    groups, times, _ = snapshots.shape
    line = lax.all_gather(snapshots, "col", axis=1, tiled=True)
    line = after(line, hub).reshape(groups, chips, CORES, times, -1)
    line = lax.dynamic_index_in_dim(line, core, axis=2, keepdims=False)
    line = jnp.swapaxes(line, 0, 1)
    lines = [line]
    for i in range(1, turns):
        lines.append(lax.ppermute(line, "row", [(r, (r + i) % turns) for r in range(turns)]))
    height = turns * groups * times

    def left_side(row_chips, places):
        rows = jnp.stack(row_chips).astype(jnp.int32)
        places = [places_of(chips) for chips in places]
        places = jnp.array([[jnp.asarray(x, jnp.int32) for x in row] for row in places])
        step = width if width % 128 == 0 else CORES * width
        owners = jnp.stack([lax.rem(line_row - i + turns, turns) for i in range(turns)])
        return arrange(lines, owners.astype(jnp.int32), rows, places, step)

    mine = [at(side, lax.rem(place + i, half)) for i in range(half)]
    others = [at(1 - side, i) for i in range(half)]
    columns = [at(side, lax.rem(place - i + half, half)) for i in range(half)]
    rows_a = left_side(
        mine,
        [
            [None if i and i == j else q for j, q in enumerate(mine + others)]
            for i in range(half)
        ],
    )
    rows_b = left_side([mine[0]] + others, [columns] * (1 + half))

    ready, totals, turned, lane = (hub,), [None], first, outer
    for k in range(1, count):
        if k == 2:
            turned = [turn(after(chunk[k], *outer, sums[0]), i) for i in spokes]
            inner = [inward(after(chunk[0], *turned), i) for i in spokes]
        elif k > 2:
            turned = [turn(after(chunk[k], *inner), i) for i in spokes]
        pieces = own[k] + [y for x in turned for y in pair(after(x, *ready))]
        sums = product(rows_b, pieces, edges[k + 1] - edges[k], [height] * (1 + half))
        sent = [None] * half
        for i in reversed(range(half)) if k == count - 1 else range(half):
            sent[i] = across(after(sums[1 + i], *lane), i)
            lane = [sent[i]]
        totals.append([sums[0], *sent])
        ready = (sums[0], sent[0])

    pieces = own[0] + [y for x in [*inner, hub, *outer] for y in pair(after(x, sums[0]))]
    sums = product(rows_a, pieces, edges[1], [height] * half)
    totals[0] = [sums[0]] + [outward(sums[i], i) for i in spokes]

    out = None
    for k in [*range(1, count - 1), 0, count - 1]:
        out = put(out, totals[k], edges[k], modes)
    return out.reshape(turns * groups, times, modes)


def solution(mesh):
    placed = (P("row", "col", None), P("row", "col"))
    return jax.shard_map(
        shards, mesh=mesh, in_specs=placed, out_specs=P(None, "col", "row"), check_vma=False
    )
```

time: 663 us -> 435 us (0.66)
  waiting for transfers between devices: 547 us -> 275 us
  Pallas kernels: 0 us -> 84.4 us
  matrix products: 74.2 us -> 0 us
  starting transfers between devices: 0.01 us -> 35.6 us
  local copies, waits for them, and re-layouts: 2.89 us -> 24.1 us
  blocking collectives: 20.1 us -> 0 us
    all_gather x1, waiting for transfers between devices: 547 us -> 0.01 us  [shards(): line = lax.all_gather(snapshots, 'col', axis=1, tiled=True)]
    ppermute x0 -> x23, waiting for transfers between devices: none -> 275 us  [the longest x20 257 us: move(): return lax.ppermute(x, 'col', pairs)]
    pallas_call x0 -> x10, Pallas kernels: none -> 84.4 us  [the longest x4 66.6 us: product(): pl.pallas_call(kernel, grid=(modes // block,), in_specs=[pl.BlockSpec((he...]
    dot_general x1 -> x0, matrix products: 74.2 us -> none  [contract(): lax.dot_general(left, right, (((1,), (1,)), ((), ())), precision=lax.Prec...]
    ppermute x0 -> x23, starting transfers between devices: none -> 35.6 us  [the longest x20 31.1 us: move(): return lax.ppermute(x, 'col', pairs)]
    unnamed x4 -> x48, local copies, waits for them, and re-layouts: 2.72 us -> 13.2 us
    all_gather x1 -> x0, blocking collectives: 10.1 us -> none  [shards(): gathered = lax.all_gather(turned, 'row', axis=2, tiled=True)]
    all_to_all x1 -> x0, blocking collectives: 9.99 us -> none  [shards(): lax.all_to_all(snapshots, 'row', split_axis=2, concat_axis=0, tiled=True)]
  transfers between devices with their start and end apart: 1 -> 24, of which waited for: 1 -> 12; matrix products, arithmetic and copies ran while one was open for 1% -> 3% of each run, Pallas kernels for 0% -> 19%
where the time goes in v2:
time: 435 us; the launch traced here: 434 us
  waiting for transfers between devices  275 us (63%)
  Pallas kernels  84.4 us (19%)
  starting transfers between devices  35.6 us (8%)
  local copies, waits for them, and re-layouts  24.1 us (6%)
  between operations  13.6 us (3%)
    ppermute x20, waiting for transfers between devices, move(): return lax.ppermute(x, 'col', pairs)  257 us
    pallas_call x4, Pallas kernels, product(): pl.pallas_call(kernel, grid=(modes // block,), in_specs=[pl.BlockSpec((he...  66.6 us
    ppermute x20, starting transfers between devices, move(): return lax.ppermute(x, 'col', pairs)  31.1 us
    ppermute x3, waiting for transfers between devices, shards(): lax.ppermute(line, 'row', [(r, (r + i) % turns) for r in range(turns)])  17.4 us
    unnamed x48, local copies, waits for them, and re-layouts  13.2 us
    pallas_call x4, Pallas kernels, put(): pl.pallas_call(kernel, grid=(span // block,), in_specs=in_specs, out_spec...  10.8 us
  transfers between devices with their start and end apart: 24, of which 12 were waited for; matrix products, arithmetic and copies ran while one was open for 3% of the time, Pallas kernels for 19%

profile of v2, /device:TPU:0, one launch (start us, length us, event | category | flops | bytes accessed | tf_op | source)
XLA Modules:
  0.0 434.3 jit_solution(17892577791550470753)
XLA Ops:
  7.0 3.9 fusion
  10.8 2.0 collective-permute-start
  12.8 4.1 collective-permute-start.6
  17.0 54.5 %collective-permute-done.6.refs_2_ = f32[4096,128]{1,0:T(8,128)} collective-permute-done((f32[4096,128]{1,0:T(8,128)S(1)}, f32[4096,128]{1,0:T(8,128)}, u32[]{:S(2)}, u32[]{:S(2)}) %collective-permute-start.6) | collective-permute-done | bytes 2097184 | tf_op jit(solution)/shard_map/ppermute | solution.py:150
  71.5 4.9 %collective-permute-start.5 = (f32[4096,128]{1,0:T(8,128)}, f32[4096,128]{1,0:T(8,128)}, u32[]{:S(2)}, u32[]{:S(2)}) collective-permute-start(f32[4096,128]{1,0:T(8,128)} %get-tuple-element.44), channel_id=1, source_target_pairs={{0,4},{1,5},{6,2},{7,3},{8,12},{9,13},{14,10},{15,11},{16,20},{17,... | collective-permute-start | bytes 6291464 | tf_op jit(solution)/shard_map/ppermute | solution.py:150
  76.5 1.1 dynamic-slice_bitcast_fusion.refs_0_
  77.6 1.5 collective-permute-start.1
  80.9 1.5 collective-permute-start.2
  82.5 10.2 %collective-permute-done.1.refs_1_ = f32[4,1,32,1024]{3,2,1,0:T(8,128)S(1)} collective-permute-done((f32[4,1,32,1024]{3,2,1,0:T(8,128)S(1)}, f32[4,1,32,1024]{3,2,1,0:T(8,128)S(1)}, u32[]{:S(2)}, u32[]{:S(2)}) %collective-permute-start.1) | collective-permute-done | bytes 524320 | tf_op jit(solution)/shard_map/ppermute | solution.py:209
  92.7 1.4 collective-permute-start.3
  94.1 4.5 %fusion.1 = (f32[4096,128]{1,0:T(8,128)}, f32[4096,128]{1,0:T(8,128)}) fusion(f32[16384,128]{1,0:T(8,128)} %refs_0_.7), kind=kLoop, calls=%fused_computation.7 | loop fusion | bytes 8388608 | tf_op jit(solution)/shard_map/slice | solution.py:193
  98.7 5.1 %collective-permute-done.2.refs_2_ = f32[4,1,32,1024]{3,2,1,0:T(8,128)S(1)} collective-permute-done((f32[4,1,32,1024]{3,2,1,0:T(8,128)S(1)}, f32[4,1,32,1024]{3,2,1,0:T(8,128)S(1)}, u32[]{:S(2)}, u32[]{:S(2)}) %collective-permute-start.2) | collective-permute-done | bytes 524320 | tf_op jit(solution)/shard_map/ppermute | solution.py:209
  103.8 2.0 collective-permute-done.3.refs_3_
  105.9 0.8 copy-done.20
  106.7 3.9 shard_map.28
  110.6 1.0 copy-done
  111.6 1.0 copy-done.1
  112.6 15.6 %shard_map.29 = (f32[128,4096]{1,0:T(8,128)S(1)}, f32[128,4096]{1,0:T(8,128)S(1)}, f32[128,4096]{1,0:T(8,128)}) custom-call(bf16[384,512]{1,0:T(8,128)(2,1)S(1)} %copy-done, bf16[384,512]{1,0:T(8,128)(2,1)S(1)} %copy-done.1, f32[16384,128]{1,0:T(8,128)} %refs_0_.7, f32[16384,128]{1,0:T(8,128)} %collective-permute-done.4.refs_1_, ...), custom_call_target="tpu_custom_call" | custom-call | tf_op jit(solution)/shard_map/pallas_call | solution.py:88
  129.5 1.3 copy-done.2
  130.8 44.6 %collective-permute-done.8.refs_2_ = f32[4096,128]{1,0:T(8,128)S(1)} collective-permute-done((f32[4096,128]{1,0:T(8,128)S(1)}, f32[4096,128]{1,0:T(8,128)S(1)}, u32[]{:S(2)}, u32[]{:S(2)}) %collective-permute-start.8) | collective-permute-done | bytes 2097184 | tf_op jit(solution)/shard_map/ppermute | solution.py:150
  175.4 1.3 collective-permute-start.13
  176.7 7.1 %collective-permute-start.9 = (f32[4096,128]{1,0:T(8,128)}, f32[4096,128]{1,0:T(8,128)}, u32[]{:S(2)}, u32[]{:S(2)}) collective-permute-start(f32[4096,128]{1,0:T(8,128)} %get-tuple-element.44), channel_id=1, source_target_pairs={{0,2},{1,3},{6,4},{7,5},{8,10},{9,11},{14,12},{15,13},{16,18},{17,... | collective-permute-start | bytes 6291464 | tf_op jit(solution)/shard_map/ppermute | solution.py:150
  183.8 15.5 %shard_map.30 = (f32[128,4096]{1,0:T(8,128)S(1)}, f32[128,4096]{1,0:T(8,128)S(1)}, f32[128,4096]{1,0:T(8,128)}) custom-call(bf16[384,512]{1,0:T(8,128)(2,1)S(1)} %copy-done, bf16[384,512]{1,0:T(8,128)(2,1)S(1)} %copy-done.1, f32[16384,128]{1,0:T(8,128)} %refs_0_.7, f32[16384,128]{1,0:T(8,128)} %collective-permute-done.4.refs_1_, f32[4096,128]{1,0:T(8,128)} %copy-done.21, ...), custom_call_target="tpu_custom_call" | custom-call | tf_op jit(solution)/shard_map/pallas_call | solution.py:88
  199.3 1.3 copy-done.4
  200.6 25.8 %collective-permute-done.13.refs_2_ = f32[128,4096]{1,0:T(8,128)S(1)} collective-permute-done((f32[128,4096]{1,0:T(8,128)}, f32[128,4096]{1,0:T(8,128)S(1)}, u32[]{:S(2)}, u32[]{:S(2)}) %collective-permute-start.13) | collective-permute-done | bytes 2097184 | tf_op jit(solution)/shard_map/ppermute | solution.py:150
  228.0 2.5 collective-permute-start.10
  230.5 1.4 copy-done.6
  231.8 43.8 %collective-permute-done.10.refs_2_ = f32[4096,128]{1,0:T(8,128)S(1)} collective-permute-done((f32[4096,128]{1,0:T(8,128)S(1)}, f32[4096,128]{1,0:T(8,128)S(1)}, u32[]{:S(2)}, u32[]{:S(2)}) %collective-permute-start.10) | collective-permute-done | bytes 2097184 | tf_op jit(solution)/shard_map/ppermute | solution.py:150
  275.7 1.3 collective-permute-start.16
  277.0 2.9 collective-permute-done.15.refs_3_
  279.8 1.3 copy-done.23
  281.1 15.5 %shard_map.31 = (f32[128,4096]{1,0:T(8,128)S(1)}, f32[128,4096]{1,0:T(8,128)S(1)}, f32[128,4096]{1,0:T(8,128)}) custom-call(bf16[384,512]{1,0:T(8,128)(2,1)S(1)} %copy-done, bf16[384,512]{1,0:T(8,128)(2,1)S(1)} %copy-done.1, f32[16384,128]{1,0:T(8,128)} %refs_0_.7, f32[16384,128]{1,0:T(8,128)} %collective-permute-done.4.refs_1_, f32[4096,128]{1,0:T(8,128)} %copy-done.22, ...), custom_call_target="tpu_custom_call" | custom-call | tf_op jit(solution)/shard_map/pallas_call | solution.py:88
  296.7 1.3 copy-done.8
  298.0 1.3 copy-done.12
  300.0 26.8 %collective-permute-done.16.refs_2_ = f32[128,4096]{1,0:T(8,128)} collective-permute-done((f32[128,4096]{1,0:T(8,128)}, f32[128,4096]{1,0:T(8,128)}, u32[]{:S(2)}, u32[]{:S(2)}) %collective-permute-start.16) | collective-permute-done | bytes 2097184 | tf_op jit(solution)/shard_map/ppermute | solution.py:150
  326.8 1.3 collective-permute-start.17
  329.5 3.0 shard_map.32
  332.6 1.0 copy-done.10
  333.7 1.0 copy-done.11
  334.7 20.0 %shard_map.33 = (f32[128,4096]{1,0:T(8,128)S(1)}, f32[128,4096]{1,0:T(8,128)}) custom-call(bf16[256,1024]{1,0:T(8,128)(2,1)S(1)} %copy-done.10, bf16[256,1024]{1,0:T(8,128)(2,1)S(1)} %copy-done.11, f32[16384,128]{1,0:T(8,128)} %refs_0_.7, f32[16384,128]{1,0:T(8,128)} %collective-permute-done.4.refs_1_, f32[4096,128]{1,0:T(8,128)} %collective-permute-done.9.refs_2_, ...), custom_call_target="tpu_custom_call" | custom-call | tf_op jit(solution)/shard_map/pallas_call | solution.py:88
  354.7 1.3 collective-permute-start.22
  355.9 21.3 %collective-permute-done.17.refs_2_ = f32[128,4096]{1,0:T(8,128)} collective-permute-done((f32[128,4096]{1,0:T(8,128)}, f32[128,4096]{1,0:T(8,128)}, u32[]{:S(2)}, u32[]{:S(2)}) %collective-permute-start.17) | collective-permute-done | bytes 2097184 | tf_op jit(solution)/shard_map/ppermute | solution.py:150
  377.3 2.2 collective-permute-start.18
  379.4 2.8 shard_map.34.refs_3_
  382.3 2.9 shard_map.35.refs_2_
  385.1 36.9 %collective-permute-done.22.refs_1_ = f32[128,4096]{1,0:T(8,128)S(1)} collective-permute-done((f32[128,4096]{1,0:T(8,128)}, f32[128,4096]{1,0:T(8,128)S(1)}, u32[]{:S(2)}, u32[]{:S(2)}) %collective-permute-start.22) | collective-permute-done | bytes 2097184 | tf_op jit(solution)/shard_map/ppermute | solution.py:150
  422.0 1.7 shard_map.36.refs_3_
  424.1 3.4 shard_map.37
  (73 shorter events, 7.7 us)
Async XLA Ops:
  6.5 69.9 %all-gather.2.cloned.1.call-start = ((), (), s32[]{:S(2)}) async-start(), calls=%async_computation | async-start | bytes 1179648 | tf_op jit(solution)/shard_map/all_gather | solution.py:203
  6.5 104.1 %collective-permute-start.4 = (f32[16384,128]{1,0:T(8,128)}, f32[16384,128]{1,0:T(8,128)}, u32[]{:S(2)}, u32[]{:S(2)}) collective-permute-start(f32[16384,128]{1,0:T(8,128)} %refs_0_.7), channel_id=1, source_target_pairs={{2,3},{3,2},{0,1},{1,0},{4,5},{5,4},{6,7},{7,6},{10,11},{11,10},{8... | collective-permute-start | bytes 25165832 | tf_op jit(solution)/shard_map/ppermute | solution.py:150
  10.8 6.1 %collective-permute-start = (f32[4096,128]{1,0:T(8,128)}, f32[4096,128]{1,0:T(8,128)}, u32[]{:S(2)}, u32[]{:S(2)}) collective-permute-start(f32[4096,128]{1,0:T(8,128)} %get-tuple-element.44), channel_id=1, source_target_pairs={{2,4},{3,5},{4,2},{5,3},{10,12},{11,13},{12,10},{13,11},{18,20},{1... | collective-permute-start | bytes 6291464 | tf_op jit(solution)/shard_map/ppermute | solution.py:150
  12.8 58.7 %collective-permute-start.6 = (f32[4096,128]{1,0:T(8,128)S(1)}, f32[4096,128]{1,0:T(8,128)}, u32[]{:S(2)}, u32[]{:S(2)}) collective-permute-start(f32[4096,128]{1,0:T(8,128)S(1)} %get-tuple-element.69), channel_id=1, source_target_pairs={{2,0},{3,1},{0,2},{1,3},{4,6},{5,7},{6,4},{7,5},{10,8},{11,9},{8,1... | collective-permute-start | bytes 6291464 | tf_op jit(solution)/shard_map/ppermute | solution.py:150
  71.5 39.1 %collective-permute-start.7 = (f32[4096,128]{1,0:T(8,128)}, f32[4096,128]{1,0:T(8,128)}, u32[]{:S(2)}, u32[]{:S(2)}) collective-permute-start(f32[4096,128]{1,0:T(8,128)} %collective-permute-done.6.refs_2_), channel_id=1, source_target_pairs={{2,3},{3,2},{0,1},{1,0},{4,5},{5,4},{6,7},{7,6},{10,11},{11,10},{8... | collective-permute-start | bytes 6291464 | tf_op jit(solution)/shard_map/ppermute | solution.py:150
  71.5 56.7 %collective-permute-start.5 = (f32[4096,128]{1,0:T(8,128)}, f32[4096,128]{1,0:T(8,128)}, u32[]{:S(2)}, u32[]{:S(2)}) collective-permute-start(f32[4096,128]{1,0:T(8,128)} %get-tuple-element.44), channel_id=1, source_target_pairs={{0,4},{1,5},{6,2},{7,3},{8,12},{9,13},{14,10},{15,11},{16,20},{17,... | collective-permute-start | bytes 6291464 | tf_op jit(solution)/shard_map/ppermute | solution.py:150
  77.6 21.1 %copy-start.14 = (f32[4,1,32,1024]{3,2,1,0:T(8,128)}, f32[4,1,32,1024]{3,2,1,0:T(8,128)S(1)}, u32[]{:S(2)}) copy-start(f32[4,1,32,1024]{3,2,1,0:T(8,128)S(1)} %dynamic-slice_bitcast_fusion.refs_0_) | copy-start | bytes 1572868
  77.6 15.1 %collective-permute-start.1 = (f32[4,1,32,1024]{3,2,1,0:T(8,128)S(1)}, f32[4,1,32,1024]{3,2,1,0:T(8,128)S(1)}, u32[]{:S(2)}, u32[]{:S(2)}) collective-permute-start(f32[4,1,32,1024]{3,2,1,0:T(8,128)S(1)} %dynamic-slice_bitcast_fusion.refs_0_), channel_id=1, source_target_pairs={{0,8},{8,16},{16,24},{24,0},{1,9},{9,17},{17,25},{25,1},{2,10},{10... | collective-permute-start | bytes 1572872 | tf_op jit(solution)/shard_map/ppermute | solution.py:209
  80.9 22.9 %collective-permute-start.2 = (f32[4,1,32,1024]{3,2,1,0:T(8,128)S(1)}, f32[4,1,32,1024]{3,2,1,0:T(8,128)S(1)}, u32[]{:S(2)}, u32[]{:S(2)}) collective-permute-start(f32[4,1,32,1024]{3,2,1,0:T(8,128)S(1)} %dynamic-slice_bitcast_fusion.refs_0_), channel_id=1, source_target_pairs={{0,16},{8,24},{16,0},{24,8},{1,17},{9,25},{17,1},{25,9},{2,18},{10... | collective-permute-start | bytes 1572872 | tf_op jit(solution)/shard_map/ppermute | solution.py:209
  92.7 6.0 %copy-start.18 = (f32[4,1,32,1024]{3,2,1,0:T(8,128)}, f32[4,1,32,1024]{3,2,1,0:T(8,128)S(1)}, u32[]{:S(2)}) copy-start(f32[4,1,32,1024]{3,2,1,0:T(8,128)S(1)} %collective-permute-done.1.refs_1_) | copy-start | bytes 1572868
  92.7 13.2 %collective-permute-start.3 = (f32[4,1,32,1024]{3,2,1,0:T(8,128)S(1)}, f32[4,1,32,1024]{3,2,1,0:T(8,128)S(1)}, u32[]{:S(2)}, u32[]{:S(2)}) collective-permute-start(f32[4,1,32,1024]{3,2,1,0:T(8,128)S(1)} %dynamic-slice_bitcast_fusion.refs_0_), channel_id=1, source_target_pairs={{0,24},{8,0},{16,8},{24,16},{1,25},{9,1},{17,9},{25,17},{2,26},{10... | collective-permute-start | bytes 1572872 | tf_op jit(solution)/shard_map/ppermute | solution.py:209
  103.8 2.0 copy-start.19
  105.9 0.8 copy-start.20
  110.6 1.0 copy-start
  111.6 1.0 copy-start.1
  112.6 16.4 %copy-start.17 = (f32[4096,128]{1,0:T(8,128)S(1)}, f32[4096,128]{1,0:T(8,128)}, u32[]{:S(2)}) copy-start(f32[4096,128]{1,0:T(8,128)} %get-tuple-element.43) | copy-start | bytes 6291460
  128.2 1.3 collective-permute-start.11
  129.0 46.4 %collective-permute-start.8 = (f32[4096,128]{1,0:T(8,128)S(1)}, f32[4096,128]{1,0:T(8,128)S(1)}, u32[]{:S(2)}, u32[]{:S(2)}) collective-permute-start(f32[4096,128]{1,0:T(8,128)S(1)} %copy-done.17), channel_id=1, source_target_pairs={{2,0},{3,1},{0,2},{1,3},{4,6},{5,7},{6,4},{7,5},{10,8},{11,9},{8,1... | collective-permute-start | bytes 6291464 | tf_op jit(solution)/shard_map/ppermute | solution.py:150
  129.5 1.3 copy-start.2
  130.8 97.2 %copy-start.16 = (f32[4096,128]{1,0:T(8,128)S(1)}, f32[4096,128]{1,0:T(8,128)}, u32[]{:S(2)}) copy-start(f32[4096,128]{1,0:T(8,128)} %get-tuple-element.45) | copy-start | bytes 6291460
  175.4 8.4 %copy-start.21 = (f32[4096,128]{1,0:T(8,128)}, f32[4096,128]{1,0:T(8,128)S(1)}, u32[]{:S(2)}) copy-start(f32[4096,128]{1,0:T(8,128)S(1)} %collective-permute-done.8.refs_2_) | copy-start | bytes 6291460
  175.4 8.4 %collective-permute-start.12 = (f32[4096,128]{1,0:T(8,128)S(1)}, f32[4096,128]{1,0:T(8,128)}, u32[]{:S(2)}, u32[]{:S(2)}) collective-permute-start(f32[4096,128]{1,0:T(8,128)S(1)} %collective-permute-done.8.refs_2_), channel_id=1, source_target_pairs={{2,3},{3,2},{0,1},{1,0},{4,5},{5,4},{6,7},{7,6},{10,11},{11,10},{8... | collective-permute-start | bytes 6291464 | tf_op jit(solution)/shard_map/ppermute | solution.py:150
  175.4 51.0 %collective-permute-start.13 = (f32[128,4096]{1,0:T(8,128)}, f32[128,4096]{1,0:T(8,128)S(1)}, u32[]{:S(2)}, u32[]{:S(2)}) collective-permute-start(f32[128,4096]{1,0:T(8,128)} %get-tuple-element.52), channel_id=1, source_target_pairs={{2,6},{3,7},{4,0},{5,1},{10,14},{11,15},{12,8},{13,9},{18,22},{19,... | collective-permute-start | bytes 6291464 | tf_op jit(solution)/shard_map/ppermute | solution.py:150
  176.7 51.3 %collective-permute-start.9 = (f32[4096,128]{1,0:T(8,128)}, f32[4096,128]{1,0:T(8,128)}, u32[]{:S(2)}, u32[]{:S(2)}) collective-permute-start(f32[4096,128]{1,0:T(8,128)} %get-tuple-element.44), channel_id=1, source_target_pairs={{0,2},{1,3},{6,4},{7,5},{8,10},{9,11},{14,12},{15,13},{16,18},{17,... | collective-permute-start | bytes 6291464 | tf_op jit(solution)/shard_map/ppermute | solution.py:150
  199.3 1.3 copy-start.4
  226.4 70.2 %copy-start.15 = (f32[128,4096]{1,0:T(8,128)}, f32[128,4096]{1,0:T(8,128)S(1)}, u32[]{:S(2)}) copy-start(f32[128,4096]{1,0:T(8,128)S(1)} %collective-permute-done.13.refs_2_) | copy-start | bytes 6291460
  226.4 4.0 collective-permute-start.14
  228.0 47.7 %collective-permute-start.10 = (f32[4096,128]{1,0:T(8,128)S(1)}, f32[4096,128]{1,0:T(8,128)S(1)}, u32[]{:S(2)}, u32[]{:S(2)}) collective-permute-start(f32[4096,128]{1,0:T(8,128)S(1)} %copy-done.16), channel_id=1, source_target_pairs={{2,0},{3,1},{0,2},{1,3},{4,6},{5,7},{6,4},{7,5},{10,8},{11,9},{8,1... | collective-permute-start | bytes 6291464 | tf_op jit(solution)/shard_map/ppermute | solution.py:150
  230.5 1.4 copy-start.6
  275.7 4.2 copy-start.22
  275.7 4.2 collective-permute-start.15
  275.7 51.1 %collective-permute-start.16 = (f32[128,4096]{1,0:T(8,128)}, f32[128,4096]{1,0:T(8,128)}, u32[]{:S(2)}, u32[]{:S(2)}) collective-permute-start(f32[128,4096]{1,0:T(8,128)} %get-tuple-element.59), channel_id=1, source_target_pairs={{2,6},{3,7},{4,0},{5,1},{10,14},{11,15},{12,8},{13,9},{18,22},{19,... | collective-permute-start | bytes 6291464 | tf_op jit(solution)/shard_map/ppermute | solution.py:150
  279.8 1.3 copy-start.23
  296.6 1.3 copy-start.8
  298.0 1.3 copy-start.12
  299.3 33.3 %collective-permute-start.19 = (f32[4096,128]{1,0:T(8,128)}, f32[4096,128]{1,0:T(8,128)}, u32[]{:S(2)}, u32[]{:S(2)}) collective-permute-start(f32[4096,128]{1,0:T(8,128)} %collective-permute-done.9.refs_2_), channel_id=1, source_target_pairs={{2,3},{3,2},{0,1},{1,0},{4,5},{5,4},{6,7},{7,6},{10,11},{11,10},{8... | collective-permute-start | bytes 6291464 | tf_op jit(solution)/shard_map/ppermute | solution.py:150
  299.4 33.1 %collective-permute-start.20 = (f32[4096,128]{1,0:T(8,128)}, f32[4096,128]{1,0:T(8,128)}, u32[]{:S(2)}, u32[]{:S(2)}) collective-permute-start(f32[4096,128]{1,0:T(8,128)} %collective-permute-done.refs_4_), channel_id=1, source_target_pairs={{2,3},{3,2},{0,1},{1,0},{4,5},{5,4},{6,7},{7,6},{10,11},{11,10},{8... | collective-permute-start | bytes 6291464 | tf_op jit(solution)/shard_map/ppermute | solution.py:150
  299.8 32.8 %collective-permute-start.21 = (f32[4096,128]{1,0:T(8,128)}, f32[4096,128]{1,0:T(8,128)}, u32[]{:S(2)}, u32[]{:S(2)}) collective-permute-start(f32[4096,128]{1,0:T(8,128)} %collective-permute-done.5.refs_6_), channel_id=1, source_target_pairs={{2,3},{3,2},{0,1},{1,0},{4,5},{5,4},{6,7},{7,6},{10,11},{11,10},{8... | collective-permute-start | bytes 6291464 | tf_op jit(solution)/shard_map/ppermute | solution.py:150
  326.8 50.5 %collective-permute-start.17 = (f32[128,4096]{1,0:T(8,128)}, f32[128,4096]{1,0:T(8,128)}, u32[]{:S(2)}, u32[]{:S(2)}) collective-permute-start(f32[128,4096]{1,0:T(8,128)} %get-tuple-element.60), channel_id=1, source_target_pairs={{2,6},{3,7},{4,0},{5,1},{10,14},{11,15},{12,8},{13,9},{18,22},{19,... | collective-permute-start | bytes 6291464 | tf_op jit(solution)/shard_map/ppermute | solution.py:150
  332.6 1.0 copy-start.10
  333.6 1.0 copy-start.11
  334.7 42.6 %copy-start.13 = (f32[128,4096]{1,0:T(8,128)S(1)}, f32[128,4096]{1,0:T(8,128)}, u32[]{:S(2)}) copy-start(f32[128,4096]{1,0:T(8,128)} %copy-done.12) | copy-start | bytes 6291460
  334.7 44.7 %copy-start.3 = (f32[128,4096]{1,0:T(8,128)S(1)}, f32[128,4096]{1,0:T(8,128)}, u32[]{:S(2)}) copy-start(f32[128,4096]{1,0:T(8,128)} %copy-done.2) | copy-start | bytes 6291460
  354.7 67.3 %collective-permute-start.22 = (f32[128,4096]{1,0:T(8,128)}, f32[128,4096]{1,0:T(8,128)S(1)}, u32[]{:S(2)}, u32[]{:S(2)}) collective-permute-start(f32[128,4096]{1,0:T(8,128)} %get-tuple-element.68), channel_id=1, source_target_pairs={{2,0},{3,1},{4,6},{5,7},{10,8},{11,9},{12,14},{13,15},{18,16},{19,... | collective-permute-start | bytes 6291464 | tf_op jit(solution)/shard_map/ppermute | solution.py:150
  377.3 5.0 %copy-start.5 = (f32[128,4096]{1,0:T(8,128)S(1)}, f32[128,4096]{1,0:T(8,128)}, u32[]{:S(2)}) copy-start(f32[128,4096]{1,0:T(8,128)} %copy-done.4) | copy-start | bytes 6291460
  377.3 5.0 %copy-start.7 = (f32[128,4096]{1,0:T(8,128)S(1)}, f32[128,4096]{1,0:T(8,128)}, u32[]{:S(2)}) copy-start(f32[128,4096]{1,0:T(8,128)} %copy-done.6) | copy-start | bytes 6291460
  377.3 46.4 %collective-permute-start.18 = (f32[128,4096]{1,0:T(8,128)S(1)}, f32[128,4096]{1,0:T(8,128)}, u32[]{:S(2)}, u32[]{:S(2)}) collective-permute-start(f32[128,4096]{1,0:T(8,128)S(1)} %copy-done.13), channel_id=1, source_target_pairs={{2,4},{3,5},{4,2},{5,3},{10,12},{11,13},{12,10},{13,11},{18,20},{1... | collective-permute-start | bytes 6291464 | tf_op jit(solution)/shard_map/ppermute | solution.py:150
  422.0 2.1 copy-start.9
Sparse Core Ops, SparseCore 0:
  17.1 26.6 all-gather.1

commit v3 on v2

--- a/solution.py
+++ b/solution.py
@@ -188,7 +188,9 @@
 
     hub = across(chunk[0])
     first = [turn(chunk[1], i) for i in spokes]
-    outer = [far(chunk[0], i) for i in spokes]
+    near = [snapshots] + [turn(snapshots, i) for i in reversed(spokes)]
+    line = jnp.stack(near + [across(snapshots)] + [far(snapshots, i) for i in spokes])
+    outer = [far(after(chunk[0], line), i) for i in spokes]
     rest = after(operator, hub)
     chunk += [rest[edges[k] : edges[k + 1]] for k in range(2, count)]
     if width % 128 == 0:
@@ -200,17 +202,13 @@
     turns = lax.axis_size("row")
     line_row = lax.axis_index("row")
     groups, times, _ = snapshots.shape
-    line = lax.all_gather(snapshots, "col", axis=1, tiled=True)
-    line = after(line, hub).reshape(groups, chips, CORES, times, -1)
-    line = lax.dynamic_index_in_dim(line, core, axis=2, keepdims=False)
-    line = jnp.swapaxes(line, 0, 1)
     lines = [line]
     for i in range(1, turns):
         lines.append(lax.ppermute(line, "row", [(r, (r + i) % turns) for r in range(turns)]))
     height = turns * groups * times
 
     def left_side(row_chips, places):
-        rows = jnp.stack(row_chips).astype(jnp.int32)
+        rows = jnp.array(row_chips, jnp.int32)
         places = [places_of(chips) for chips in places]
         places = jnp.array([[jnp.asarray(x, jnp.int32) for x in row] for row in places])
         step = width if width % 128 == 0 else CORES * width
@@ -221,13 +219,13 @@
     others = [at(1 - side, i) for i in range(half)]
     columns = [at(side, lax.rem(place - i + half, half)) for i in range(half)]
     rows_a = left_side(
-        mine,
+        range(half),
         [
             [None if i and i == j else q for j, q in enumerate(mine + others)]
             for i in range(half)
         ],
     )
-    rows_b = left_side([mine[0]] + others, [columns] * (1 + half))
+    rows_b = left_side([0, *range(half, 2 * half)], [columns] * (1 + half))
 
     ready, totals, turned, lane = (hub,), [None], first, outer
     for k in range(1, count):

time: 435 us -> 421 us (0.968)
  starting transfers between devices: 35.6 us -> 92 us
  waiting for transfers between devices: 275 us -> 223 us
  between operations: 13.6 us -> 0.27 us
  local copies, waits for them, and re-layouts: 24.1 us -> 19.7 us
    ppermute x20 -> x23, starting transfers between devices: 31.1 us -> 87.5 us  [move(): return lax.ppermute(x, 'col', pairs)]
    ppermute x20 -> x23, waiting for transfers between devices: 257 us -> 209 us  [move(): return lax.ppermute(x, 'col', pairs)]
  transfers between devices with their start and end apart: 24 -> 26, of which waited for: 12 -> 12; matrix products, arithmetic and copies ran while one was open for 3% -> 2% of each run, Pallas kernels for 19% -> 19%
where the time goes in v3:
time: 421 us; the launch traced here: 420 us
  waiting for transfers between devices  223 us (53%)
  starting transfers between devices  92 us (22%)
  Pallas kernels  84.2 us (20%)
  local copies, waits for them, and re-layouts  19.7 us (5%)
    ppermute x23, waiting for transfers between devices, move(): return lax.ppermute(x, 'col', pairs)  209 us
    ppermute x23, starting transfers between devices, move(): return lax.ppermute(x, 'col', pairs)  87.5 us
    pallas_call x4, Pallas kernels, product(): pl.pallas_call(kernel, grid=(modes // block,), in_specs=[pl.BlockSpec((he...  66.5 us
    ppermute x3, waiting for transfers between devices, shards(): lax.ppermute(line, 'row', [(r, (r + i) % turns) for r in range(turns)])  13.9 us
    unnamed x48, local copies, waits for them, and re-layouts  11.3 us
    pallas_call x4, Pallas kernels, put(): pl.pallas_call(kernel, grid=(span // block,), in_specs=in_specs, out_spec...  10.8 us
  transfers between devices with their start and end apart: 26, of which 12 were waited for; matrix products, arithmetic and copies ran while one was open for 2% of the time, Pallas kernels for 19%

profile of v3, /device:TPU:0, one launch (start us, length us, event | category | flops | bytes accessed | tf_op | source)
XLA Modules:
  0.0 420.3 jit_solution(8524662604337218456)
XLA Ops:
  0.5 3.8 fusion
  5.1 5.4 %collective-permute-start.9 = (f32[4096,128]{1,0:T(8,128)S(1)}, f32[4096,128]{1,0:T(8,128)}, u32[]{:S(2)}, u32[]{:S(2)}) collective-permute-start(f32[4096,128]{1,0:T(8,128)S(1)} %get-tuple-element.69), channel_id=1, source_target_pairs={{2,0},{3,1},{0,2},{1,3},{4,6},{5,7},{6,4},{7,5},{10,8},{11,9},{8,1... | collective-permute-start | bytes 6291464 | tf_op jit(solution)/shard_map/ppermute | solution.py:150
  11.1 4.6 %collective-permute-start.2 = (f32[1,32,1024]{2,1,0:T(8,128)S(1)}, f32[1,32,1024]{2,1,0:T(8,128)S(1)}, u32[]{:S(2)}, u32[]{:S(2)}) collective-permute-start(f32[1,32,1024]{2,1,0:T(8,128)S(1)} %copy-done.23), channel_id=1, source_target_pairs={{0,4},{1,5},{6,2},{7,3},{8,12},{9,13},{14,10},{15,11},{16,20},{17,... | collective-permute-start | bytes 393224 | tf_op jit(solution)/shard_map/ppermute | solution.py:150
  15.8 46.8 %collective-permute-start = (f32[1,32,1024]{2,1,0:T(8,128)S(1)}, f32[1,32,1024]{2,1,0:T(8,128)S(1)}, u32[]{:S(2)}, u32[]{:S(2)}) collective-permute-start(f32[1,32,1024]{2,1,0:T(8,128)S(1)} %copy-done.23), channel_id=1, source_target_pairs={{2,0},{3,1},{0,2},{1,3},{4,6},{5,7},{6,4},{7,5},{10,8},{11,9},{8,1... | collective-permute-start | bytes 393224 | tf_op jit(solution)/shard_map/ppermute | solution.py:150
  62.6 3.3 collective-permute-done
  66.0 1.5 collective-permute-start.3
  67.6 6.1 %collective-permute-start.8 = (f32[4096,128]{1,0:T(8,128)}, f32[4096,128]{1,0:T(8,128)}, u32[]{:S(2)}, u32[]{:S(2)}) collective-permute-start(f32[4096,128]{1,0:T(8,128)} %get-tuple-element.44), channel_id=1, source_target_pairs={{0,4},{1,5},{6,2},{7,3},{8,12},{9,13},{14,10},{15,11},{16,20},{17,... | collective-permute-start | bytes 6291464 | tf_op jit(solution)/shard_map/ppermute | solution.py:150
  73.7 1.5 collective-permute-start.4
  75.2 4.8 %collective-permute-done.3.refs_1_ = f32[4,1,32,1024]{3,2,1,0:T(8,128)S(1)} collective-permute-done((f32[4,1,32,1024]{3,2,1,0:T(8,128)S(1)}, f32[4,1,32,1024]{3,2,1,0:T(8,128)S(1)}, u32[]{:S(2)}, u32[]{:S(2)}) %collective-permute-start.3) | collective-permute-done | bytes 524320 | tf_op jit(solution)/shard_map/ppermute | solution.py:207
  80.0 1.4 collective-permute-start.5
  82.7 8.4 %collective-permute-done.4.refs_2_ = f32[4,1,32,1024]{3,2,1,0:T(8,128)S(1)} collective-permute-done((f32[4,1,32,1024]{3,2,1,0:T(8,128)S(1)}, f32[4,1,32,1024]{3,2,1,0:T(8,128)S(1)}, u32[]{:S(2)}, u32[]{:S(2)}) %collective-permute-start.4) | collective-permute-done | bytes 524320 | tf_op jit(solution)/shard_map/ppermute | solution.py:207
  91.1 0.8 collective-permute-done.5.refs_3_
  91.9 0.8 copy-done.18
  92.7 3.9 shard_map.46
  96.7 2.6 fusion.1
  99.3 15.5 %shard_map.47 = (f32[128,4096]{1,0:T(8,128)S(1)}, f32[128,4096]{1,0:T(8,128)S(1)}, f32[128,4096]{1,0:T(8,128)}) custom-call(bf16[384,512]{1,0:T(8,128)(2,1)S(1)} %copy-done, bf16[384,512]{1,0:T(8,128)(2,1)S(1)} %copy-done.1, f32[16384,128]{1,0:T(8,128)} %refs_0_.7, f32[16384,128]{1,0:T(8,128)} %collective-permute-done.6.refs_1_, ...), custom_call_target="tpu_custom_call" | custom-call | tf_op jit(solution)/shard_map/pallas_call | solution.py:88
  114.8 3.4 collective-permute-done.8.refs_6_
  118.9 5.1 %collective-permute-start.11 = (f32[4096,128]{1,0:T(8,128)S(1)}, f32[4096,128]{1,0:T(8,128)S(1)}, u32[]{:S(2)}, u32[]{:S(2)}) collective-permute-start(f32[4096,128]{1,0:T(8,128)S(1)} %get-tuple-element.43), channel_id=1, source_target_pairs={{2,0},{3,1},{0,2},{1,3},{4,6},{5,7},{6,4},{7,5},{10,8},{11,9},{8,1... | collective-permute-start | bytes 6291464 | tf_op jit(solution)/shard_map/ppermute | solution.py:150
  124.1 1.3 copy-done.2
  125.4 43.9 %collective-permute-done.11.refs_2_ = f32[4096,128]{1,0:T(8,128)S(1)} collective-permute-done((f32[4096,128]{1,0:T(8,128)S(1)}, f32[4096,128]{1,0:T(8,128)S(1)}, u32[]{:S(2)}, u32[]{:S(2)}) %collective-permute-start.11) | collective-permute-done | bytes 2097184 | tf_op jit(solution)/shard_map/ppermute | solution.py:150
  169.3 1.3 collective-permute-start.16
  170.6 5.9 %collective-permute-start.12 = (f32[4096,128]{1,0:T(8,128)}, f32[4096,128]{1,0:T(8,128)}, u32[]{:S(2)}, u32[]{:S(2)}) collective-permute-start(f32[4096,128]{1,0:T(8,128)} %get-tuple-element.44), channel_id=1, source_target_pairs={{0,2},{1,3},{6,4},{7,5},{8,10},{9,11},{14,12},{15,13},{16,18},{17,... | collective-permute-start | bytes 6291464 | tf_op jit(solution)/shard_map/ppermute | solution.py:150
  176.5 15.5 %shard_map.48 = (f32[128,4096]{1,0:T(8,128)S(1)}, f32[128,4096]{1,0:T(8,128)S(1)}, f32[128,4096]{1,0:T(8,128)}) custom-call(bf16[384,512]{1,0:T(8,128)(2,1)S(1)} %copy-done, bf16[384,512]{1,0:T(8,128)(2,1)S(1)} %copy-done.1, f32[16384,128]{1,0:T(8,128)} %refs_0_.7, f32[16384,128]{1,0:T(8,128)} %collective-permute-done.6.refs_1_, f32[4096,128]{1,0:T(8,128)} %copy-done.19, ...), custom_call_target="tpu_custom_call" | custom-call | tf_op jit(solution)/shard_map/pallas_call | solution.py:88
  192.0 1.3 copy-done.4
  193.3 27.0 %collective-permute-done.16.refs_2_ = f32[128,4096]{1,0:T(8,128)S(1)} collective-permute-done((f32[128,4096]{1,0:T(8,128)}, f32[128,4096]{1,0:T(8,128)S(1)}, u32[]{:S(2)}, u32[]{:S(2)}) %collective-permute-start.16) | collective-permute-done | bytes 2097184 | tf_op jit(solution)/shard_map/ppermute | solution.py:150
  221.1 2.1 collective-permute-start.13
  223.2 1.3 copy-done.6
  224.5 43.9 %collective-permute-done.13.refs_2_ = f32[4096,128]{1,0:T(8,128)S(1)} collective-permute-done((f32[4096,128]{1,0:T(8,128)S(1)}, f32[4096,128]{1,0:T(8,128)S(1)}, u32[]{:S(2)}, u32[]{:S(2)}) %collective-permute-start.13) | collective-permute-done | bytes 2097184 | tf_op jit(solution)/shard_map/ppermute | solution.py:150
  268.4 1.3 collective-permute-start.19
  269.7 2.9 collective-permute-done.18.refs_3_
  272.6 1.4 copy-done.21
  274.0 15.5 %shard_map.49 = (f32[128,4096]{1,0:T(8,128)S(1)}, f32[128,4096]{1,0:T(8,128)S(1)}, f32[128,4096]{1,0:T(8,128)}) custom-call(bf16[384,512]{1,0:T(8,128)(2,1)S(1)} %copy-done, bf16[384,512]{1,0:T(8,128)(2,1)S(1)} %copy-done.1, f32[16384,128]{1,0:T(8,128)} %refs_0_.7, f32[16384,128]{1,0:T(8,128)} %collective-permute-done.6.refs_1_, f32[4096,128]{1,0:T(8,128)} %copy-done.20, ...), custom_call_target="tpu_custom_call" | custom-call | tf_op jit(solution)/shard_map/pallas_call | solution.py:88
  289.5 1.4 copy-done.8
  290.9 1.3 copy-done.12
  292.8 26.8 %collective-permute-done.19.refs_2_ = f32[128,4096]{1,0:T(8,128)} collective-permute-done((f32[128,4096]{1,0:T(8,128)}, f32[128,4096]{1,0:T(8,128)}, u32[]{:S(2)}, u32[]{:S(2)}) %collective-permute-start.19) | collective-permute-done | bytes 2097184 | tf_op jit(solution)/shard_map/ppermute | solution.py:150
  319.6 1.3 collective-permute-start.20
  322.3 3.0 shard_map.50
  325.3 1.0 copy-done.10
  326.4 1.0 copy-done.11
  327.4 19.9 %shard_map.51 = (f32[128,4096]{1,0:T(8,128)S(1)}, f32[128,4096]{1,0:T(8,128)}) custom-call(bf16[256,1024]{1,0:T(8,128)(2,1)S(1)} %copy-done.10, bf16[256,1024]{1,0:T(8,128)(2,1)S(1)} %copy-done.11, f32[16384,128]{1,0:T(8,128)} %refs_0_.7, f32[16384,128]{1,0:T(8,128)} %collective-permute-done.6.refs_1_, f32[4096,128]{1,0:T(8,128)} %collective-permute-done.12.refs_2_, ...), custom_call_target="tpu_custom_call" | custom-call | tf_op jit(solution)/shard_map/pallas_call | solution.py:88
  347.4 1.3 collective-permute-start.25
  348.6 21.4 %collective-permute-done.20.refs_2_ = f32[128,4096]{1,0:T(8,128)} collective-permute-done((f32[128,4096]{1,0:T(8,128)}, f32[128,4096]{1,0:T(8,128)}, u32[]{:S(2)}, u32[]{:S(2)}) %collective-permute-start.20) | collective-permute-done | bytes 2097184 | tf_op jit(solution)/shard_map/ppermute | solution.py:150
  370.1 2.1 collective-permute-start.21
  372.2 2.8 shard_map.52.refs_3_
  375.0 2.9 shard_map.53.refs_2_
  377.9 36.9 %collective-permute-done.25.refs_1_ = f32[128,4096]{1,0:T(8,128)S(1)} collective-permute-done((f32[128,4096]{1,0:T(8,128)}, f32[128,4096]{1,0:T(8,128)S(1)}, u32[]{:S(2)}, u32[]{:S(2)}) %collective-permute-start.25) | collective-permute-done | bytes 2097184 | tf_op jit(solution)/shard_map/ppermute | solution.py:150
  414.8 1.7 shard_map.54.refs_3_
  416.9 3.4 shard_map.55
  (75 shorter events, 7.4 us)
Async XLA Ops:
  0.0 10.4 %copy-start.23 = (f32[1,32,1024]{2,1,0:T(8,128)S(1)}, f32[1,32,1024]{2,1,0:T(8,128)}, u32[]{:S(2)}) copy-start(f32[1,32,1024]{2,1,0:T(8,128)} %param.4) | copy-start | bytes 393220
  0.0 99.2 %collective-permute-start.6 = (f32[16384,128]{1,0:T(8,128)}, f32[16384,128]{1,0:T(8,128)}, u32[]{:S(2)}, u32[]{:S(2)}) collective-permute-start(f32[16384,128]{1,0:T(8,128)} %refs_0_.7), channel_id=1, source_target_pairs={{2,3},{3,2},{0,1},{1,0},{4,5},{5,4},{6,7},{7,6},{10,11},{11,10},{8... | collective-permute-start | bytes 25165832 | tf_op jit(solution)/shard_map/ppermute | solution.py:150
  4.3 63.3 %collective-permute-start.7 = (f32[4096,128]{1,0:T(8,128)}, f32[4096,128]{1,0:T(8,128)S(1)}, u32[]{:S(2)}, u32[]{:S(2)}) collective-permute-start(f32[4096,128]{1,0:T(8,128)} %get-tuple-element.44), channel_id=1, source_target_pairs={{2,4},{3,5},{4,2},{5,3},{10,12},{11,13},{12,10},{13,11},{18,20},{1... | collective-permute-start | bytes 6291464 | tf_op jit(solution)/shard_map/ppermute | solution.py:150
  5.1 62.5 %collective-permute-start.9 = (f32[4096,128]{1,0:T(8,128)S(1)}, f32[4096,128]{1,0:T(8,128)}, u32[]{:S(2)}, u32[]{:S(2)}) collective-permute-start(f32[4096,128]{1,0:T(8,128)S(1)} %get-tuple-element.69), channel_id=1, source_target_pairs={{2,0},{3,1},{0,2},{1,3},{4,6},{5,7},{6,4},{7,5},{10,8},{11,9},{8,1... | collective-permute-start | bytes 6291464 | tf_op jit(solution)/shard_map/ppermute | solution.py:150
  10.4 5.3 %collective-permute-start.1 = (f32[1,32,1024]{2,1,0:T(8,128)S(1)}, f32[1,32,1024]{2,1,0:T(8,128)S(1)}, u32[]{:S(2)}, u32[]{:S(2)}) collective-permute-start(f32[1,32,1024]{2,1,0:T(8,128)S(1)} %copy-done.23), channel_id=1, source_target_pairs={{2,4},{3,5},{4,2},{5,3},{10,12},{11,13},{12,10},{13,11},{18,20},{1... | collective-permute-start | bytes 393224 | tf_op jit(solution)/shard_map/ppermute | solution.py:150
  11.1 51.5 %collective-permute-start.2 = (f32[1,32,1024]{2,1,0:T(8,128)S(1)}, f32[1,32,1024]{2,1,0:T(8,128)S(1)}, u32[]{:S(2)}, u32[]{:S(2)}) collective-permute-start(f32[1,32,1024]{2,1,0:T(8,128)S(1)} %copy-done.23), channel_id=1, source_target_pairs={{0,4},{1,5},{6,2},{7,3},{8,12},{9,13},{14,10},{15,11},{16,20},{17,... | collective-permute-start | bytes 393224 | tf_op jit(solution)/shard_map/ppermute | solution.py:150
  15.8 50.2 %collective-permute-start = (f32[1,32,1024]{2,1,0:T(8,128)S(1)}, f32[1,32,1024]{2,1,0:T(8,128)S(1)}, u32[]{:S(2)}, u32[]{:S(2)}) collective-permute-start(f32[1,32,1024]{2,1,0:T(8,128)S(1)} %copy-done.23), channel_id=1, source_target_pairs={{2,0},{3,1},{0,2},{1,3},{4,6},{5,7},{6,4},{7,5},{10,8},{11,9},{8,1... | collective-permute-start | bytes 393224 | tf_op jit(solution)/shard_map/ppermute | solution.py:150
  66.0 25.9 %copy-start.14 = (f32[4,1,32,1024]{3,2,1,0:T(8,128)}, f32[4,1,32,1024]{3,2,1,0:T(8,128)S(1)}, u32[]{:S(2)}) copy-start(f32[4,1,32,1024]{3,2,1,0:T(8,128)S(1)} %pad_maximum_fusion.refs_0_) | copy-start | bytes 1572868
  66.0 14.0 %collective-permute-start.3 = (f32[4,1,32,1024]{3,2,1,0:T(8,128)S(1)}, f32[4,1,32,1024]{3,2,1,0:T(8,128)S(1)}, u32[]{:S(2)}, u32[]{:S(2)}) collective-permute-start(f32[4,1,32,1024]{3,2,1,0:T(8,128)S(1)} %pad_maximum_fusion.refs_0_), channel_id=1, source_target_pairs={{0,8},{8,16},{16,24},{24,0},{1,9},{9,17},{17,25},{25,1},{2,10},{10... | collective-permute-start | bytes 1572872 | tf_op jit(solution)/shard_map/ppermute | solution.py:207
  67.5 12.5 %copy-start.22 = (f32[4096,128]{1,0:T(8,128)}, f32[4096,128]{1,0:T(8,128)S(1)}, u32[]{:S(2)}) copy-start(f32[4096,128]{1,0:T(8,128)S(1)} %collective-permute-done.7.refs_4_) | copy-start | bytes 6291460
  67.6 31.7 %collective-permute-start.10 = (f32[4096,128]{1,0:T(8,128)}, f32[4096,128]{1,0:T(8,128)}, u32[]{:S(2)}, u32[]{:S(2)}) collective-permute-start(f32[4096,128]{1,0:T(8,128)} %collective-permute-done.9.refs_2_), channel_id=1, source_target_pairs={{2,3},{3,2},{0,1},{1,0},{4,5},{5,4},{6,7},{7,6},{10,11},{11,10},{8... | collective-permute-start | bytes 6291464 | tf_op jit(solution)/shard_map/ppermute | solution.py:150
  67.6 50.5 %collective-permute-start.8 = (f32[4096,128]{1,0:T(8,128)}, f32[4096,128]{1,0:T(8,128)}, u32[]{:S(2)}, u32[]{:S(2)}) collective-permute-start(f32[4096,128]{1,0:T(8,128)} %get-tuple-element.44), channel_id=1, source_target_pairs={{0,4},{1,5},{6,2},{7,3},{8,12},{9,13},{14,10},{15,11},{16,20},{17,... | collective-permute-start | bytes 6291464 | tf_op jit(solution)/shard_map/ppermute | solution.py:150
  73.7 17.4 %collective-permute-start.4 = (f32[4,1,32,1024]{3,2,1,0:T(8,128)S(1)}, f32[4,1,32,1024]{3,2,1,0:T(8,128)S(1)}, u32[]{:S(2)}, u32[]{:S(2)}) collective-permute-start(f32[4,1,32,1024]{3,2,1,0:T(8,128)S(1)} %pad_maximum_fusion.refs_0_), channel_id=1, source_target_pairs={{0,16},{8,24},{16,0},{24,8},{1,17},{9,25},{17,1},{25,9},{2,18},{10... | collective-permute-start | bytes 1572872 | tf_op jit(solution)/shard_map/ppermute | solution.py:207
  80.0 11.9 %copy-start.16 = (f32[4,1,32,1024]{3,2,1,0:T(8,128)}, f32[4,1,32,1024]{3,2,1,0:T(8,128)S(1)}, u32[]{:S(2)}) copy-start(f32[4,1,32,1024]{3,2,1,0:T(8,128)S(1)} %collective-permute-done.3.refs_1_) | copy-start | bytes 1572868
  80.0 11.9 %collective-permute-start.5 = (f32[4,1,32,1024]{3,2,1,0:T(8,128)S(1)}, f32[4,1,32,1024]{3,2,1,0:T(8,128)S(1)}, u32[]{:S(2)}, u32[]{:S(2)}) collective-permute-start(f32[4,1,32,1024]{3,2,1,0:T(8,128)S(1)} %pad_maximum_fusion.refs_0_), channel_id=1, source_target_pairs={{0,24},{8,0},{16,8},{24,16},{1,25},{9,1},{17,9},{25,17},{2,26},{10... | collective-permute-start | bytes 1572872 | tf_op jit(solution)/shard_map/ppermute | solution.py:207
  96.7 2.6 copy-start
  96.7 2.6 copy-start.1
  118.1 5.9 %collective-permute-start.14 = (f32[128,4096]{1,0:T(8,128)S(1)}, f32[128,4096]{1,0:T(8,128)S(1)}, u32[]{:S(2)}, u32[]{:S(2)}) collective-permute-start(f32[128,4096]{1,0:T(8,128)S(1)} %get-tuple-element.47), channel_id=1, source_target_pairs={{2,4},{3,5},{4,2},{5,3},{10,12},{11,13},{12,10},{13,11},{18,20},{1... | collective-permute-start | bytes 6291464 | tf_op jit(solution)/shard_map/ppermute | solution.py:150
  118.9 50.3 %collective-permute-start.11 = (f32[4096,128]{1,0:T(8,128)S(1)}, f32[4096,128]{1,0:T(8,128)S(1)}, u32[]{:S(2)}, u32[]{:S(2)}) collective-permute-start(f32[4096,128]{1,0:T(8,128)S(1)} %get-tuple-element.43), channel_id=1, source_target_pairs={{2,0},{3,1},{0,2},{1,3},{4,6},{5,7},{6,4},{7,5},{10,8},{11,9},{8,1... | collective-permute-start | bytes 6291464 | tf_op jit(solution)/shard_map/ppermute | solution.py:150
  124.1 1.3 copy-start.2
  169.3 7.2 %copy-start.19 = (f32[4096,128]{1,0:T(8,128)}, f32[4096,128]{1,0:T(8,128)S(1)}, u32[]{:S(2)}) copy-start(f32[4096,128]{1,0:T(8,128)S(1)} %collective-permute-done.11.refs_2_) | copy-start | bytes 6291460
  169.3 7.2 %collective-permute-start.15 = (f32[4096,128]{1,0:T(8,128)S(1)}, f32[4096,128]{1,0:T(8,128)}, u32[]{:S(2)}, u32[]{:S(2)}) collective-permute-start(f32[4096,128]{1,0:T(8,128)S(1)} %collective-permute-done.11.refs_2_), channel_id=1, source_target_pairs={{2,3},{3,2},{0,1},{1,0},{4,5},{5,4},{6,7},{7,6},{10,11},{11,10},{8... | collective-permute-start | bytes 6291464 | tf_op jit(solution)/shard_map/ppermute | solution.py:150
  169.3 51.0 %collective-permute-start.16 = (f32[128,4096]{1,0:T(8,128)}, f32[128,4096]{1,0:T(8,128)S(1)}, u32[]{:S(2)}, u32[]{:S(2)}) collective-permute-start(f32[128,4096]{1,0:T(8,128)} %get-tuple-element.52), channel_id=1, source_target_pairs={{2,6},{3,7},{4,0},{5,1},{10,14},{11,15},{12,8},{13,9},{18,22},{19,... | collective-permute-start | bytes 6291464 | tf_op jit(solution)/shard_map/ppermute | solution.py:150
  170.6 50.5 %collective-permute-start.12 = (f32[4096,128]{1,0:T(8,128)}, f32[4096,128]{1,0:T(8,128)}, u32[]{:S(2)}, u32[]{:S(2)}) collective-permute-start(f32[4096,128]{1,0:T(8,128)} %get-tuple-element.44), channel_id=1, source_target_pairs={{0,2},{1,3},{6,4},{7,5},{8,10},{9,11},{14,12},{15,13},{16,18},{17,... | collective-permute-start | bytes 6291464 | tf_op jit(solution)/shard_map/ppermute | solution.py:150
  192.0 1.3 copy-start.4
  220.3 69.2 %copy-start.15 = (f32[128,4096]{1,0:T(8,128)}, f32[128,4096]{1,0:T(8,128)S(1)}, u32[]{:S(2)}) copy-start(f32[128,4096]{1,0:T(8,128)S(1)} %collective-permute-done.16.refs_2_) | copy-start | bytes 6291460
  220.3 2.9 collective-permute-start.17
  221.1 47.3 %collective-permute-start.13 = (f32[4096,128]{1,0:T(8,128)S(1)}, f32[4096,128]{1,0:T(8,128)S(1)}, u32[]{:S(2)}, u32[]{:S(2)}) collective-permute-start(f32[4096,128]{1,0:T(8,128)S(1)} %get-tuple-element.45), channel_id=1, source_target_pairs={{2,0},{3,1},{0,2},{1,3},{4,6},{5,7},{6,4},{7,5},{10,8},{11,9},{8,1... | collective-permute-start | bytes 6291464 | tf_op jit(solution)/shard_map/ppermute | solution.py:150
  223.2 1.3 copy-start.6
  268.4 4.2 copy-start.20
  268.4 4.2 collective-permute-start.18
  268.4 51.1 %collective-permute-start.19 = (f32[128,4096]{1,0:T(8,128)}, f32[128,4096]{1,0:T(8,128)}, u32[]{:S(2)}, u32[]{:S(2)}) collective-permute-start(f32[128,4096]{1,0:T(8,128)} %get-tuple-element.59), channel_id=1, source_target_pairs={{2,6},{3,7},{4,0},{5,1},{10,14},{11,15},{12,8},{13,9},{18,22},{19,... | collective-permute-start | bytes 6291464 | tf_op jit(solution)/shard_map/ppermute | solution.py:150
  272.6 1.4 copy-start.21
  289.5 1.4 copy-start.8
  290.8 1.3 copy-start.12
  292.2 33.1 %collective-permute-start.22 = (f32[4096,128]{1,0:T(8,128)}, f32[4096,128]{1,0:T(8,128)}, u32[]{:S(2)}, u32[]{:S(2)}) collective-permute-start(f32[4096,128]{1,0:T(8,128)} %collective-permute-done.12.refs_2_), channel_id=1, source_target_pairs={{2,3},{3,2},{0,1},{1,0},{4,5},{5,4},{6,7},{7,6},{10,11},{11,10},{8... | collective-permute-start | bytes 6291464 | tf_op jit(solution)/shard_map/ppermute | solution.py:150
  292.3 33.0 %collective-permute-start.24 = (f32[4096,128]{1,0:T(8,128)}, f32[4096,128]{1,0:T(8,128)}, u32[]{:S(2)}, u32[]{:S(2)}) collective-permute-start(f32[4096,128]{1,0:T(8,128)} %collective-permute-done.8.refs_6_), channel_id=1, source_target_pairs={{2,3},{3,2},{0,1},{1,0},{4,5},{5,4},{6,7},{7,6},{10,11},{11,10},{8... | collective-permute-start | bytes 6291464 | tf_op jit(solution)/shard_map/ppermute | solution.py:150
  292.7 32.6 %collective-permute-start.23 = (f32[4096,128]{1,0:T(8,128)}, f32[4096,128]{1,0:T(8,128)}, u32[]{:S(2)}, u32[]{:S(2)}) collective-permute-start(f32[4096,128]{1,0:T(8,128)} %copy-done.22), channel_id=1, source_target_pairs={{2,3},{3,2},{0,1},{1,0},{4,5},{5,4},{6,7},{7,6},{10,11},{11,10},{8... | collective-permute-start | bytes 6291464 | tf_op jit(solution)/shard_map/ppermute | solution.py:150
  319.6 50.5 %collective-permute-start.20 = (f32[128,4096]{1,0:T(8,128)}, f32[128,4096]{1,0:T(8,128)}, u32[]{:S(2)}, u32[]{:S(2)}) collective-permute-start(f32[128,4096]{1,0:T(8,128)} %get-tuple-element.60), channel_id=1, source_target_pairs={{2,6},{3,7},{4,0},{5,1},{10,14},{11,15},{12,8},{13,9},{18,22},{19,... | collective-permute-start | bytes 6291464 | tf_op jit(solution)/shard_map/ppermute | solution.py:150
  325.3 1.0 copy-start.10
  326.4 1.0 copy-start.11
  327.4 42.6 %copy-start.13 = (f32[128,4096]{1,0:T(8,128)S(1)}, f32[128,4096]{1,0:T(8,128)}, u32[]{:S(2)}) copy-start(f32[128,4096]{1,0:T(8,128)} %copy-done.12) | copy-start | bytes 6291460
  327.4 44.8 %copy-start.3 = (f32[128,4096]{1,0:T(8,128)S(1)}, f32[128,4096]{1,0:T(8,128)}, u32[]{:S(2)}) copy-start(f32[128,4096]{1,0:T(8,128)} %copy-done.2) | copy-start | bytes 6291460
  347.4 67.4 %collective-permute-start.25 = (f32[128,4096]{1,0:T(8,128)}, f32[128,4096]{1,0:T(8,128)S(1)}, u32[]{:S(2)}, u32[]{:S(2)}) collective-permute-start(f32[128,4096]{1,0:T(8,128)} %get-tuple-element.68), channel_id=1, source_target_pairs={{2,0},{3,1},{4,6},{5,7},{10,8},{11,9},{12,14},{13,15},{18,16},{19,... | collective-permute-start | bytes 6291464 | tf_op jit(solution)/shard_map/ppermute | solution.py:150
  370.0 5.0 %copy-start.5 = (f32[128,4096]{1,0:T(8,128)S(1)}, f32[128,4096]{1,0:T(8,128)}, u32[]{:S(2)}) copy-start(f32[128,4096]{1,0:T(8,128)} %copy-done.4) | copy-start | bytes 6291460
  370.1 5.0 %copy-start.7 = (f32[128,4096]{1,0:T(8,128)S(1)}, f32[128,4096]{1,0:T(8,128)}, u32[]{:S(2)}) copy-start(f32[128,4096]{1,0:T(8,128)} %copy-done.6) | copy-start | bytes 6291460
  370.1 46.4 %collective-permute-start.21 = (f32[128,4096]{1,0:T(8,128)S(1)}, f32[128,4096]{1,0:T(8,128)}, u32[]{:S(2)}, u32[]{:S(2)}) collective-permute-start(f32[128,4096]{1,0:T(8,128)S(1)} %copy-done.13), channel_id=1, source_target_pairs={{2,4},{3,5},{4,2},{5,3},{10,12},{11,13},{12,10},{13,11},{18,20},{1... | collective-permute-start | bytes 6291464 | tf_op jit(solution)/shard_map/ppermute | solution.py:150
  414.8 2.1 copy-start.9
  (2 other events, 1.6 us)

commit v4 on v3

--- a/solution.py
+++ b/solution.py
@@ -193,12 +193,6 @@
     outer = [far(after(chunk[0], line), i) for i in spokes]
     rest = after(operator, hub)
     chunk += [rest[edges[k] : edges[k + 1]] for k in range(2, count)]
-    if width % 128 == 0:
-        other = swap(operator)
-        own = [[(operator, edges[k]), (other, edges[k])] for k in range(count)]
-    else:
-        own = [pair(operator[edges[k] : edges[k + 1]]) for k in range(count)]
-
     turns = lax.axis_size("row")
     line_row = lax.axis_index("row")
     groups, times, _ = snapshots.shape
@@ -227,14 +221,14 @@
     )
     rows_b = left_side([0, *range(half, 2 * half)], [columns] * (1 + half))
 
-    ready, totals, turned, lane = (hub,), [None], first, outer
+    ready, totals, turned, lane = (hub,), [None], first, ()
     for k in range(1, count):
         if k == 2:
             turned = [turn(after(chunk[k], *outer, sums[0]), i) for i in spokes]
             inner = [inward(after(chunk[0], *turned), i) for i in spokes]
         elif k > 2:
             turned = [turn(after(chunk[k], *inner), i) for i in spokes]
-        pieces = own[k] + [y for x in turned for y in pair(after(x, *ready))]
+        pieces = [y for x in [chunk[k], *turned] for y in pair(after(x, *ready))]
         sums = product(rows_b, pieces, edges[k + 1] - edges[k], [height] * (1 + half))
         sent = [None] * half
         for i in reversed(range(half)) if k == count - 1 else range(half):
@@ -243,7 +237,7 @@
         totals.append([sums[0], *sent])
         ready = (sums[0], sent[0])
 
-    pieces = own[0] + [y for x in [*inner, hub, *outer] for y in pair(after(x, sums[0]))]
+    pieces = [y for x in [chunk[0], *inner, hub, *outer] for y in pair(after(x, sums[0]))]
     sums = product(rows_a, pieces, edges[1], [height] * half)
     totals[0] = [sums[0]] + [outward(sums[i], i) for i in spokes]
 

time: 421 us -> 414 us (0.983)
  starting transfers between devices: 92 us -> 45.1 us
  waiting for transfers between devices: 223 us -> 259 us
    ppermute x23 -> x26, starting transfers between devices: 87.5 us -> 40.6 us  [move(): return lax.ppermute(x, 'col', pairs)]
    ppermute x23 -> x26, waiting for transfers between devices: 209 us -> 246 us  [move(): return lax.ppermute(x, 'col', pairs)]
    unnamed x48 -> x50, local copies, waits for them, and re-layouts: 11.3 us -> 12 us
  transfers between devices with their start and end apart: 26 -> 29, of which waited for: 12 -> 13; matrix products, arithmetic and copies ran while one was open for 2% -> 1% of each run, Pallas kernels for 19% -> 20%
where the time goes in v4:
time: 414 us; the launch traced here: 411 us
  waiting for transfers between devices  259 us (63%)
  Pallas kernels  85.3 us (21%)
  starting transfers between devices  45.1 us (11%)
  local copies, waits for them, and re-layouts  20.4 us (5%)
    ppermute x26, waiting for transfers between devices, move(): return lax.ppermute(x, 'col', pairs)  246 us
    pallas_call x4, Pallas kernels, product(): pl.pallas_call(kernel, grid=(modes // block,), in_specs=[pl.BlockSpec((he...  67.5 us
    ppermute x26, starting transfers between devices, move(): return lax.ppermute(x, 'col', pairs)  40.6 us
    ppermute x3, waiting for transfers between devices, shards(): lax.ppermute(line, 'row', [(r, (r + i) % turns) for r in range(turns)])  13.1 us
    unnamed x50, local copies, waits for them, and re-layouts  12 us
    pallas_call x4, Pallas kernels, put(): pl.pallas_call(kernel, grid=(span // block,), in_specs=in_specs, out_spec...  10.8 us
  transfers between devices with their start and end apart: 29, of which 13 were waited for; matrix products, arithmetic and copies ran while one was open for 1% of the time, Pallas kernels for 20%

profile of v4, /device:TPU:0, one launch (start us, length us, event | category | flops | bytes accessed | tf_op | source)
XLA Modules:
  0.0 411.2 jit_solution(9131712127190249989)
XLA Ops:
  0.0 3.9 fusion
  3.9 2.1 collective-permute-start.6
  6.0 4.4 %collective-permute-start.8 = (f32[4096,128]{1,0:T(8,128)S(1)}, f32[4096,128]{1,0:T(8,128)}, u32[]{:S(2)}, u32[]{:S(2)}) collective-permute-start(f32[4096,128]{1,0:T(8,128)S(1)} %get-tuple-element.43.refs_0_), channel_id=1, source_target_pairs={{2,0},{3,1},{0,2},{1,3},{4,6},{5,7},{6,4},{7,5},{10,8},{11,9},{8,1... | collective-permute-start | bytes 6291464 | tf_op jit(solution)/shard_map/ppermute | solution.py:150
  11.1 4.6 %collective-permute-start.2 = (f32[1,32,1024]{2,1,0:T(8,128)S(1)}, f32[1,32,1024]{2,1,0:T(8,128)S(1)}, u32[]{:S(2)}, u32[]{:S(2)}) collective-permute-start(f32[1,32,1024]{2,1,0:T(8,128)S(1)} %copy-done.24), channel_id=1, source_target_pairs={{0,4},{1,5},{6,2},{7,3},{8,12},{9,13},{14,10},{15,11},{16,20},{17,... | collective-permute-start | bytes 393224 | tf_op jit(solution)/shard_map/ppermute | solution.py:150
  15.9 43.4 %collective-permute-done.2 = f32[1,32,1024]{2,1,0:T(8,128)S(1)} collective-permute-done((f32[1,32,1024]{2,1,0:T(8,128)S(1)}, f32[1,32,1024]{2,1,0:T(8,128)S(1)}, u32[]{:S(2)}, u32[]{:S(2)}) %collective-permute-start.2) | collective-permute-done | bytes 131104 | tf_op jit(solution)/shard_map/ppermute | solution.py:150
  59.3 1.4 collective-permute-done
  60.7 1.5 collective-permute-start.3
  62.8 5.6 %collective-permute-start.12 = (f32[4096,128]{1,0:T(8,128)}, f32[4096,128]{1,0:T(8,128)}, u32[]{:S(2)}, u32[]{:S(2)}) collective-permute-start(f32[4096,128]{1,0:T(8,128)} %get-tuple-element.69.refs_0_), channel_id=1, source_target_pairs={{0,4},{1,5},{6,2},{7,3},{8,12},{9,13},{14,10},{15,11},{16,20},{17,... | collective-permute-start | bytes 6291464 | tf_op jit(solution)/shard_map/ppermute | solution.py:150
  68.4 1.5 collective-permute-start.4
  70.0 4.3 %collective-permute-done.3.refs_1_ = f32[4,1,32,1024]{3,2,1,0:T(8,128)S(1)} collective-permute-done((f32[4,1,32,1024]{3,2,1,0:T(8,128)S(1)}, f32[4,1,32,1024]{3,2,1,0:T(8,128)S(1)}, u32[]{:S(2)}, u32[]{:S(2)}) %collective-permute-start.3) | collective-permute-done | bytes 524320 | tf_op jit(solution)/shard_map/ppermute | solution.py:201
  74.3 1.4 collective-permute-start.5
  77.0 8.5 %collective-permute-done.4.refs_2_ = f32[4,1,32,1024]{3,2,1,0:T(8,128)} collective-permute-done((f32[4,1,32,1024]{3,2,1,0:T(8,128)S(1)}, f32[4,1,32,1024]{3,2,1,0:T(8,128)}, u32[]{:S(2)}, u32[]{:S(2)}) %collective-permute-start.4) | collective-permute-done | bytes 524320 | tf_op jit(solution)/shard_map/ppermute | solution.py:201
  85.8 4.0 shard_map.46
  89.8 2.6 fusion.1
  92.4 16.4 %shard_map.47 = (f32[128,4096]{1,0:T(8,128)S(1)}, f32[128,4096]{1,0:T(8,128)S(1)}, f32[128,4096]{1,0:T(8,128)}) custom-call(bf16[384,512]{1,0:T(8,128)(2,1)S(1)} %copy-done, bf16[384,512]{1,0:T(8,128)(2,1)S(1)} %copy-done.1, f32[4096,128]{1,0:T(8,128)} %copy-done.14, f32[4096,128]{1,0:T(8,128)} %collective-permute-done.7.refs_1_, ...), custom_call_target="tpu_custom_call" | custom-call | tf_op jit(solution)/shard_map/pallas_call | solution.py:88
  109.6 2.9 collective-permute-done.12.refs_6_
  112.5 3.5 collective-permute-start.13
  116.0 1.4 copy-done.2
  117.4 43.6 %collective-permute-done.13.refs_2_ = f32[4096,128]{1,0:T(8,128)S(1)} collective-permute-done((f32[4096,128]{1,0:T(8,128)S(1)}, f32[4096,128]{1,0:T(8,128)S(1)}, u32[]{:S(2)}, u32[]{:S(2)}) %collective-permute-start.13) | collective-permute-done | bytes 2097184 | tf_op jit(solution)/shard_map/ppermute | solution.py:150
  161.5 1.3 collective-permute-start.15
  162.8 6.0 %collective-permute-start.18 = (f32[4096,128]{1,0:T(8,128)}, f32[4096,128]{1,0:T(8,128)}, u32[]{:S(2)}, u32[]{:S(2)}) collective-permute-start(f32[4096,128]{1,0:T(8,128)} %get-tuple-element.69.refs_0_), channel_id=1, source_target_pairs={{0,2},{1,3},{6,4},{7,5},{8,10},{9,11},{14,12},{15,13},{16,18},{17,... | collective-permute-start | bytes 6291464 | tf_op jit(solution)/shard_map/ppermute | solution.py:150
  168.8 1.4 copy-done.21
  170.2 15.6 %shard_map.48 = (f32[128,4096]{1,0:T(8,128)S(1)}, f32[128,4096]{1,0:T(8,128)S(1)}, f32[128,4096]{1,0:T(8,128)}) custom-call(bf16[384,512]{1,0:T(8,128)(2,1)S(1)} %copy-done, bf16[384,512]{1,0:T(8,128)(2,1)S(1)} %copy-done.1, f32[4096,128]{1,0:T(8,128)} %copy-done.16, f32[4096,128]{1,0:T(8,128)} %collective-permute-done.11.refs_1_, f32[4096,128]{1,0:T(8,128)} %copy-done.19, ...), custom_call_target="tpu_custom_call" | custom-call | tf_op jit(solution)/shard_map/pallas_call | solution.py:88
  185.8 1.3 copy-done.4
  187.1 25.1 %collective-permute-done.15.refs_2_ = f32[128,4096]{1,0:T(8,128)S(1)} collective-permute-done((f32[128,4096]{1,0:T(8,128)}, f32[128,4096]{1,0:T(8,128)S(1)}, u32[]{:S(2)}, u32[]{:S(2)}) %collective-permute-start.15) | collective-permute-done | bytes 2097184 | tf_op jit(solution)/shard_map/ppermute | solution.py:150
  212.9 2.1 collective-permute-start.19
  215.0 1.3 copy-done.6
  216.3 43.5 %collective-permute-done.19.refs_2_ = f32[4096,128]{1,0:T(8,128)S(1)} collective-permute-done((f32[4096,128]{1,0:T(8,128)S(1)}, f32[4096,128]{1,0:T(8,128)S(1)}, u32[]{:S(2)}, u32[]{:S(2)}) %collective-permute-start.19) | collective-permute-done | bytes 2097184 | tf_op jit(solution)/shard_map/ppermute | solution.py:150
  260.3 1.3 collective-permute-start.21
  261.6 4.6 %collective-permute-done.20.refs_3_ = f32[4096,128]{1,0:T(8,128)S(1)} collective-permute-done((f32[4096,128]{1,0:T(8,128)S(1)}, f32[4096,128]{1,0:T(8,128)S(1)}, u32[]{:S(2)}, u32[]{:S(2)}) %collective-permute-start.20) | collective-permute-done | bytes 2097184 | tf_op jit(solution)/shard_map/ppermute | solution.py:150
  266.2 1.4 copy-done.22
  267.6 15.5 %shard_map.49 = (f32[128,4096]{1,0:T(8,128)S(1)}, f32[128,4096]{1,0:T(8,128)S(1)}, f32[128,4096]{1,0:T(8,128)}) custom-call(bf16[384,512]{1,0:T(8,128)(2,1)S(1)} %copy-done, bf16[384,512]{1,0:T(8,128)(2,1)S(1)} %copy-done.1, f32[4096,128]{1,0:T(8,128)} %copy-done.15, f32[4096,128]{1,0:T(8,128)} %collective-permute-done.17.refs_1_, f32[4096,128]{1,0:T(8,128)} %copy-done.20, ...), custom_call_target="tpu_custom_call" | custom-call | tf_op jit(solution)/shard_map/pallas_call | solution.py:88
  283.2 1.4 copy-done.8
  284.5 1.3 copy-done.12
  286.9 24.1 %collective-permute-done.21.refs_2_ = f32[128,4096]{1,0:T(8,128)} collective-permute-done((f32[128,4096]{1,0:T(8,128)}, f32[128,4096]{1,0:T(8,128)}, u32[]{:S(2)}, u32[]{:S(2)}) %collective-permute-start.21) | collective-permute-done | bytes 2097184 | tf_op jit(solution)/shard_map/ppermute | solution.py:150
  311.0 1.3 collective-permute-start.22
  313.7 3.0 shard_map.50
  316.8 1.0 copy-done.10
  317.8 1.0 copy-done.11
  318.9 20.0 %shard_map.51 = (f32[128,4096]{1,0:T(8,128)S(1)}, f32[128,4096]{1,0:T(8,128)}) custom-call(bf16[256,1024]{1,0:T(8,128)(2,1)S(1)} %copy-done.10, bf16[256,1024]{1,0:T(8,128)(2,1)S(1)} %copy-done.11, f32[4096,128]{1,0:T(8,128)} %get-tuple-element.69.refs_0_, f32[4096,128]{1,0:T(8,128)} %collective-permute-done.24.refs_1_, ...), custom_call_target="tpu_custom_call" | custom-call | tf_op jit(solution)/shard_map/pallas_call | solution.py:88
  338.8 1.3 collective-permute-start.28
  340.1 20.9 %collective-permute-done.22.refs_2_ = f32[128,4096]{1,0:T(8,128)} collective-permute-done((f32[128,4096]{1,0:T(8,128)}, f32[128,4096]{1,0:T(8,128)}, u32[]{:S(2)}, u32[]{:S(2)}) %collective-permute-start.22) | collective-permute-done | bytes 2097184 | tf_op jit(solution)/shard_map/ppermute | solution.py:150
  361.0 2.2 collective-permute-start.23
  363.2 2.8 shard_map.52.refs_3_
  366.0 2.9 shard_map.53.refs_2_
  368.9 36.8 %collective-permute-done.28.refs_1_ = f32[128,4096]{1,0:T(8,128)S(1)} collective-permute-done((f32[128,4096]{1,0:T(8,128)}, f32[128,4096]{1,0:T(8,128)S(1)}, u32[]{:S(2)}, u32[]{:S(2)}) %collective-permute-start.28) | collective-permute-done | bytes 2097184 | tf_op jit(solution)/shard_map/ppermute | solution.py:150
  405.7 1.7 shard_map.54.refs_3_
  407.8 3.4 shard_map.55
  (83 shorter events, 8.4 us)
Async XLA Ops:
  0.0 10.5 %copy-start.24 = (f32[1,32,1024]{2,1,0:T(8,128)S(1)}, f32[1,32,1024]{2,1,0:T(8,128)}, u32[]{:S(2)}) copy-start(f32[1,32,1024]{2,1,0:T(8,128)} %param.4) | copy-start | bytes 393220
  3.9 88.5 %copy-start.14 = (f32[4096,128]{1,0:T(8,128)}, f32[4096,128]{1,0:T(8,128)S(1)}, u32[]{:S(2)}) copy-start(f32[4096,128]{1,0:T(8,128)S(1)} %get-tuple-element.43.refs_0_) | copy-start | bytes 6291460
  3.9 58.4 %collective-permute-start.6 = (f32[4096,128]{1,0:T(8,128)}, f32[4096,128]{1,0:T(8,128)}, u32[]{:S(2)}, u32[]{:S(2)}) collective-permute-start(f32[4096,128]{1,0:T(8,128)} %get-tuple-element.69.refs_0_), channel_id=1, source_target_pairs={{2,4},{3,5},{4,2},{5,3},{10,12},{11,13},{12,10},{13,11},{18,20},{1... | collective-permute-start | bytes 6291464 | tf_op jit(solution)/shard_map/ppermute | solution.py:150
  6.0 56.3 %collective-permute-start.8 = (f32[4096,128]{1,0:T(8,128)S(1)}, f32[4096,128]{1,0:T(8,128)}, u32[]{:S(2)}, u32[]{:S(2)}) collective-permute-start(f32[4096,128]{1,0:T(8,128)S(1)} %get-tuple-element.43.refs_0_), channel_id=1, source_target_pairs={{2,0},{3,1},{0,2},{1,3},{4,6},{5,7},{6,4},{7,5},{10,8},{11,9},{8,1... | collective-permute-start | bytes 6291464 | tf_op jit(solution)/shard_map/ppermute | solution.py:150
  10.5 5.4 %collective-permute-start.1 = (f32[1,32,1024]{2,1,0:T(8,128)S(1)}, f32[1,32,1024]{2,1,0:T(8,128)S(1)}, u32[]{:S(2)}, u32[]{:S(2)}) collective-permute-start(f32[1,32,1024]{2,1,0:T(8,128)S(1)} %copy-done.24), channel_id=1, source_target_pairs={{2,4},{3,5},{4,2},{5,3},{10,12},{11,13},{12,10},{13,11},{18,20},{1... | collective-permute-start | bytes 393224 | tf_op jit(solution)/shard_map/ppermute | solution.py:150
  11.1 48.2 %collective-permute-start.2 = (f32[1,32,1024]{2,1,0:T(8,128)S(1)}, f32[1,32,1024]{2,1,0:T(8,128)S(1)}, u32[]{:S(2)}, u32[]{:S(2)}) collective-permute-start(f32[1,32,1024]{2,1,0:T(8,128)S(1)} %copy-done.24), channel_id=1, source_target_pairs={{0,4},{1,5},{6,2},{7,3},{8,12},{9,13},{14,10},{15,11},{16,20},{17,... | collective-permute-start | bytes 393224 | tf_op jit(solution)/shard_map/ppermute | solution.py:150
  15.8 44.9 %collective-permute-start = (f32[1,32,1024]{2,1,0:T(8,128)S(1)}, f32[1,32,1024]{2,1,0:T(8,128)S(1)}, u32[]{:S(2)}, u32[]{:S(2)}) collective-permute-start(f32[1,32,1024]{2,1,0:T(8,128)S(1)} %copy-done.24), channel_id=1, source_target_pairs={{2,0},{3,1},{0,2},{1,3},{4,6},{5,7},{6,4},{7,5},{10,8},{11,9},{8,1... | collective-permute-start | bytes 393224 | tf_op jit(solution)/shard_map/ppermute | solution.py:150
  60.7 25.1 %copy-start.17 = (f32[4,1,32,1024]{3,2,1,0:T(8,128)}, f32[4,1,32,1024]{3,2,1,0:T(8,128)S(1)}, u32[]{:S(2)}) copy-start(f32[4,1,32,1024]{3,2,1,0:T(8,128)S(1)} %pad_maximum_fusion.refs_0_) | copy-start | bytes 1572868
  60.7 13.5 %collective-permute-start.3 = (f32[4,1,32,1024]{3,2,1,0:T(8,128)S(1)}, f32[4,1,32,1024]{3,2,1,0:T(8,128)S(1)}, u32[]{:S(2)}, u32[]{:S(2)}) collective-permute-start(f32[4,1,32,1024]{3,2,1,0:T(8,128)S(1)} %pad_maximum_fusion.refs_0_), channel_id=1, source_target_pairs={{0,8},{8,16},{16,24},{24,0},{1,9},{9,17},{17,25},{25,1},{2,10},{10... | collective-permute-start | bytes 1572872 | tf_op jit(solution)/shard_map/ppermute | solution.py:201
  62.3 30.1 %collective-permute-start.9 = (f32[4096,128]{1,0:T(8,128)}, f32[4096,128]{1,0:T(8,128)}, u32[]{:S(2)}, u32[]{:S(2)}) collective-permute-start(f32[4096,128]{1,0:T(8,128)} %collective-permute-done.8.refs_2_), channel_id=1, source_target_pairs={{2,3},{3,2},{0,1},{1,0},{4,5},{5,4},{6,7},{7,6},{10,11},{11,10},{8... | collective-permute-start | bytes 6291464 | tf_op jit(solution)/shard_map/ppermute | solution.py:150
  62.3 30.1 %collective-permute-start.7 = (f32[4096,128]{1,0:T(8,128)S(1)}, f32[4096,128]{1,0:T(8,128)}, u32[]{:S(2)}, u32[]{:S(2)}) collective-permute-start(f32[4096,128]{1,0:T(8,128)S(1)} %get-tuple-element.43.refs_0_), channel_id=1, source_target_pairs={{2,3},{3,2},{0,1},{1,0},{4,5},{5,4},{6,7},{7,6},{10,11},{11,10},{8... | collective-permute-start | bytes 6291464 | tf_op jit(solution)/shard_map/ppermute | solution.py:150
  62.8 49.7 %collective-permute-start.12 = (f32[4096,128]{1,0:T(8,128)}, f32[4096,128]{1,0:T(8,128)}, u32[]{:S(2)}, u32[]{:S(2)}) collective-permute-start(f32[4096,128]{1,0:T(8,128)} %get-tuple-element.69.refs_0_), channel_id=1, source_target_pairs={{0,4},{1,5},{6,2},{7,3},{8,12},{9,13},{14,10},{15,11},{16,20},{17,... | collective-permute-start | bytes 6291464 | tf_op jit(solution)/shard_map/ppermute | solution.py:150
  68.4 17.1 %collective-permute-start.4 = (f32[4,1,32,1024]{3,2,1,0:T(8,128)S(1)}, f32[4,1,32,1024]{3,2,1,0:T(8,128)}, u32[]{:S(2)}, u32[]{:S(2)}) collective-permute-start(f32[4,1,32,1024]{3,2,1,0:T(8,128)S(1)} %pad_maximum_fusion.refs_0_), channel_id=1, source_target_pairs={{0,16},{8,24},{16,0},{24,8},{1,17},{9,25},{17,1},{25,9},{2,18},{10... | collective-permute-start | bytes 1572872 | tf_op jit(solution)/shard_map/ppermute | solution.py:201
  74.3 11.6 %copy-start.23 = (f32[4,1,32,1024]{3,2,1,0:T(8,128)}, f32[4,1,32,1024]{3,2,1,0:T(8,128)S(1)}, u32[]{:S(2)}) copy-start(f32[4,1,32,1024]{3,2,1,0:T(8,128)S(1)} %collective-permute-done.3.refs_1_) | copy-start | bytes 1572868
  74.3 11.6 %collective-permute-start.5 = (f32[4,1,32,1024]{3,2,1,0:T(8,128)S(1)}, f32[4,1,32,1024]{3,2,1,0:T(8,128)}, u32[]{:S(2)}, u32[]{:S(2)}) collective-permute-start(f32[4,1,32,1024]{3,2,1,0:T(8,128)S(1)} %pad_maximum_fusion.refs_0_), channel_id=1, source_target_pairs={{0,24},{8,0},{16,8},{24,16},{1,25},{9,1},{17,9},{25,17},{2,26},{10... | collective-permute-start | bytes 1572872 | tf_op jit(solution)/shard_map/ppermute | solution.py:201
  89.8 2.6 copy-start
  89.8 2.6 copy-start.1
  92.4 68.6 %copy-start.16 = (f32[4096,128]{1,0:T(8,128)}, f32[4096,128]{1,0:T(8,128)S(1)}, u32[]{:S(2)}) copy-start(f32[4096,128]{1,0:T(8,128)S(1)} %get-tuple-element.49.refs_0_) | copy-start | bytes 6291460
  92.4 167.4 %copy-start.15 = (f32[4096,128]{1,0:T(8,128)}, f32[4096,128]{1,0:T(8,128)S(1)}, u32[]{:S(2)}) copy-start(f32[4096,128]{1,0:T(8,128)S(1)} %get-tuple-element.58.refs_0_) | copy-start | bytes 6291460
  108.8 7.2 %collective-permute-start.10 = (f32[128,4096]{1,0:T(8,128)S(1)}, f32[128,4096]{1,0:T(8,128)S(1)}, u32[]{:S(2)}, u32[]{:S(2)}) collective-permute-start(f32[128,4096]{1,0:T(8,128)S(1)} %get-tuple-element.46), channel_id=1, source_target_pairs={{2,4},{3,5},{4,2},{5,3},{10,12},{11,13},{12,10},{13,11},{18,20},{1... | collective-permute-start | bytes 6291464 | tf_op jit(solution)/shard_map/ppermute | solution.py:150
  112.5 48.5 %collective-permute-start.13 = (f32[4096,128]{1,0:T(8,128)S(1)}, f32[4096,128]{1,0:T(8,128)S(1)}, u32[]{:S(2)}, u32[]{:S(2)}) collective-permute-start(f32[4096,128]{1,0:T(8,128)S(1)} %get-tuple-element.49.refs_0_), channel_id=1, source_target_pairs={{2,0},{3,1},{0,2},{1,3},{4,6},{5,7},{6,4},{7,5},{10,8},{11,9},{8,1... | collective-permute-start | bytes 6291464 | tf_op jit(solution)/shard_map/ppermute | solution.py:150
  116.0 1.4 copy-start.2
  161.0 7.8 %copy-start.19 = (f32[4096,128]{1,0:T(8,128)}, f32[4096,128]{1,0:T(8,128)S(1)}, u32[]{:S(2)}) copy-start(f32[4096,128]{1,0:T(8,128)S(1)} %collective-permute-done.13.refs_2_) | copy-start | bytes 6291460
  161.0 7.8 %collective-permute-start.14 = (f32[4096,128]{1,0:T(8,128)S(1)}, f32[4096,128]{1,0:T(8,128)S(1)}, u32[]{:S(2)}, u32[]{:S(2)}) collective-permute-start(f32[4096,128]{1,0:T(8,128)S(1)} %collective-permute-done.13.refs_2_), channel_id=1, source_target_pairs={{2,3},{3,2},{0,1},{1,0},{4,5},{5,4},{6,7},{7,6},{10,11},{11,10},{8... | collective-permute-start | bytes 6291464 | tf_op jit(solution)/shard_map/ppermute | solution.py:150
  161.0 9.1 %collective-permute-start.11 = (f32[4096,128]{1,0:T(8,128)S(1)}, f32[4096,128]{1,0:T(8,128)}, u32[]{:S(2)}, u32[]{:S(2)}) collective-permute-start(f32[4096,128]{1,0:T(8,128)S(1)} %get-tuple-element.49.refs_0_), channel_id=1, source_target_pairs={{2,3},{3,2},{0,1},{1,0},{4,5},{5,4},{6,7},{7,6},{10,11},{11,10},{8... | collective-permute-start | bytes 6291464 | tf_op jit(solution)/shard_map/ppermute | solution.py:150
  161.5 50.6 %collective-permute-start.15 = (f32[128,4096]{1,0:T(8,128)}, f32[128,4096]{1,0:T(8,128)S(1)}, u32[]{:S(2)}, u32[]{:S(2)}) collective-permute-start(f32[128,4096]{1,0:T(8,128)} %get-tuple-element.54), channel_id=1, source_target_pairs={{2,6},{3,7},{4,0},{5,1},{10,14},{11,15},{12,8},{13,9},{18,22},{19,... | collective-permute-start | bytes 6291464 | tf_op jit(solution)/shard_map/ppermute | solution.py:150
  162.8 50.1 %collective-permute-start.18 = (f32[4096,128]{1,0:T(8,128)}, f32[4096,128]{1,0:T(8,128)}, u32[]{:S(2)}, u32[]{:S(2)}) collective-permute-start(f32[4096,128]{1,0:T(8,128)} %get-tuple-element.69.refs_0_), channel_id=1, source_target_pairs={{0,2},{1,3},{6,4},{7,5},{8,10},{9,11},{14,12},{15,13},{16,18},{17,... | collective-permute-start | bytes 6291464 | tf_op jit(solution)/shard_map/ppermute | solution.py:150
  168.8 1.4 copy-start.21
  212.1 71.0 %copy-start.18 = (f32[128,4096]{1,0:T(8,128)}, f32[128,4096]{1,0:T(8,128)S(1)}, u32[]{:S(2)}) copy-start(f32[128,4096]{1,0:T(8,128)S(1)} %collective-permute-done.15.refs_2_) | copy-start | bytes 6291460
  212.1 2.9 collective-permute-start.16
  212.9 46.8 %collective-permute-start.19 = (f32[4096,128]{1,0:T(8,128)S(1)}, f32[4096,128]{1,0:T(8,128)S(1)}, u32[]{:S(2)}, u32[]{:S(2)}) collective-permute-start(f32[4096,128]{1,0:T(8,128)S(1)} %get-tuple-element.58.refs_0_), channel_id=1, source_target_pairs={{2,0},{3,1},{0,2},{1,3},{4,6},{5,7},{6,4},{7,5},{10,8},{11,9},{8,1... | collective-permute-start | bytes 6291464 | tf_op jit(solution)/shard_map/ppermute | solution.py:150
  259.8 7.8 %copy-start.20 = (f32[4096,128]{1,0:T(8,128)}, f32[4096,128]{1,0:T(8,128)S(1)}, u32[]{:S(2)}) copy-start(f32[4096,128]{1,0:T(8,128)S(1)} %collective-permute-done.19.refs_2_) | copy-start | bytes 6291460
  259.8 6.4 %collective-permute-start.20 = (f32[4096,128]{1,0:T(8,128)S(1)}, f32[4096,128]{1,0:T(8,128)S(1)}, u32[]{:S(2)}, u32[]{:S(2)}) collective-permute-start(f32[4096,128]{1,0:T(8,128)S(1)} %collective-permute-done.19.refs_2_), channel_id=1, source_target_pairs={{2,3},{3,2},{0,1},{1,0},{4,5},{5,4},{6,7},{7,6},{10,11},{11,10},{8... | collective-permute-start | bytes 6291464 | tf_op jit(solution)/shard_map/ppermute | solution.py:150
  259.8 7.8 %collective-permute-start.17 = (f32[4096,128]{1,0:T(8,128)S(1)}, f32[4096,128]{1,0:T(8,128)}, u32[]{:S(2)}, u32[]{:S(2)}) collective-permute-start(f32[4096,128]{1,0:T(8,128)S(1)} %get-tuple-element.58.refs_0_), channel_id=1, source_target_pairs={{2,3},{3,2},{0,1},{1,0},{4,5},{5,4},{6,7},{7,6},{10,11},{11,10},{8... | collective-permute-start | bytes 6291464 | tf_op jit(solution)/shard_map/ppermute | solution.py:150
  260.3 50.7 %collective-permute-start.21 = (f32[128,4096]{1,0:T(8,128)}, f32[128,4096]{1,0:T(8,128)}, u32[]{:S(2)}, u32[]{:S(2)}) collective-permute-start(f32[128,4096]{1,0:T(8,128)} %get-tuple-element.64), channel_id=1, source_target_pairs={{2,6},{3,7},{4,0},{5,1},{10,14},{11,15},{12,8},{13,9},{18,22},{19,... | collective-permute-start | bytes 6291464 | tf_op jit(solution)/shard_map/ppermute | solution.py:150
  266.2 1.4 copy-start.22
  285.9 30.9 %collective-permute-start.25 = (f32[4096,128]{1,0:T(8,128)}, f32[4096,128]{1,0:T(8,128)}, u32[]{:S(2)}, u32[]{:S(2)}) collective-permute-start(f32[4096,128]{1,0:T(8,128)} %collective-permute-done.18.refs_2_), channel_id=1, source_target_pairs={{2,3},{3,2},{0,1},{1,0},{4,5},{5,4},{6,7},{7,6},{10,11},{11,10},{8... | collective-permute-start | bytes 6291464 | tf_op jit(solution)/shard_map/ppermute | solution.py:150
  286.0 30.7 %collective-permute-start.27 = (f32[4096,128]{1,0:T(8,128)}, f32[4096,128]{1,0:T(8,128)}, u32[]{:S(2)}, u32[]{:S(2)}) collective-permute-start(f32[4096,128]{1,0:T(8,128)} %collective-permute-done.12.refs_6_), channel_id=1, source_target_pairs={{2,3},{3,2},{0,1},{1,0},{4,5},{5,4},{6,7},{7,6},{10,11},{11,10},{8... | collective-permute-start | bytes 6291464 | tf_op jit(solution)/shard_map/ppermute | solution.py:150
  286.4 30.4 %collective-permute-start.26 = (f32[4096,128]{1,0:T(8,128)}, f32[4096,128]{1,0:T(8,128)}, u32[]{:S(2)}, u32[]{:S(2)}) collective-permute-start(f32[4096,128]{1,0:T(8,128)} %collective-permute-done.6.refs_4_), channel_id=1, source_target_pairs={{2,3},{3,2},{0,1},{1,0},{4,5},{5,4},{6,7},{7,6},{10,11},{11,10},{8... | collective-permute-start | bytes 6291464 | tf_op jit(solution)/shard_map/ppermute | solution.py:150
  286.5 30.2 %collective-permute-start.24 = (f32[4096,128]{1,0:T(8,128)}, f32[4096,128]{1,0:T(8,128)}, u32[]{:S(2)}, u32[]{:S(2)}) collective-permute-start(f32[4096,128]{1,0:T(8,128)} %get-tuple-element.69.refs_0_), channel_id=1, source_target_pairs={{2,3},{3,2},{0,1},{1,0},{4,5},{5,4},{6,7},{7,6},{10,11},{11,10},{8... | collective-permute-start | bytes 6291464 | tf_op jit(solution)/shard_map/ppermute | solution.py:150
  311.0 50.0 %collective-permute-start.22 = (f32[128,4096]{1,0:T(8,128)}, f32[128,4096]{1,0:T(8,128)}, u32[]{:S(2)}, u32[]{:S(2)}) collective-permute-start(f32[128,4096]{1,0:T(8,128)} %get-tuple-element.65), channel_id=1, source_target_pairs={{2,6},{3,7},{4,0},{5,1},{10,14},{11,15},{12,8},{13,9},{18,22},{19,... | collective-permute-start | bytes 6291464 | tf_op jit(solution)/shard_map/ppermute | solution.py:150
  318.8 42.1 %copy-start.13 = (f32[128,4096]{1,0:T(8,128)S(1)}, f32[128,4096]{1,0:T(8,128)}, u32[]{:S(2)}) copy-start(f32[128,4096]{1,0:T(8,128)} %copy-done.12) | copy-start | bytes 6291460
  318.8 44.3 %copy-start.3 = (f32[128,4096]{1,0:T(8,128)S(1)}, f32[128,4096]{1,0:T(8,128)}, u32[]{:S(2)}) copy-start(f32[128,4096]{1,0:T(8,128)} %copy-done.2) | copy-start | bytes 6291460
  338.8 66.9 %collective-permute-start.28 = (f32[128,4096]{1,0:T(8,128)}, f32[128,4096]{1,0:T(8,128)S(1)}, u32[]{:S(2)}, u32[]{:S(2)}) collective-permute-start(f32[128,4096]{1,0:T(8,128)} %get-tuple-element.74), channel_id=1, source_target_pairs={{2,0},{3,1},{4,6},{5,7},{10,8},{11,9},{12,14},{13,15},{18,16},{19,... | collective-permute-start | bytes 6291464 | tf_op jit(solution)/shard_map/ppermute | solution.py:150
  361.0 5.1 %copy-start.5 = (f32[128,4096]{1,0:T(8,128)S(1)}, f32[128,4096]{1,0:T(8,128)}, u32[]{:S(2)}) copy-start(f32[128,4096]{1,0:T(8,128)} %copy-done.4) | copy-start | bytes 6291460
  361.0 5.1 %copy-start.7 = (f32[128,4096]{1,0:T(8,128)S(1)}, f32[128,4096]{1,0:T(8,128)}, u32[]{:S(2)}) copy-start(f32[128,4096]{1,0:T(8,128)} %copy-done.6) | copy-start | bytes 6291460
  361.0 46.4 %collective-permute-start.23 = (f32[128,4096]{1,0:T(8,128)S(1)}, f32[128,4096]{1,0:T(8,128)}, u32[]{:S(2)}, u32[]{:S(2)}) collective-permute-start(f32[128,4096]{1,0:T(8,128)S(1)} %copy-done.13), channel_id=1, source_target_pairs={{2,4},{3,5},{4,2},{5,3},{10,12},{11,13},{12,10},{13,11},{18,20},{1... | collective-permute-start | bytes 6291464 | tf_op jit(solution)/shard_map/ppermute | solution.py:150
  405.7 2.1 copy-start.9
  (6 other events, 7.4 us)

commit v5 on v4

--- a/solution.py
+++ b/solution.py
@@ -72,12 +72,35 @@
 def product(rows, pieces, modes, heights):
     depth = rows[0].shape[1]
     height = sum(heights)
-    block = math.gcd(BLOCK, modes, *(start for _, start in pieces))
-    count = len(pieces)
+    block = math.gcd(BLOCK, modes // 2, *(start for _, start in pieces))
+    steps = modes // block
+    widths = [len(arrays) for arrays, _ in pieces]
+    operands, in_specs = [], []
+    for arrays, start in pieces:
+        first, size = start // block, steps // len(arrays)
+        for j, x in enumerate(arrays):
+            operands.append(x)
+            in_specs.append(
+                pl.BlockSpec(
+                    (block, x.shape[1]),
+                    lambda i, first=first, size=size, j=j: (
+                        first + jnp.clip(i - j * size, 0, size - 1),
+                        0,
+                    ),
+                )
+            )
+    count = len(operands)
 
     def kernel(high_ref, low_ref, *refs):
-        parts = [piece[...] for piece in refs[:count]]
-        high, low = split(parts[0] if count == 1 else jnp.concatenate(parts, axis=1))
+        parts, first = [], 0
+        for size in widths:
+            part = refs[first][...]
+            if size == 2:
+                early = pl.program_id(0) < steps // 2
+                part = jnp.where(early, part, refs[first + 1][...])
+            parts.append(part)
+            first += size
+        high, low = split(parts[0] if len(parts) == 1 else jnp.concatenate(parts, axis=1))
         at = 0
         for out_ref in refs[count:]:
             span = pl.ds(at, out_ref.shape[0])
@@ -88,16 +111,12 @@
     return pl.pallas_call(
         kernel,
         grid=(modes // block,),
-        in_specs=[pl.BlockSpec((height, depth), lambda i: (0, 0))] * 2
-        + [
-            pl.BlockSpec((block, x.shape[1]), lambda i, first=start // block: (first + i, 0))
-            for x, start in pieces
-        ],
+        in_specs=[pl.BlockSpec((height, depth), lambda i: (0, 0))] * 2 + in_specs,
         out_specs=[pl.BlockSpec((h, block), lambda i: (0, i)) for h in heights],
         out_shape=[jax.ShapeDtypeStruct((h, modes), jnp.float32) for h in heights],
         compiler_params=pltpu.CompilerParams(vmem_limit_bytes=48 * 2**20),
         cost_estimate=pl.CostEstimate(flops=0, bytes_accessed=0, transcendentals=0),
-    )(*rows, *(x for x, _ in pieces))
+    )(*rows, *operands)
 
 
 def put(out, parts, start, modes):
@@ -174,12 +193,14 @@
     spokes = range(1, half)
     chunk = [operator[edges[k] : edges[k + 1]] for k in range(2)]
 
-    def pair(x):
+    def pair(x, cut=False):
         if width % 128 == 0:
-            return [(x, 0), (swap(x), 0)]
+            middle = x.shape[0] // 2
+            ends = (x[:middle], x[middle:]) if cut else (x,)
+            return [((x,), 0), (tuple(swap(end) for end in ends), 0)]
         other = swap(x)
         ends = jnp.where(core == 0, x, other), jnp.where(core == 0, other, x)
-        return [(jnp.concatenate(ends, axis=1), 0)]
+        return [((jnp.concatenate(ends, axis=1),), 0)]
 
     def places_of(chips):
         if width % 128 == 0:
@@ -228,12 +249,13 @@
             inner = [inward(after(chunk[0], *turned), i) for i in spokes]
         elif k > 2:
             turned = [turn(after(chunk[k], *inner), i) for i in spokes]
-        pieces = [y for x in [chunk[k], *turned] for y in pair(after(x, *ready))]
+        pieces = pair(after(chunk[k], *ready) if k == 1 else chunk[k])
+        pieces += [y for x in turned for y in pair(after(x, *ready), k > 1)]
         sums = product(rows_b, pieces, edges[k + 1] - edges[k], [height] * (1 + half))
         sent = [None] * half
         for i in reversed(range(half)) if k == count - 1 else range(half):
             sent[i] = across(after(sums[1 + i], *lane), i)
-            lane = [sent[i]]
+        lane = sent[-1:] if k < count - 1 else ()
         totals.append([sums[0], *sent])
         ready = (sums[0], sent[0])
 

time: 414 us -> 409 us (0.988)
  local copies, waits for them, and re-layouts: 20.4 us -> 14.8 us
  waiting for transfers between devices: 259 us -> 264 us
    unnamed x50 -> x46, local copies, waits for them, and re-layouts: 12 us -> 5.99 us
    ppermute x26 -> x28, waiting for transfers between devices: 246 us -> 251 us  [move(): return lax.ppermute(x, 'col', pairs)]
    ppermute x26 -> x28, starting transfers between devices: 40.6 us -> 39 us  [move(): return lax.ppermute(x, 'col', pairs)]
  transfers between devices with their start and end apart: 29 -> 31, of which waited for: 13 -> 15; matrix products, arithmetic and copies ran while one was open for 1% -> 1% of each run, Pallas kernels for 20% -> 20%
where the time goes in v5:
time: 409 us; the launch traced here: 408 us
  waiting for transfers between devices  264 us (65%)
  Pallas kernels  84.9 us (21%)
  starting transfers between devices  43.5 us (11%)
  local copies, waits for them, and re-layouts  14.8 us (4%)
    ppermute x28, waiting for transfers between devices, move(): return lax.ppermute(x, 'col', pairs)  251 us
    pallas_call x4, Pallas kernels, product(): pl.pallas_call(kernel, grid=(modes // block,), in_specs=[pl.BlockSpec((he...  67.1 us
    ppermute x28, starting transfers between devices, move(): return lax.ppermute(x, 'col', pairs)  39 us
    ppermute x3, waiting for transfers between devices, shards(): lax.ppermute(line, 'row', [(r, (r + i) % turns) for r in range(turns)])  13 us
    pallas_call x4, Pallas kernels, put(): pl.pallas_call(kernel, grid=(span // block,), in_specs=in_specs, out_spec...  10.8 us
  transfers between devices with their start and end apart: 31, of which 15 were waited for; matrix products, arithmetic and copies ran while one was open for 1% of the time, Pallas kernels for 20%

profile of v5, /device:TPU:0, one launch (start us, length us, event | category | flops | bytes accessed | tf_op | source)
XLA Modules:
  0.0 408.4 jit_solution(12224744480680620370)
XLA Ops:
  0.0 3.9 fusion
  3.9 2.1 collective-permute-start.6
  6.0 4.4 %collective-permute-start.10 = (f32[4096,128]{1,0:T(8,128)S(1)}, f32[4096,128]{1,0:T(8,128)}, u32[]{:S(2)}, u32[]{:S(2)}) collective-permute-start(f32[4096,128]{1,0:T(8,128)S(1)} %get-tuple-element.41.refs_0_), channel_id=1, source_target_pairs={{2,0},{3,1},{0,2},{1,3},{4,6},{5,7},{6,4},{7,5},{10,8},{11,9},{8,1... | collective-permute-start | bytes 6291464 | tf_op jit(solution)/shard_map/ppermute | solution.py:169
  11.1 4.6 %collective-permute-start.2 = (f32[1,32,1024]{2,1,0:T(8,128)S(1)}, f32[1,32,1024]{2,1,0:T(8,128)S(1)}, u32[]{:S(2)}, u32[]{:S(2)}) collective-permute-start(f32[1,32,1024]{2,1,0:T(8,128)S(1)} %copy-done.22), channel_id=1, source_target_pairs={{0,4},{1,5},{6,2},{7,3},{8,12},{9,13},{14,10},{15,11},{16,20},{17,... | collective-permute-start | bytes 393224 | tf_op jit(solution)/shard_map/ppermute | solution.py:169
  15.9 43.4 %collective-permute-done.2 = f32[1,32,1024]{2,1,0:T(8,128)S(1)} collective-permute-done((f32[1,32,1024]{2,1,0:T(8,128)S(1)}, f32[1,32,1024]{2,1,0:T(8,128)S(1)}, u32[]{:S(2)}, u32[]{:S(2)}) %collective-permute-start.2) | collective-permute-done | bytes 131104 | tf_op jit(solution)/shard_map/ppermute | solution.py:169
  59.3 1.4 collective-permute-done
  60.7 1.5 collective-permute-start.3
  62.8 5.6 %collective-permute-start.8 = (f32[4096,128]{1,0:T(8,128)}, f32[4096,128]{1,0:T(8,128)}, u32[]{:S(2)}, u32[]{:S(2)}) collective-permute-start(f32[4096,128]{1,0:T(8,128)} %get-tuple-element.63.refs_0_), channel_id=1, source_target_pairs={{0,4},{1,5},{6,2},{7,3},{8,12},{9,13},{14,10},{15,11},{16,20},{17,... | collective-permute-start | bytes 6291464 | tf_op jit(solution)/shard_map/ppermute | solution.py:169
  68.4 1.5 collective-permute-start.4
  70.0 4.3 %collective-permute-done.3.refs_1_ = f32[4,1,32,1024]{3,2,1,0:T(8,128)S(1)} collective-permute-done((f32[4,1,32,1024]{3,2,1,0:T(8,128)S(1)}, f32[4,1,32,1024]{3,2,1,0:T(8,128)S(1)}, u32[]{:S(2)}, u32[]{:S(2)}) %collective-permute-start.3) | collective-permute-done | bytes 524320 | tf_op jit(solution)/shard_map/ppermute | solution.py:222
  74.3 1.4 collective-permute-start.5
  77.1 8.4 %collective-permute-done.4.refs_2_ = f32[4,1,32,1024]{3,2,1,0:T(8,128)} collective-permute-done((f32[4,1,32,1024]{3,2,1,0:T(8,128)S(1)}, f32[4,1,32,1024]{3,2,1,0:T(8,128)}, u32[]{:S(2)}, u32[]{:S(2)}) %collective-permute-start.4) | collective-permute-done | bytes 524320 | tf_op jit(solution)/shard_map/ppermute | solution.py:222
  85.8 3.9 shard_map.46
  89.8 2.6 fusion.1
  92.4 16.3 %shard_map.47 = (f32[128,4096]{1,0:T(8,128)S(1)}, f32[128,4096]{1,0:T(8,128)S(1)}, f32[128,4096]{1,0:T(8,128)}) custom-call(bf16[384,512]{1,0:T(8,128)(2,1)S(1)} %copy-done, bf16[384,512]{1,0:T(8,128)(2,1)S(1)} %copy-done.1, f32[4096,128]{1,0:T(8,128)} %copy-done.14, f32[4096,128]{1,0:T(8,128)} %collective-permute-done.9.refs_1_, ...), custom_call_target="tpu_custom_call" | custom-call | tf_op jit(solution)/shard_map/pallas_call | solution.py:111
  108.8 3.7 collective-permute-done.8.refs_6_
  112.5 3.5 collective-permute-start.12
  116.0 0.8 collective-permute-start.16
  116.9 1.3 collective-permute-start.19
  118.2 42.8 %collective-permute-done.12.refs_2_ = f32[4096,128]{1,0:T(8,128)S(1)} collective-permute-done((f32[4096,128]{1,0:T(8,128)S(1)}, f32[4096,128]{1,0:T(8,128)S(1)}, u32[]{:S(2)}, u32[]{:S(2)}) %collective-permute-start.12) | collective-permute-done | bytes 2097184 | tf_op jit(solution)/shard_map/ppermute | solution.py:169
  161.0 5.1 %collective-permute-start.13 = (f32[4096,128]{1,0:T(8,128)}, f32[4096,128]{1,0:T(8,128)}, u32[]{:S(2)}, u32[]{:S(2)}) collective-permute-start(f32[4096,128]{1,0:T(8,128)} %get-tuple-element.63.refs_0_), channel_id=1, source_target_pairs={{0,2},{1,3},{6,4},{7,5},{8,10},{9,11},{14,12},{15,13},{16,18},{17,... | collective-permute-start | bytes 6291464 | tf_op jit(solution)/shard_map/ppermute | solution.py:169
  166.2 1.2 copy-done.2
  167.9 2.1 collective-permute-done.17.refs_3_
  170.1 1.5 collective-permute-done.18.refs_4_
  171.6 15.3 %shard_map.48 = (f32[128,4096]{1,0:T(8,128)S(1)}, f32[128,4096]{1,0:T(8,128)}, f32[128,4096]{1,0:T(8,128)}) custom-call(bf16[384,512]{1,0:T(8,128)(2,1)S(1)} %copy-done, bf16[384,512]{1,0:T(8,128)(2,1)S(1)} %copy-done.1, f32[4096,128]{1,0:T(8,128)} %copy-done.16, f32[4096,128]{1,0:T(8,128)} %copy-done.18, f32[4096,128]{1,0:T(8,128)} %copy-done.12, ...), custom_call_target="tpu_custom_call" | custom-call | tf_op jit(solution)/shard_map/pallas_call | solution.py:111
  186.9 22.2 %collective-permute-done.19.refs_2_ = f32[128,4096]{1,0:T(8,128)} collective-permute-done((f32[128,4096]{1,0:T(8,128)}, f32[128,4096]{1,0:T(8,128)}, u32[]{:S(2)}, u32[]{:S(2)}) %collective-permute-start.19) | collective-permute-done | bytes 2097184 | tf_op jit(solution)/shard_map/ppermute | solution.py:169
  209.1 0.8 collective-permute-start.20
  209.9 1.3 collective-permute-start.14
  211.2 44.6 %collective-permute-done.14.refs_2_ = f32[4096,128]{1,0:T(8,128)S(1)} collective-permute-done((f32[4096,128]{1,0:T(8,128)S(1)}, f32[4096,128]{1,0:T(8,128)S(1)}, u32[]{:S(2)}, u32[]{:S(2)}) %collective-permute-start.14) | collective-permute-done | bytes 2097184 | tf_op jit(solution)/shard_map/ppermute | solution.py:169
  256.6 1.3 collective-permute-start.23
  257.9 0.8 collective-permute-done.21.refs_3_
  258.7 1.5 collective-permute-done.22.refs_4_
  260.2 15.4 %shard_map.49 = (f32[128,4096]{1,0:T(8,128)S(1)}, f32[128,4096]{1,0:T(8,128)}, f32[128,4096]{1,0:T(8,128)}) custom-call(bf16[384,512]{1,0:T(8,128)(2,1)S(1)} %copy-done, bf16[384,512]{1,0:T(8,128)(2,1)S(1)} %copy-done.1, f32[4096,128]{1,0:T(8,128)} %copy-done.15, f32[4096,128]{1,0:T(8,128)} %copy-done.19, f32[4096,128]{1,0:T(8,128)} %copy-done.13, ...), custom_call_target="tpu_custom_call" | custom-call | tf_op jit(solution)/shard_map/pallas_call | solution.py:111
  275.6 1.4 copy-done.8
  279.4 3.0 shard_map.50
  282.4 24.9 %collective-permute-done.23.refs_2_ = f32[128,4096]{1,0:T(8,128)} collective-permute-done((f32[128,4096]{1,0:T(8,128)}, f32[128,4096]{1,0:T(8,128)}, u32[]{:S(2)}, u32[]{:S(2)}) %collective-permute-start.23) | collective-permute-done | bytes 2097184 | tf_op jit(solution)/shard_map/ppermute | solution.py:169
  307.3 1.3 collective-permute-start.25
  308.6 1.0 copy-done.10
  309.7 1.0 copy-done.11
  310.7 20.0 %shard_map.51 = (f32[128,4096]{1,0:T(8,128)S(1)}, f32[128,4096]{1,0:T(8,128)}) custom-call(bf16[256,1024]{1,0:T(8,128)(2,1)S(1)} %copy-done.10, bf16[256,1024]{1,0:T(8,128)(2,1)S(1)} %copy-done.11, f32[4096,128]{1,0:T(8,128)} %get-tuple-element.63.refs_0_, f32[4096,128]{1,0:T(8,128)} %collective-permute-done.26.refs_1_, ...), custom_call_target="tpu_custom_call" | custom-call | tf_op jit(solution)/shard_map/pallas_call | solution.py:111
  330.8 1.3 collective-permute-start.30
  332.1 2.2 collective-permute-start.24
  334.3 2.8 shard_map.52.refs_3_
  337.1 2.9 shard_map.53.refs_2_
  340.0 62.0 %collective-permute-done.30.refs_1_ = f32[128,4096]{1,0:T(8,128)S(1)} collective-permute-done((f32[128,4096]{1,0:T(8,128)}, f32[128,4096]{1,0:T(8,128)S(1)}, u32[]{:S(2)}, u32[]{:S(2)}) %collective-permute-start.30) | collective-permute-done | bytes 2097184 | tf_op jit(solution)/shard_map/ppermute | solution.py:169
  402.0 1.7 shard_map.54.refs_3_
  403.7 1.3 copy-done.21
  405.0 3.4 shard_map.55
  (85 shorter events, 6.9 us)
Async XLA Ops:
  0.0 10.5 %copy-start.22 = (f32[1,32,1024]{2,1,0:T(8,128)S(1)}, f32[1,32,1024]{2,1,0:T(8,128)}, u32[]{:S(2)}) copy-start(f32[1,32,1024]{2,1,0:T(8,128)} %param.4) | copy-start | bytes 393220
  3.9 88.5 %copy-start.14 = (f32[4096,128]{1,0:T(8,128)}, f32[4096,128]{1,0:T(8,128)S(1)}, u32[]{:S(2)}) copy-start(f32[4096,128]{1,0:T(8,128)S(1)} %get-tuple-element.41.refs_0_) | copy-start | bytes 6291460
  3.9 58.4 %collective-permute-start.6 = (f32[4096,128]{1,0:T(8,128)}, f32[4096,128]{1,0:T(8,128)}, u32[]{:S(2)}, u32[]{:S(2)}) collective-permute-start(f32[4096,128]{1,0:T(8,128)} %get-tuple-element.63.refs_0_), channel_id=1, source_target_pairs={{2,4},{3,5},{4,2},{5,3},{10,12},{11,13},{12,10},{13,11},{18,20},{1... | collective-permute-start | bytes 6291464 | tf_op jit(solution)/shard_map/ppermute | solution.py:169
  6.0 56.3 %collective-permute-start.10 = (f32[4096,128]{1,0:T(8,128)S(1)}, f32[4096,128]{1,0:T(8,128)}, u32[]{:S(2)}, u32[]{:S(2)}) collective-permute-start(f32[4096,128]{1,0:T(8,128)S(1)} %get-tuple-element.41.refs_0_), channel_id=1, source_target_pairs={{2,0},{3,1},{0,2},{1,3},{4,6},{5,7},{6,4},{7,5},{10,8},{11,9},{8,1... | collective-permute-start | bytes 6291464 | tf_op jit(solution)/shard_map/ppermute | solution.py:169
  10.5 5.4 %collective-permute-start.1 = (f32[1,32,1024]{2,1,0:T(8,128)S(1)}, f32[1,32,1024]{2,1,0:T(8,128)S(1)}, u32[]{:S(2)}, u32[]{:S(2)}) collective-permute-start(f32[1,32,1024]{2,1,0:T(8,128)S(1)} %copy-done.22), channel_id=1, source_target_pairs={{2,4},{3,5},{4,2},{5,3},{10,12},{11,13},{12,10},{13,11},{18,20},{1... | collective-permute-start | bytes 393224 | tf_op jit(solution)/shard_map/ppermute | solution.py:169
  11.1 48.2 %collective-permute-start.2 = (f32[1,32,1024]{2,1,0:T(8,128)S(1)}, f32[1,32,1024]{2,1,0:T(8,128)S(1)}, u32[]{:S(2)}, u32[]{:S(2)}) collective-permute-start(f32[1,32,1024]{2,1,0:T(8,128)S(1)} %copy-done.22), channel_id=1, source_target_pairs={{0,4},{1,5},{6,2},{7,3},{8,12},{9,13},{14,10},{15,11},{16,20},{17,... | collective-permute-start | bytes 393224 | tf_op jit(solution)/shard_map/ppermute | solution.py:169
  15.8 44.9 %collective-permute-start = (f32[1,32,1024]{2,1,0:T(8,128)S(1)}, f32[1,32,1024]{2,1,0:T(8,128)S(1)}, u32[]{:S(2)}, u32[]{:S(2)}) collective-permute-start(f32[1,32,1024]{2,1,0:T(8,128)S(1)} %copy-done.22), channel_id=1, source_target_pairs={{2,0},{3,1},{0,2},{1,3},{4,6},{5,7},{6,4},{7,5},{10,8},{11,9},{8,1... | collective-permute-start | bytes 393224 | tf_op jit(solution)/shard_map/ppermute | solution.py:169
  60.7 25.1 %copy-start.17 = (f32[4,1,32,1024]{3,2,1,0:T(8,128)}, f32[4,1,32,1024]{3,2,1,0:T(8,128)S(1)}, u32[]{:S(2)}) copy-start(f32[4,1,32,1024]{3,2,1,0:T(8,128)S(1)} %pad_maximum_fusion.refs_0_) | copy-start | bytes 1572868
  60.7 13.5 %collective-permute-start.3 = (f32[4,1,32,1024]{3,2,1,0:T(8,128)S(1)}, f32[4,1,32,1024]{3,2,1,0:T(8,128)S(1)}, u32[]{:S(2)}, u32[]{:S(2)}) collective-permute-start(f32[4,1,32,1024]{3,2,1,0:T(8,128)S(1)} %pad_maximum_fusion.refs_0_), channel_id=1, source_target_pairs={{0,8},{8,16},{16,24},{24,0},{1,9},{9,17},{17,25},{25,1},{2,10},{10... | collective-permute-start | bytes 1572872 | tf_op jit(solution)/shard_map/ppermute | solution.py:222
  62.3 30.1 %collective-permute-start.11 = (f32[4096,128]{1,0:T(8,128)}, f32[4096,128]{1,0:T(8,128)}, u32[]{:S(2)}, u32[]{:S(2)}) collective-permute-start(f32[4096,128]{1,0:T(8,128)} %collective-permute-done.10.refs_2_), channel_id=1, source_target_pairs={{2,3},{3,2},{0,1},{1,0},{4,5},{5,4},{6,7},{7,6},{10,11},{11,10},{8... | collective-permute-start | bytes 6291464 | tf_op jit(solution)/shard_map/ppermute | solution.py:169
  62.3 30.1 %collective-permute-start.9 = (f32[4096,128]{1,0:T(8,128)S(1)}, f32[4096,128]{1,0:T(8,128)}, u32[]{:S(2)}, u32[]{:S(2)}) collective-permute-start(f32[4096,128]{1,0:T(8,128)S(1)} %get-tuple-element.41.refs_0_), channel_id=1, source_target_pairs={{2,3},{3,2},{0,1},{1,0},{4,5},{5,4},{6,7},{7,6},{10,11},{11,10},{8... | collective-permute-start | bytes 6291464 | tf_op jit(solution)/shard_map/ppermute | solution.py:169
  62.8 49.7 %collective-permute-start.8 = (f32[4096,128]{1,0:T(8,128)}, f32[4096,128]{1,0:T(8,128)}, u32[]{:S(2)}, u32[]{:S(2)}) collective-permute-start(f32[4096,128]{1,0:T(8,128)} %get-tuple-element.63.refs_0_), channel_id=1, source_target_pairs={{0,4},{1,5},{6,2},{7,3},{8,12},{9,13},{14,10},{15,11},{16,20},{17,... | collective-permute-start | bytes 6291464 | tf_op jit(solution)/shard_map/ppermute | solution.py:169
  68.4 17.1 %collective-permute-start.4 = (f32[4,1,32,1024]{3,2,1,0:T(8,128)S(1)}, f32[4,1,32,1024]{3,2,1,0:T(8,128)}, u32[]{:S(2)}, u32[]{:S(2)}) collective-permute-start(f32[4,1,32,1024]{3,2,1,0:T(8,128)S(1)} %pad_maximum_fusion.refs_0_), channel_id=1, source_target_pairs={{0,16},{8,24},{16,0},{24,8},{1,17},{9,25},{17,1},{25,9},{2,18},{10... | collective-permute-start | bytes 1572872 | tf_op jit(solution)/shard_map/ppermute | solution.py:222
  74.3 11.6 %copy-start.20 = (f32[4,1,32,1024]{3,2,1,0:T(8,128)}, f32[4,1,32,1024]{3,2,1,0:T(8,128)S(1)}, u32[]{:S(2)}) copy-start(f32[4,1,32,1024]{3,2,1,0:T(8,128)S(1)} %collective-permute-done.3.refs_1_) | copy-start | bytes 1572868
  74.3 11.6 %collective-permute-start.5 = (f32[4,1,32,1024]{3,2,1,0:T(8,128)S(1)}, f32[4,1,32,1024]{3,2,1,0:T(8,128)}, u32[]{:S(2)}, u32[]{:S(2)}) collective-permute-start(f32[4,1,32,1024]{3,2,1,0:T(8,128)S(1)} %pad_maximum_fusion.refs_0_), channel_id=1, source_target_pairs={{0,24},{8,0},{16,8},{24,16},{1,25},{9,1},{17,9},{25,17},{2,26},{10... | collective-permute-start | bytes 1572872 | tf_op jit(solution)/shard_map/ppermute | solution.py:222
  89.8 2.6 copy-start
  89.8 2.6 copy-start.1
  92.4 24.4 %copy-start.16 = (f32[4096,128]{1,0:T(8,128)}, f32[4096,128]{1,0:T(8,128)S(1)}, u32[]{:S(2)}) copy-start(f32[4096,128]{1,0:T(8,128)S(1)} %get-tuple-element.44.refs_0_) | copy-start | bytes 6291460
  92.4 118.8 %copy-start.15 = (f32[4096,128]{1,0:T(8,128)}, f32[4096,128]{1,0:T(8,128)S(1)}, u32[]{:S(2)}) copy-start(f32[4096,128]{1,0:T(8,128)S(1)} %get-tuple-element.46.refs_0_) | copy-start | bytes 6291460
  112.5 48.5 %collective-permute-start.12 = (f32[4096,128]{1,0:T(8,128)S(1)}, f32[4096,128]{1,0:T(8,128)S(1)}, u32[]{:S(2)}, u32[]{:S(2)}) collective-permute-start(f32[4096,128]{1,0:T(8,128)S(1)} %get-tuple-element.44.refs_0_), channel_id=1, source_target_pairs={{2,0},{3,1},{0,2},{1,3},{4,6},{5,7},{6,4},{7,5},{10,8},{11,9},{8,1... | collective-permute-start | bytes 6291464 | tf_op jit(solution)/shard_map/ppermute | solution.py:169
  116.0 50.1 %collective-permute-start.16 = (f32[128,4096]{1,0:T(8,128)S(1)}, f32[128,4096]{1,0:T(8,128)S(1)}, u32[]{:S(2)}, u32[]{:S(2)}) collective-permute-start(f32[128,4096]{1,0:T(8,128)S(1)} %get-tuple-element.47), channel_id=1, source_target_pairs={{2,4},{3,5},{4,2},{5,3},{10,12},{11,13},{12,10},{13,11},{18,20},{1... | collective-permute-start | bytes 6291464 | tf_op jit(solution)/shard_map/ppermute | solution.py:169
  116.8 51.1 %collective-permute-start.15 = (f32[4096,128]{1,0:T(8,128)S(1)}, f32[4096,128]{1,0:T(8,128)S(1)}, u32[]{:S(2)}, u32[]{:S(2)}) collective-permute-start(f32[4096,128]{1,0:T(8,128)S(1)} %get-tuple-element.44.refs_0_), channel_id=1, source_target_pairs={{2,3},{3,2},{0,1},{1,0},{4,5},{5,4},{6,7},{7,6},{10,11},{11,10},{8... | collective-permute-start | bytes 6291464 | tf_op jit(solution)/shard_map/ppermute | solution.py:169
  116.9 92.3 %collective-permute-start.19 = (f32[128,4096]{1,0:T(8,128)}, f32[128,4096]{1,0:T(8,128)}, u32[]{:S(2)}, u32[]{:S(2)}) collective-permute-start(f32[128,4096]{1,0:T(8,128)} %get-tuple-element.51), channel_id=1, source_target_pairs={{2,6},{3,7},{4,0},{5,1},{10,14},{11,15},{12,8},{13,9},{18,22},{19,... | collective-permute-start | bytes 6291464 | tf_op jit(solution)/shard_map/ppermute | solution.py:169
  161.0 5.2 %copy-start.12 = (f32[4096,128]{1,0:T(8,128)}, f32[4096,128]{1,0:T(8,128)S(1)}, u32[]{:S(2)}) copy-start(f32[4096,128]{1,0:T(8,128)S(1)} %collective-permute-done.12.refs_2_) | copy-start | bytes 6291460
  161.0 48.9 %collective-permute-start.13 = (f32[4096,128]{1,0:T(8,128)}, f32[4096,128]{1,0:T(8,128)}, u32[]{:S(2)}, u32[]{:S(2)}) collective-permute-start(f32[4096,128]{1,0:T(8,128)} %get-tuple-element.63.refs_0_), channel_id=1, source_target_pairs={{0,2},{1,3},{6,4},{7,5},{8,10},{9,11},{14,12},{15,13},{16,18},{17,... | collective-permute-start | bytes 6291464 | tf_op jit(solution)/shard_map/ppermute | solution.py:169
  167.4 2.7 collective-permute-start.17
  167.4 4.2 %collective-permute-start.18 = (f32[2048,128]{1,0:T(8,128)S(1)}, f32[2048,128]{1,0:T(8,128)S(1)}, u32[]{:S(2)}, u32[]{:S(2)}) collective-permute-start(f32[2048,128]{1,0:T(8,128)S(1)} %get-tuple-element.75), channel_id=1, source_target_pairs={{2,3},{3,2},{0,1},{1,0},{4,5},{5,4},{6,7},{7,6},{10,11},{11,10},{8... | collective-permute-start | bytes 3145736 | tf_op jit(solution)/shard_map/ppermute | solution.py:169
  186.9 69.1 %copy-start.4 = (f32[128,4096]{1,0:T(8,128)}, f32[128,4096]{1,0:T(8,128)S(1)}, u32[]{:S(2)}) copy-start(f32[128,4096]{1,0:T(8,128)S(1)} %get-tuple-element.49.refs_0_) | copy-start | bytes 6291460
  209.1 2.1 collective-permute-start.20
  209.9 45.9 %collective-permute-start.14 = (f32[4096,128]{1,0:T(8,128)S(1)}, f32[4096,128]{1,0:T(8,128)S(1)}, u32[]{:S(2)}, u32[]{:S(2)}) collective-permute-start(f32[4096,128]{1,0:T(8,128)S(1)} %get-tuple-element.46.refs_0_), channel_id=1, source_target_pairs={{2,0},{3,1},{0,2},{1,3},{4,6},{5,7},{6,4},{7,5},{10,8},{11,9},{8,1... | collective-permute-start | bytes 6291464 | tf_op jit(solution)/shard_map/ppermute | solution.py:169
  211.2 46.7 %collective-permute-start.7 = (f32[4096,128]{1,0:T(8,128)S(1)}, f32[4096,128]{1,0:T(8,128)S(1)}, u32[]{:S(2)}, u32[]{:S(2)}) collective-permute-start(f32[4096,128]{1,0:T(8,128)S(1)} %get-tuple-element.46.refs_0_), channel_id=1, source_target_pairs={{2,3},{3,2},{0,1},{1,0},{4,5},{5,4},{6,7},{7,6},{10,11},{11,10},{8... | collective-permute-start | bytes 6291464 | tf_op jit(solution)/shard_map/ppermute | solution.py:169
  211.2 44.8 %copy-start.6 = (f32[128,4096]{1,0:T(8,128)}, f32[128,4096]{1,0:T(8,128)S(1)}, u32[]{:S(2)}) copy-start(f32[128,4096]{1,0:T(8,128)S(1)} %collective-permute-done.20.refs_1_) | copy-start | bytes 6291460
  255.8 4.4 %copy-start.13 = (f32[4096,128]{1,0:T(8,128)}, f32[4096,128]{1,0:T(8,128)S(1)}, u32[]{:S(2)}) copy-start(f32[4096,128]{1,0:T(8,128)S(1)} %collective-permute-done.14.refs_2_) | copy-start | bytes 6291460
  256.0 2.7 collective-permute-start.21
  256.1 4.1 %collective-permute-start.22 = (f32[2048,128]{1,0:T(8,128)S(1)}, f32[2048,128]{1,0:T(8,128)S(1)}, u32[]{:S(2)}, u32[]{:S(2)}) collective-permute-start(f32[2048,128]{1,0:T(8,128)S(1)} %get-tuple-element.73), channel_id=1, source_target_pairs={{2,3},{3,2},{0,1},{1,0},{4,5},{5,4},{6,7},{7,6},{10,11},{11,10},{8... | collective-permute-start | bytes 3145736 | tf_op jit(solution)/shard_map/ppermute | solution.py:169
  256.6 50.7 %collective-permute-start.23 = (f32[128,4096]{1,0:T(8,128)}, f32[128,4096]{1,0:T(8,128)}, u32[]{:S(2)}, u32[]{:S(2)}) collective-permute-start(f32[128,4096]{1,0:T(8,128)} %get-tuple-element.57), channel_id=1, source_target_pairs={{2,6},{3,7},{4,0},{5,1},{10,14},{11,15},{12,8},{13,9},{18,22},{19,... | collective-permute-start | bytes 6291464 | tf_op jit(solution)/shard_map/ppermute | solution.py:169
  257.9 2.4 copy-start.19
  277.0 31.6 %collective-permute-start.27 = (f32[4096,128]{1,0:T(8,128)}, f32[4096,128]{1,0:T(8,128)}, u32[]{:S(2)}, u32[]{:S(2)}) collective-permute-start(f32[4096,128]{1,0:T(8,128)} %collective-permute-done.13.refs_2_), channel_id=1, source_target_pairs={{2,3},{3,2},{0,1},{1,0},{4,5},{5,4},{6,7},{7,6},{10,11},{11,10},{8... | collective-permute-start | bytes 6291464 | tf_op jit(solution)/shard_map/ppermute | solution.py:169
  277.1 31.5 %collective-permute-start.29 = (f32[4096,128]{1,0:T(8,128)}, f32[4096,128]{1,0:T(8,128)}, u32[]{:S(2)}, u32[]{:S(2)}) collective-permute-start(f32[4096,128]{1,0:T(8,128)} %collective-permute-done.8.refs_6_), channel_id=1, source_target_pairs={{2,3},{3,2},{0,1},{1,0},{4,5},{5,4},{6,7},{7,6},{10,11},{11,10},{8... | collective-permute-start | bytes 6291464 | tf_op jit(solution)/shard_map/ppermute | solution.py:169
  277.5 31.1 %collective-permute-start.28 = (f32[4096,128]{1,0:T(8,128)}, f32[4096,128]{1,0:T(8,128)}, u32[]{:S(2)}, u32[]{:S(2)}) collective-permute-start(f32[4096,128]{1,0:T(8,128)} %collective-permute-done.6.refs_4_), channel_id=1, source_target_pairs={{2,3},{3,2},{0,1},{1,0},{4,5},{5,4},{6,7},{7,6},{10,11},{11,10},{8... | collective-permute-start | bytes 6291464 | tf_op jit(solution)/shard_map/ppermute | solution.py:169
  277.6 31.0 %collective-permute-start.26 = (f32[4096,128]{1,0:T(8,128)}, f32[4096,128]{1,0:T(8,128)}, u32[]{:S(2)}, u32[]{:S(2)}) collective-permute-start(f32[4096,128]{1,0:T(8,128)} %get-tuple-element.63.refs_0_), channel_id=1, source_target_pairs={{2,3},{3,2},{0,1},{1,0},{4,5},{5,4},{6,7},{7,6},{10,11},{11,10},{8... | collective-permute-start | bytes 6291464 | tf_op jit(solution)/shard_map/ppermute | solution.py:169
  307.3 96.4 %collective-permute-start.25 = (f32[128,4096]{1,0:T(8,128)}, f32[128,4096]{1,0:T(8,128)S(1)}, u32[]{:S(2)}, u32[]{:S(2)}) collective-permute-start(f32[128,4096]{1,0:T(8,128)} %get-tuple-element.60), channel_id=1, source_target_pairs={{2,6},{3,7},{4,0},{5,1},{10,14},{11,15},{12,8},{13,9},{18,22},{19,... | collective-permute-start | bytes 6291464 | tf_op jit(solution)/shard_map/ppermute | solution.py:169
  310.7 23.6 %copy-start.3 = (f32[128,4096]{1,0:T(8,128)S(1)}, f32[128,4096]{1,0:T(8,128)}, u32[]{:S(2)}) copy-start(f32[128,4096]{1,0:T(8,128)} %copy-done.2) | copy-start | bytes 6291460
  330.8 71.2 %collective-permute-start.30 = (f32[128,4096]{1,0:T(8,128)}, f32[128,4096]{1,0:T(8,128)S(1)}, u32[]{:S(2)}, u32[]{:S(2)}) collective-permute-start(f32[128,4096]{1,0:T(8,128)} %get-tuple-element.68), channel_id=1, source_target_pairs={{2,0},{3,1},{4,6},{5,7},{10,8},{11,9},{12,14},{13,15},{18,16},{19,... | collective-permute-start | bytes 6291464 | tf_op jit(solution)/shard_map/ppermute | solution.py:169
  332.0 5.1 %copy-start.5 = (f32[128,4096]{1,0:T(8,128)S(1)}, f32[128,4096]{1,0:T(8,128)}, u32[]{:S(2)}) copy-start(f32[128,4096]{1,0:T(8,128)} %copy-done.4) | copy-start | bytes 6291460
  332.1 5.1 %copy-start.7 = (f32[128,4096]{1,0:T(8,128)S(1)}, f32[128,4096]{1,0:T(8,128)}, u32[]{:S(2)}) copy-start(f32[128,4096]{1,0:T(8,128)} %copy-done.6) | copy-start | bytes 6291460
  332.1 71.7 %collective-permute-start.24 = (f32[128,4096]{1,0:T(8,128)}, f32[128,4096]{1,0:T(8,128)}, u32[]{:S(2)}, u32[]{:S(2)}) collective-permute-start(f32[128,4096]{1,0:T(8,128)} %get-tuple-element.58), channel_id=1, source_target_pairs={{2,4},{3,5},{4,2},{5,3},{10,12},{11,13},{12,10},{13,11},{18,20},{1... | collective-permute-start | bytes 6291464 | tf_op jit(solution)/shard_map/ppermute | solution.py:169
  402.0 3.0 copy-start.9
  (6 other events, 8.2 us)

commit v6 on v5

--- a/solution.py
+++ b/solution.py
@@ -121,7 +121,7 @@
 
 def put(out, parts, start, modes):
     height, span = parts[0].shape
-    block = math.gcd(math.gcd(4 * BLOCK, span), start or span)
+    block = math.gcd(math.gcd(8 * BLOCK, span), start or span)
     first = start // block
     count = len(parts)
 

time: 409 us -> 409 us (level)
  no operation moved by 1% of the time
where the time goes in v6:
time: 409 us
  waiting for transfers between devices  263 us (64%)
  Pallas kernels  85.9 us (21%)
  starting transfers between devices  43.5 us (11%)
  local copies, waits for them, and re-layouts  14.8 us (4%)
    ppermute x28, waiting for transfers between devices, move(): return lax.ppermute(x, 'col', pairs)  250 us
    pallas_call x4, Pallas kernels, product(): pl.pallas_call(kernel, grid=(modes // block,), in_specs=[pl.BlockSpec((he...  67.1 us
    ppermute x28, starting transfers between devices, move(): return lax.ppermute(x, 'col', pairs)  39 us
    ppermute x3, waiting for transfers between devices, shards(): lax.ppermute(line, 'row', [(r, (r + i) % turns) for r in range(turns)])  13 us
    pallas_call x4, Pallas kernels, put(): pl.pallas_call(kernel, grid=(span // block,), in_specs=in_specs, out_spec...  11.8 us
  transfers between devices with their start and end apart: 31, of which 15 were waited for; matrix products, arithmetic and copies ran while one was open for 1% of the time, Pallas kernels for 20%

profile of v6, /device:TPU:0, one launch (start us, length us, event | category | flops | bytes accessed | tf_op | source)
XLA Modules:
  0.0 408.7 jit_solution(12271328581941540608)
XLA Ops:
  0.0 3.9 fusion
  3.9 2.1 collective-permute-start.6
  6.0 4.4 %collective-permute-start.10 = (f32[4096,128]{1,0:T(8,128)S(1)}, f32[4096,128]{1,0:T(8,128)}, u32[]{:S(2)}, u32[]{:S(2)}) collective-permute-start(f32[4096,128]{1,0:T(8,128)S(1)} %get-tuple-element.41.refs_0_), channel_id=1, source_target_pairs={{2,0},{3,1},{0,2},{1,3},{4,6},{5,7},{6,4},{7,5},{10,8},{11,9},{8,1... | collective-permute-start | bytes 6291464 | tf_op jit(solution)/shard_map/ppermute | solution.py:169
  11.1 4.6 %collective-permute-start.2 = (f32[1,32,1024]{2,1,0:T(8,128)S(1)}, f32[1,32,1024]{2,1,0:T(8,128)S(1)}, u32[]{:S(2)}, u32[]{:S(2)}) collective-permute-start(f32[1,32,1024]{2,1,0:T(8,128)S(1)} %copy-done.22), channel_id=1, source_target_pairs={{0,4},{1,5},{6,2},{7,3},{8,12},{9,13},{14,10},{15,11},{16,20},{17,... | collective-permute-start | bytes 393224 | tf_op jit(solution)/shard_map/ppermute | solution.py:169
  15.9 43.4 %collective-permute-done.2 = f32[1,32,1024]{2,1,0:T(8,128)S(1)} collective-permute-done((f32[1,32,1024]{2,1,0:T(8,128)S(1)}, f32[1,32,1024]{2,1,0:T(8,128)S(1)}, u32[]{:S(2)}, u32[]{:S(2)}) %collective-permute-start.2) | collective-permute-done | bytes 131104 | tf_op jit(solution)/shard_map/ppermute | solution.py:169
  59.3 1.4 collective-permute-done
  60.7 1.5 collective-permute-start.3
  62.8 5.6 %collective-permute-start.8 = (f32[4096,128]{1,0:T(8,128)}, f32[4096,128]{1,0:T(8,128)}, u32[]{:S(2)}, u32[]{:S(2)}) collective-permute-start(f32[4096,128]{1,0:T(8,128)} %get-tuple-element.63.refs_0_), channel_id=1, source_target_pairs={{0,4},{1,5},{6,2},{7,3},{8,12},{9,13},{14,10},{15,11},{16,20},{17,... | collective-permute-start | bytes 6291464 | tf_op jit(solution)/shard_map/ppermute | solution.py:169
  68.4 1.5 collective-permute-start.4
  70.0 4.3 %collective-permute-done.3.refs_1_ = f32[4,1,32,1024]{3,2,1,0:T(8,128)S(1)} collective-permute-done((f32[4,1,32,1024]{3,2,1,0:T(8,128)S(1)}, f32[4,1,32,1024]{3,2,1,0:T(8,128)S(1)}, u32[]{:S(2)}, u32[]{:S(2)}) %collective-permute-start.3) | collective-permute-done | bytes 524320 | tf_op jit(solution)/shard_map/ppermute | solution.py:222
  74.3 1.4 collective-permute-start.5
  77.1 8.4 %collective-permute-done.4.refs_2_ = f32[4,1,32,1024]{3,2,1,0:T(8,128)} collective-permute-done((f32[4,1,32,1024]{3,2,1,0:T(8,128)S(1)}, f32[4,1,32,1024]{3,2,1,0:T(8,128)}, u32[]{:S(2)}, u32[]{:S(2)}) %collective-permute-start.4) | collective-permute-done | bytes 524320 | tf_op jit(solution)/shard_map/ppermute | solution.py:222
  85.8 3.9 shard_map.46
  89.8 2.6 fusion.1
  92.4 16.3 %shard_map.47 = (f32[128,4096]{1,0:T(8,128)S(1)}, f32[128,4096]{1,0:T(8,128)S(1)}, f32[128,4096]{1,0:T(8,128)}) custom-call(bf16[384,512]{1,0:T(8,128)(2,1)S(1)} %copy-done, bf16[384,512]{1,0:T(8,128)(2,1)S(1)} %copy-done.1, f32[4096,128]{1,0:T(8,128)} %copy-done.14, f32[4096,128]{1,0:T(8,128)} %collective-permute-done.9.refs_1_, ...), custom_call_target="tpu_custom_call" | custom-call | tf_op jit(solution)/shard_map/pallas_call | solution.py:111
  108.8 3.7 collective-permute-done.8.refs_6_
  112.5 3.5 collective-permute-start.12
  116.0 0.8 collective-permute-start.16
  116.9 1.3 collective-permute-start.19
  118.2 42.8 %collective-permute-done.12.refs_2_ = f32[4096,128]{1,0:T(8,128)S(1)} collective-permute-done((f32[4096,128]{1,0:T(8,128)S(1)}, f32[4096,128]{1,0:T(8,128)S(1)}, u32[]{:S(2)}, u32[]{:S(2)}) %collective-permute-start.12) | collective-permute-done | bytes 2097184 | tf_op jit(solution)/shard_map/ppermute | solution.py:169
  161.0 5.1 %collective-permute-start.13 = (f32[4096,128]{1,0:T(8,128)}, f32[4096,128]{1,0:T(8,128)}, u32[]{:S(2)}, u32[]{:S(2)}) collective-permute-start(f32[4096,128]{1,0:T(8,128)} %get-tuple-element.63.refs_0_), channel_id=1, source_target_pairs={{0,2},{1,3},{6,4},{7,5},{8,10},{9,11},{14,12},{15,13},{16,18},{17,... | collective-permute-start | bytes 6291464 | tf_op jit(solution)/shard_map/ppermute | solution.py:169
  166.2 1.2 copy-done.2
  167.9 2.1 collective-permute-done.17.refs_3_
  170.1 1.5 collective-permute-done.18.refs_4_
  171.6 15.3 %shard_map.48 = (f32[128,4096]{1,0:T(8,128)S(1)}, f32[128,4096]{1,0:T(8,128)}, f32[128,4096]{1,0:T(8,128)}) custom-call(bf16[384,512]{1,0:T(8,128)(2,1)S(1)} %copy-done, bf16[384,512]{1,0:T(8,128)(2,1)S(1)} %copy-done.1, f32[4096,128]{1,0:T(8,128)} %copy-done.16, f32[4096,128]{1,0:T(8,128)} %copy-done.18, f32[4096,128]{1,0:T(8,128)} %copy-done.12, ...), custom_call_target="tpu_custom_call" | custom-call | tf_op jit(solution)/shard_map/pallas_call | solution.py:111
  186.9 22.2 %collective-permute-done.19.refs_2_ = f32[128,4096]{1,0:T(8,128)} collective-permute-done((f32[128,4096]{1,0:T(8,128)}, f32[128,4096]{1,0:T(8,128)}, u32[]{:S(2)}, u32[]{:S(2)}) %collective-permute-start.19) | collective-permute-done | bytes 2097184 | tf_op jit(solution)/shard_map/ppermute | solution.py:169
  209.1 0.8 collective-permute-start.20
  209.9 1.3 collective-permute-start.14
  211.2 44.6 %collective-permute-done.14.refs_2_ = f32[4096,128]{1,0:T(8,128)S(1)} collective-permute-done((f32[4096,128]{1,0:T(8,128)S(1)}, f32[4096,128]{1,0:T(8,128)S(1)}, u32[]{:S(2)}, u32[]{:S(2)}) %collective-permute-start.14) | collective-permute-done | bytes 2097184 | tf_op jit(solution)/shard_map/ppermute | solution.py:169
  256.6 1.3 collective-permute-start.23
  257.9 0.8 collective-permute-done.21.refs_3_
  258.7 1.5 collective-permute-done.22.refs_4_
  260.2 15.4 %shard_map.49 = (f32[128,4096]{1,0:T(8,128)S(1)}, f32[128,4096]{1,0:T(8,128)}, f32[128,4096]{1,0:T(8,128)}) custom-call(bf16[384,512]{1,0:T(8,128)(2,1)S(1)} %copy-done, bf16[384,512]{1,0:T(8,128)(2,1)S(1)} %copy-done.1, f32[4096,128]{1,0:T(8,128)} %copy-done.15, f32[4096,128]{1,0:T(8,128)} %copy-done.19, f32[4096,128]{1,0:T(8,128)} %copy-done.13, ...), custom_call_target="tpu_custom_call" | custom-call | tf_op jit(solution)/shard_map/pallas_call | solution.py:111
  275.6 1.4 copy-done.8
  279.4 3.0 shard_map.50
  282.4 24.9 %collective-permute-done.23.refs_2_ = f32[128,4096]{1,0:T(8,128)} collective-permute-done((f32[128,4096]{1,0:T(8,128)}, f32[128,4096]{1,0:T(8,128)}, u32[]{:S(2)}, u32[]{:S(2)}) %collective-permute-start.23) | collective-permute-done | bytes 2097184 | tf_op jit(solution)/shard_map/ppermute | solution.py:169
  307.3 1.3 collective-permute-start.25
  308.6 1.0 copy-done.10
  309.7 1.0 copy-done.11
  310.7 20.0 %shard_map.51 = (f32[128,4096]{1,0:T(8,128)S(1)}, f32[128,4096]{1,0:T(8,128)}) custom-call(bf16[256,1024]{1,0:T(8,128)(2,1)S(1)} %copy-done.10, bf16[256,1024]{1,0:T(8,128)(2,1)S(1)} %copy-done.11, f32[4096,128]{1,0:T(8,128)} %get-tuple-element.63.refs_0_, f32[4096,128]{1,0:T(8,128)} %collective-permute-done.26.refs_1_, ...), custom_call_target="tpu_custom_call" | custom-call | tf_op jit(solution)/shard_map/pallas_call | solution.py:111
  330.8 1.3 collective-permute-start.30
  332.1 2.2 collective-permute-start.24
  334.3 3.2 shard_map.52.refs_3_
  337.5 3.2 shard_map.53.refs_2_
  340.7 61.3 %collective-permute-done.30.refs_1_ = f32[128,4096]{1,0:T(8,128)S(1)} collective-permute-done((f32[128,4096]{1,0:T(8,128)}, f32[128,4096]{1,0:T(8,128)S(1)}, u32[]{:S(2)}, u32[]{:S(2)}) %collective-permute-start.30) | collective-permute-done | bytes 2097184 | tf_op jit(solution)/shard_map/ppermute | solution.py:169
  402.0 1.5 shard_map.54.refs_3_
  403.5 1.3 copy-done.21
  404.8 3.8 shard_map.55
  (85 shorter events, 6.9 us)
Async XLA Ops:
  0.0 10.5 %copy-start.22 = (f32[1,32,1024]{2,1,0:T(8,128)S(1)}, f32[1,32,1024]{2,1,0:T(8,128)}, u32[]{:S(2)}) copy-start(f32[1,32,1024]{2,1,0:T(8,128)} %param.4) | copy-start | bytes 393220
  3.9 88.5 %copy-start.14 = (f32[4096,128]{1,0:T(8,128)}, f32[4096,128]{1,0:T(8,128)S(1)}, u32[]{:S(2)}) copy-start(f32[4096,128]{1,0:T(8,128)S(1)} %get-tuple-element.41.refs_0_) | copy-start | bytes 6291460
  3.9 58.4 %collective-permute-start.6 = (f32[4096,128]{1,0:T(8,128)}, f32[4096,128]{1,0:T(8,128)}, u32[]{:S(2)}, u32[]{:S(2)}) collective-permute-start(f32[4096,128]{1,0:T(8,128)} %get-tuple-element.63.refs_0_), channel_id=1, source_target_pairs={{2,4},{3,5},{4,2},{5,3},{10,12},{11,13},{12,10},{13,11},{18,20},{1... | collective-permute-start | bytes 6291464 | tf_op jit(solution)/shard_map/ppermute | solution.py:169
  6.0 56.3 %collective-permute-start.10 = (f32[4096,128]{1,0:T(8,128)S(1)}, f32[4096,128]{1,0:T(8,128)}, u32[]{:S(2)}, u32[]{:S(2)}) collective-permute-start(f32[4096,128]{1,0:T(8,128)S(1)} %get-tuple-element.41.refs_0_), channel_id=1, source_target_pairs={{2,0},{3,1},{0,2},{1,3},{4,6},{5,7},{6,4},{7,5},{10,8},{11,9},{8,1... | collective-permute-start | bytes 6291464 | tf_op jit(solution)/shard_map/ppermute | solution.py:169
  10.5 5.4 %collective-permute-start.1 = (f32[1,32,1024]{2,1,0:T(8,128)S(1)}, f32[1,32,1024]{2,1,0:T(8,128)S(1)}, u32[]{:S(2)}, u32[]{:S(2)}) collective-permute-start(f32[1,32,1024]{2,1,0:T(8,128)S(1)} %copy-done.22), channel_id=1, source_target_pairs={{2,4},{3,5},{4,2},{5,3},{10,12},{11,13},{12,10},{13,11},{18,20},{1... | collective-permute-start | bytes 393224 | tf_op jit(solution)/shard_map/ppermute | solution.py:169
  11.1 48.2 %collective-permute-start.2 = (f32[1,32,1024]{2,1,0:T(8,128)S(1)}, f32[1,32,1024]{2,1,0:T(8,128)S(1)}, u32[]{:S(2)}, u32[]{:S(2)}) collective-permute-start(f32[1,32,1024]{2,1,0:T(8,128)S(1)} %copy-done.22), channel_id=1, source_target_pairs={{0,4},{1,5},{6,2},{7,3},{8,12},{9,13},{14,10},{15,11},{16,20},{17,... | collective-permute-start | bytes 393224 | tf_op jit(solution)/shard_map/ppermute | solution.py:169
  15.8 44.9 %collective-permute-start = (f32[1,32,1024]{2,1,0:T(8,128)S(1)}, f32[1,32,1024]{2,1,0:T(8,128)S(1)}, u32[]{:S(2)}, u32[]{:S(2)}) collective-permute-start(f32[1,32,1024]{2,1,0:T(8,128)S(1)} %copy-done.22), channel_id=1, source_target_pairs={{2,0},{3,1},{0,2},{1,3},{4,6},{5,7},{6,4},{7,5},{10,8},{11,9},{8,1... | collective-permute-start | bytes 393224 | tf_op jit(solution)/shard_map/ppermute | solution.py:169
  60.7 25.1 %copy-start.17 = (f32[4,1,32,1024]{3,2,1,0:T(8,128)}, f32[4,1,32,1024]{3,2,1,0:T(8,128)S(1)}, u32[]{:S(2)}) copy-start(f32[4,1,32,1024]{3,2,1,0:T(8,128)S(1)} %pad_maximum_fusion.refs_0_) | copy-start | bytes 1572868
  60.7 13.5 %collective-permute-start.3 = (f32[4,1,32,1024]{3,2,1,0:T(8,128)S(1)}, f32[4,1,32,1024]{3,2,1,0:T(8,128)S(1)}, u32[]{:S(2)}, u32[]{:S(2)}) collective-permute-start(f32[4,1,32,1024]{3,2,1,0:T(8,128)S(1)} %pad_maximum_fusion.refs_0_), channel_id=1, source_target_pairs={{0,8},{8,16},{16,24},{24,0},{1,9},{9,17},{17,25},{25,1},{2,10},{10... | collective-permute-start | bytes 1572872 | tf_op jit(solution)/shard_map/ppermute | solution.py:222
  62.3 30.1 %collective-permute-start.11 = (f32[4096,128]{1,0:T(8,128)}, f32[4096,128]{1,0:T(8,128)}, u32[]{:S(2)}, u32[]{:S(2)}) collective-permute-start(f32[4096,128]{1,0:T(8,128)} %collective-permute-done.10.refs_2_), channel_id=1, source_target_pairs={{2,3},{3,2},{0,1},{1,0},{4,5},{5,4},{6,7},{7,6},{10,11},{11,10},{8... | collective-permute-start | bytes 6291464 | tf_op jit(solution)/shard_map/ppermute | solution.py:169
  62.3 30.1 %collective-permute-start.9 = (f32[4096,128]{1,0:T(8,128)S(1)}, f32[4096,128]{1,0:T(8,128)}, u32[]{:S(2)}, u32[]{:S(2)}) collective-permute-start(f32[4096,128]{1,0:T(8,128)S(1)} %get-tuple-element.41.refs_0_), channel_id=1, source_target_pairs={{2,3},{3,2},{0,1},{1,0},{4,5},{5,4},{6,7},{7,6},{10,11},{11,10},{8... | collective-permute-start | bytes 6291464 | tf_op jit(solution)/shard_map/ppermute | solution.py:169
  62.8 49.7 %collective-permute-start.8 = (f32[4096,128]{1,0:T(8,128)}, f32[4096,128]{1,0:T(8,128)}, u32[]{:S(2)}, u32[]{:S(2)}) collective-permute-start(f32[4096,128]{1,0:T(8,128)} %get-tuple-element.63.refs_0_), channel_id=1, source_target_pairs={{0,4},{1,5},{6,2},{7,3},{8,12},{9,13},{14,10},{15,11},{16,20},{17,... | collective-permute-start | bytes 6291464 | tf_op jit(solution)/shard_map/ppermute | solution.py:169
  68.4 17.1 %collective-permute-start.4 = (f32[4,1,32,1024]{3,2,1,0:T(8,128)S(1)}, f32[4,1,32,1024]{3,2,1,0:T(8,128)}, u32[]{:S(2)}, u32[]{:S(2)}) collective-permute-start(f32[4,1,32,1024]{3,2,1,0:T(8,128)S(1)} %pad_maximum_fusion.refs_0_), channel_id=1, source_target_pairs={{0,16},{8,24},{16,0},{24,8},{1,17},{9,25},{17,1},{25,9},{2,18},{10... | collective-permute-start | bytes 1572872 | tf_op jit(solution)/shard_map/ppermute | solution.py:222
  74.3 11.6 %copy-start.20 = (f32[4,1,32,1024]{3,2,1,0:T(8,128)}, f32[4,1,32,1024]{3,2,1,0:T(8,128)S(1)}, u32[]{:S(2)}) copy-start(f32[4,1,32,1024]{3,2,1,0:T(8,128)S(1)} %collective-permute-done.3.refs_1_) | copy-start | bytes 1572868
  74.3 11.6 %collective-permute-start.5 = (f32[4,1,32,1024]{3,2,1,0:T(8,128)S(1)}, f32[4,1,32,1024]{3,2,1,0:T(8,128)}, u32[]{:S(2)}, u32[]{:S(2)}) collective-permute-start(f32[4,1,32,1024]{3,2,1,0:T(8,128)S(1)} %pad_maximum_fusion.refs_0_), channel_id=1, source_target_pairs={{0,24},{8,0},{16,8},{24,16},{1,25},{9,1},{17,9},{25,17},{2,26},{10... | collective-permute-start | bytes 1572872 | tf_op jit(solution)/shard_map/ppermute | solution.py:222
  89.8 2.6 copy-start
  89.8 2.6 copy-start.1
  92.4 24.4 %copy-start.16 = (f32[4096,128]{1,0:T(8,128)}, f32[4096,128]{1,0:T(8,128)S(1)}, u32[]{:S(2)}) copy-start(f32[4096,128]{1,0:T(8,128)S(1)} %get-tuple-element.44.refs_0_) | copy-start | bytes 6291460
  92.4 118.8 %copy-start.15 = (f32[4096,128]{1,0:T(8,128)}, f32[4096,128]{1,0:T(8,128)S(1)}, u32[]{:S(2)}) copy-start(f32[4096,128]{1,0:T(8,128)S(1)} %get-tuple-element.46.refs_0_) | copy-start | bytes 6291460
  112.5 48.5 %collective-permute-start.12 = (f32[4096,128]{1,0:T(8,128)S(1)}, f32[4096,128]{1,0:T(8,128)S(1)}, u32[]{:S(2)}, u32[]{:S(2)}) collective-permute-start(f32[4096,128]{1,0:T(8,128)S(1)} %get-tuple-element.44.refs_0_), channel_id=1, source_target_pairs={{2,0},{3,1},{0,2},{1,3},{4,6},{5,7},{6,4},{7,5},{10,8},{11,9},{8,1... | collective-permute-start | bytes 6291464 | tf_op jit(solution)/shard_map/ppermute | solution.py:169
  116.0 50.1 %collective-permute-start.16 = (f32[128,4096]{1,0:T(8,128)S(1)}, f32[128,4096]{1,0:T(8,128)S(1)}, u32[]{:S(2)}, u32[]{:S(2)}) collective-permute-start(f32[128,4096]{1,0:T(8,128)S(1)} %get-tuple-element.47), channel_id=1, source_target_pairs={{2,4},{3,5},{4,2},{5,3},{10,12},{11,13},{12,10},{13,11},{18,20},{1... | collective-permute-start | bytes 6291464 | tf_op jit(solution)/shard_map/ppermute | solution.py:169
  116.8 51.1 %collective-permute-start.15 = (f32[4096,128]{1,0:T(8,128)S(1)}, f32[4096,128]{1,0:T(8,128)S(1)}, u32[]{:S(2)}, u32[]{:S(2)}) collective-permute-start(f32[4096,128]{1,0:T(8,128)S(1)} %get-tuple-element.44.refs_0_), channel_id=1, source_target_pairs={{2,3},{3,2},{0,1},{1,0},{4,5},{5,4},{6,7},{7,6},{10,11},{11,10},{8... | collective-permute-start | bytes 6291464 | tf_op jit(solution)/shard_map/ppermute | solution.py:169
  116.9 92.3 %collective-permute-start.19 = (f32[128,4096]{1,0:T(8,128)}, f32[128,4096]{1,0:T(8,128)}, u32[]{:S(2)}, u32[]{:S(2)}) collective-permute-start(f32[128,4096]{1,0:T(8,128)} %get-tuple-element.51), channel_id=1, source_target_pairs={{2,6},{3,7},{4,0},{5,1},{10,14},{11,15},{12,8},{13,9},{18,22},{19,... | collective-permute-start | bytes 6291464 | tf_op jit(solution)/shard_map/ppermute | solution.py:169
  161.0 5.2 %copy-start.12 = (f32[4096,128]{1,0:T(8,128)}, f32[4096,128]{1,0:T(8,128)S(1)}, u32[]{:S(2)}) copy-start(f32[4096,128]{1,0:T(8,128)S(1)} %collective-permute-done.12.refs_2_) | copy-start | bytes 6291460
  161.0 48.9 %collective-permute-start.13 = (f32[4096,128]{1,0:T(8,128)}, f32[4096,128]{1,0:T(8,128)}, u32[]{:S(2)}, u32[]{:S(2)}) collective-permute-start(f32[4096,128]{1,0:T(8,128)} %get-tuple-element.63.refs_0_), channel_id=1, source_target_pairs={{0,2},{1,3},{6,4},{7,5},{8,10},{9,11},{14,12},{15,13},{16,18},{17,... | collective-permute-start | bytes 6291464 | tf_op jit(solution)/shard_map/ppermute | solution.py:169
  167.4 2.7 collective-permute-start.17
  167.4 4.2 %collective-permute-start.18 = (f32[2048,128]{1,0:T(8,128)S(1)}, f32[2048,128]{1,0:T(8,128)S(1)}, u32[]{:S(2)}, u32[]{:S(2)}) collective-permute-start(f32[2048,128]{1,0:T(8,128)S(1)} %get-tuple-element.75), channel_id=1, source_target_pairs={{2,3},{3,2},{0,1},{1,0},{4,5},{5,4},{6,7},{7,6},{10,11},{11,10},{8... | collective-permute-start | bytes 3145736 | tf_op jit(solution)/shard_map/ppermute | solution.py:169
  186.9 69.1 %copy-start.4 = (f32[128,4096]{1,0:T(8,128)}, f32[128,4096]{1,0:T(8,128)S(1)}, u32[]{:S(2)}) copy-start(f32[128,4096]{1,0:T(8,128)S(1)} %get-tuple-element.49.refs_0_) | copy-start | bytes 6291460
  209.1 2.1 collective-permute-start.20
  209.9 45.9 %collective-permute-start.14 = (f32[4096,128]{1,0:T(8,128)S(1)}, f32[4096,128]{1,0:T(8,128)S(1)}, u32[]{:S(2)}, u32[]{:S(2)}) collective-permute-start(f32[4096,128]{1,0:T(8,128)S(1)} %get-tuple-element.46.refs_0_), channel_id=1, source_target_pairs={{2,0},{3,1},{0,2},{1,3},{4,6},{5,7},{6,4},{7,5},{10,8},{11,9},{8,1... | collective-permute-start | bytes 6291464 | tf_op jit(solution)/shard_map/ppermute | solution.py:169
  211.2 46.7 %collective-permute-start.7 = (f32[4096,128]{1,0:T(8,128)S(1)}, f32[4096,128]{1,0:T(8,128)S(1)}, u32[]{:S(2)}, u32[]{:S(2)}) collective-permute-start(f32[4096,128]{1,0:T(8,128)S(1)} %get-tuple-element.46.refs_0_), channel_id=1, source_target_pairs={{2,3},{3,2},{0,1},{1,0},{4,5},{5,4},{6,7},{7,6},{10,11},{11,10},{8... | collective-permute-start | bytes 6291464 | tf_op jit(solution)/shard_map/ppermute | solution.py:169
  211.2 44.8 %copy-start.6 = (f32[128,4096]{1,0:T(8,128)}, f32[128,4096]{1,0:T(8,128)S(1)}, u32[]{:S(2)}) copy-start(f32[128,4096]{1,0:T(8,128)S(1)} %collective-permute-done.20.refs_1_) | copy-start | bytes 6291460
  255.8 4.4 %copy-start.13 = (f32[4096,128]{1,0:T(8,128)}, f32[4096,128]{1,0:T(8,128)S(1)}, u32[]{:S(2)}) copy-start(f32[4096,128]{1,0:T(8,128)S(1)} %collective-permute-done.14.refs_2_) | copy-start | bytes 6291460
  256.0 2.7 collective-permute-start.21
  256.1 4.1 %collective-permute-start.22 = (f32[2048,128]{1,0:T(8,128)S(1)}, f32[2048,128]{1,0:T(8,128)S(1)}, u32[]{:S(2)}, u32[]{:S(2)}) collective-permute-start(f32[2048,128]{1,0:T(8,128)S(1)} %get-tuple-element.73), channel_id=1, source_target_pairs={{2,3},{3,2},{0,1},{1,0},{4,5},{5,4},{6,7},{7,6},{10,11},{11,10},{8... | collective-permute-start | bytes 3145736 | tf_op jit(solution)/shard_map/ppermute | solution.py:169
  256.6 50.7 %collective-permute-start.23 = (f32[128,4096]{1,0:T(8,128)}, f32[128,4096]{1,0:T(8,128)}, u32[]{:S(2)}, u32[]{:S(2)}) collective-permute-start(f32[128,4096]{1,0:T(8,128)} %get-tuple-element.57), channel_id=1, source_target_pairs={{2,6},{3,7},{4,0},{5,1},{10,14},{11,15},{12,8},{13,9},{18,22},{19,... | collective-permute-start | bytes 6291464 | tf_op jit(solution)/shard_map/ppermute | solution.py:169
  257.9 2.4 copy-start.19
  277.0 31.6 %collective-permute-start.27 = (f32[4096,128]{1,0:T(8,128)}, f32[4096,128]{1,0:T(8,128)}, u32[]{:S(2)}, u32[]{:S(2)}) collective-permute-start(f32[4096,128]{1,0:T(8,128)} %collective-permute-done.13.refs_2_), channel_id=1, source_target_pairs={{2,3},{3,2},{0,1},{1,0},{4,5},{5,4},{6,7},{7,6},{10,11},{11,10},{8... | collective-permute-start | bytes 6291464 | tf_op jit(solution)/shard_map/ppermute | solution.py:169
  277.1 31.5 %collective-permute-start.29 = (f32[4096,128]{1,0:T(8,128)}, f32[4096,128]{1,0:T(8,128)}, u32[]{:S(2)}, u32[]{:S(2)}) collective-permute-start(f32[4096,128]{1,0:T(8,128)} %collective-permute-done.8.refs_6_), channel_id=1, source_target_pairs={{2,3},{3,2},{0,1},{1,0},{4,5},{5,4},{6,7},{7,6},{10,11},{11,10},{8... | collective-permute-start | bytes 6291464 | tf_op jit(solution)/shard_map/ppermute | solution.py:169
  277.5 31.1 %collective-permute-start.28 = (f32[4096,128]{1,0:T(8,128)}, f32[4096,128]{1,0:T(8,128)}, u32[]{:S(2)}, u32[]{:S(2)}) collective-permute-start(f32[4096,128]{1,0:T(8,128)} %collective-permute-done.6.refs_4_), channel_id=1, source_target_pairs={{2,3},{3,2},{0,1},{1,0},{4,5},{5,4},{6,7},{7,6},{10,11},{11,10},{8... | collective-permute-start | bytes 6291464 | tf_op jit(solution)/shard_map/ppermute | solution.py:169
  277.6 31.0 %collective-permute-start.26 = (f32[4096,128]{1,0:T(8,128)}, f32[4096,128]{1,0:T(8,128)}, u32[]{:S(2)}, u32[]{:S(2)}) collective-permute-start(f32[4096,128]{1,0:T(8,128)} %get-tuple-element.63.refs_0_), channel_id=1, source_target_pairs={{2,3},{3,2},{0,1},{1,0},{4,5},{5,4},{6,7},{7,6},{10,11},{11,10},{8... | collective-permute-start | bytes 6291464 | tf_op jit(solution)/shard_map/ppermute | solution.py:169
  307.3 96.2 %collective-permute-start.25 = (f32[128,4096]{1,0:T(8,128)}, f32[128,4096]{1,0:T(8,128)S(1)}, u32[]{:S(2)}, u32[]{:S(2)}) collective-permute-start(f32[128,4096]{1,0:T(8,128)} %get-tuple-element.60), channel_id=1, source_target_pairs={{2,6},{3,7},{4,0},{5,1},{10,14},{11,15},{12,8},{13,9},{18,22},{19,... | collective-permute-start | bytes 6291464 | tf_op jit(solution)/shard_map/ppermute | solution.py:169
  310.7 23.6 %copy-start.3 = (f32[128,4096]{1,0:T(8,128)S(1)}, f32[128,4096]{1,0:T(8,128)}, u32[]{:S(2)}) copy-start(f32[128,4096]{1,0:T(8,128)} %copy-done.2) | copy-start | bytes 6291460
  330.8 71.2 %collective-permute-start.30 = (f32[128,4096]{1,0:T(8,128)}, f32[128,4096]{1,0:T(8,128)S(1)}, u32[]{:S(2)}, u32[]{:S(2)}) collective-permute-start(f32[128,4096]{1,0:T(8,128)} %get-tuple-element.68), channel_id=1, source_target_pairs={{2,0},{3,1},{4,6},{5,7},{10,8},{11,9},{12,14},{13,15},{18,16},{19,... | collective-permute-start | bytes 6291464 | tf_op jit(solution)/shard_map/ppermute | solution.py:169
  332.0 5.5 %copy-start.5 = (f32[128,4096]{1,0:T(8,128)S(1)}, f32[128,4096]{1,0:T(8,128)}, u32[]{:S(2)}) copy-start(f32[128,4096]{1,0:T(8,128)} %copy-done.4) | copy-start | bytes 6291460
  332.1 5.5 %copy-start.7 = (f32[128,4096]{1,0:T(8,128)S(1)}, f32[128,4096]{1,0:T(8,128)}, u32[]{:S(2)}) copy-start(f32[128,4096]{1,0:T(8,128)} %copy-done.6) | copy-start | bytes 6291460
  332.1 71.5 %collective-permute-start.24 = (f32[128,4096]{1,0:T(8,128)}, f32[128,4096]{1,0:T(8,128)}, u32[]{:S(2)}, u32[]{:S(2)}) collective-permute-start(f32[128,4096]{1,0:T(8,128)} %get-tuple-element.58), channel_id=1, source_target_pairs={{2,4},{3,5},{4,2},{5,3},{10,12},{11,13},{12,10},{13,11},{18,20},{1... | collective-permute-start | bytes 6291464 | tf_op jit(solution)/shard_map/ppermute | solution.py:169
  402.0 2.8 copy-start.9
  (6 other events, 8.2 us)

commit v7 on v5

--- a/solution.py
+++ b/solution.py
@@ -8,7 +8,7 @@
 from jax.sharding import PartitionSpec as P
 
 CORES = 2
-BLOCK = 512
+BLOCK = 1024
 SIXTEENTHS = (4, 4, 4, 4)
 
 

time: 409 us -> 410 us (level)
  no operation moved by 1% of the time
where the time goes in v7:
time: 410 us; the launch traced here: 409 us
  waiting for transfers between devices  264 us (64%)
  Pallas kernels  85.6 us (21%)
  starting transfers between devices  43.7 us (11%)
  local copies, waits for them, and re-layouts  14.8 us (4%)
    ppermute x28, waiting for transfers between devices, move(): return lax.ppermute(x, 'col', pairs)  250 us
    pallas_call x4, Pallas kernels, product(): pl.pallas_call(kernel, grid=(modes // block,), in_specs=[pl.BlockSpec((he...  66.8 us
    ppermute x28, starting transfers between devices, move(): return lax.ppermute(x, 'col', pairs)  39.2 us
    ppermute x3, waiting for transfers between devices, shards(): lax.ppermute(line, 'row', [(r, (r + i) % turns) for r in range(turns)])  13 us
    pallas_call x4, Pallas kernels, put(): pl.pallas_call(kernel, grid=(span // block,), in_specs=in_specs, out_spec...  11.8 us
  transfers between devices with their start and end apart: 31, of which 15 were waited for; matrix products, arithmetic and copies ran while one was open for 1% of the time, Pallas kernels for 20%

profile of v7, /device:TPU:0, one launch (start us, length us, event | category | flops | bytes accessed | tf_op | source)
XLA Modules:
  0.0 408.7 jit_solution(9942449229320019109)
XLA Ops:
  0.0 3.9 fusion
  3.9 2.1 collective-permute-start.6
  6.0 4.4 %collective-permute-start.10 = (f32[4096,128]{1,0:T(8,128)S(1)}, f32[4096,128]{1,0:T(8,128)}, u32[]{:S(2)}, u32[]{:S(2)}) collective-permute-start(f32[4096,128]{1,0:T(8,128)S(1)} %get-tuple-element.41.refs_0_), channel_id=1, source_target_pairs={{2,0},{3,1},{0,2},{1,3},{4,6},{5,7},{6,4},{7,5},{10,8},{11,9},{8,1... | collective-permute-start | bytes 6291464 | tf_op jit(solution)/shard_map/ppermute | solution.py:169
  11.1 4.6 %collective-permute-start.2 = (f32[1,32,1024]{2,1,0:T(8,128)S(1)}, f32[1,32,1024]{2,1,0:T(8,128)S(1)}, u32[]{:S(2)}, u32[]{:S(2)}) collective-permute-start(f32[1,32,1024]{2,1,0:T(8,128)S(1)} %copy-done.22), channel_id=1, source_target_pairs={{0,4},{1,5},{6,2},{7,3},{8,12},{9,13},{14,10},{15,11},{16,20},{17,... | collective-permute-start | bytes 393224 | tf_op jit(solution)/shard_map/ppermute | solution.py:169
  15.9 43.4 %collective-permute-done.2 = f32[1,32,1024]{2,1,0:T(8,128)S(1)} collective-permute-done((f32[1,32,1024]{2,1,0:T(8,128)S(1)}, f32[1,32,1024]{2,1,0:T(8,128)S(1)}, u32[]{:S(2)}, u32[]{:S(2)}) %collective-permute-start.2) | collective-permute-done | bytes 131104 | tf_op jit(solution)/shard_map/ppermute | solution.py:169
  59.3 1.4 collective-permute-done
  60.7 1.5 collective-permute-start.3
  62.8 5.6 %collective-permute-start.8 = (f32[4096,128]{1,0:T(8,128)}, f32[4096,128]{1,0:T(8,128)}, u32[]{:S(2)}, u32[]{:S(2)}) collective-permute-start(f32[4096,128]{1,0:T(8,128)} %get-tuple-element.63.refs_0_), channel_id=1, source_target_pairs={{0,4},{1,5},{6,2},{7,3},{8,12},{9,13},{14,10},{15,11},{16,20},{17,... | collective-permute-start | bytes 6291464 | tf_op jit(solution)/shard_map/ppermute | solution.py:169
  68.4 1.5 collective-permute-start.4
  70.0 4.3 %collective-permute-done.3.refs_1_ = f32[4,1,32,1024]{3,2,1,0:T(8,128)S(1)} collective-permute-done((f32[4,1,32,1024]{3,2,1,0:T(8,128)S(1)}, f32[4,1,32,1024]{3,2,1,0:T(8,128)S(1)}, u32[]{:S(2)}, u32[]{:S(2)}) %collective-permute-start.3) | collective-permute-done | bytes 524320 | tf_op jit(solution)/shard_map/ppermute | solution.py:222
  74.3 1.4 collective-permute-start.5
  77.1 8.4 %collective-permute-done.4.refs_2_ = f32[4,1,32,1024]{3,2,1,0:T(8,128)} collective-permute-done((f32[4,1,32,1024]{3,2,1,0:T(8,128)S(1)}, f32[4,1,32,1024]{3,2,1,0:T(8,128)}, u32[]{:S(2)}, u32[]{:S(2)}) %collective-permute-start.4) | collective-permute-done | bytes 524320 | tf_op jit(solution)/shard_map/ppermute | solution.py:222
  85.8 3.9 shard_map.46
  89.8 2.6 fusion.1
  92.4 16.7 %shard_map.47 = (f32[128,4096]{1,0:T(8,128)S(1)}, f32[128,4096]{1,0:T(8,128)S(1)}, f32[128,4096]{1,0:T(8,128)}) custom-call(bf16[384,512]{1,0:T(8,128)(2,1)S(1)} %copy-done, bf16[384,512]{1,0:T(8,128)(2,1)S(1)} %copy-done.1, f32[4096,128]{1,0:T(8,128)} %copy-done.14, f32[4096,128]{1,0:T(8,128)} %collective-permute-done.9.refs_1_, ...), custom_call_target="tpu_custom_call" | custom-call | tf_op jit(solution)/shard_map/pallas_call | solution.py:111
  109.1 3.4 collective-permute-done.8.refs_6_
  112.5 3.5 collective-permute-start.12
  116.0 0.8 collective-permute-start.16
  116.9 1.3 collective-permute-start.19
  118.2 42.8 %collective-permute-done.12.refs_2_ = f32[4096,128]{1,0:T(8,128)S(1)} collective-permute-done((f32[4096,128]{1,0:T(8,128)S(1)}, f32[4096,128]{1,0:T(8,128)S(1)}, u32[]{:S(2)}, u32[]{:S(2)}) %collective-permute-start.12) | collective-permute-done | bytes 2097184 | tf_op jit(solution)/shard_map/ppermute | solution.py:169
  161.0 5.1 %collective-permute-start.13 = (f32[4096,128]{1,0:T(8,128)}, f32[4096,128]{1,0:T(8,128)}, u32[]{:S(2)}, u32[]{:S(2)}) collective-permute-start(f32[4096,128]{1,0:T(8,128)} %get-tuple-element.63.refs_0_), channel_id=1, source_target_pairs={{0,2},{1,3},{6,4},{7,5},{8,10},{9,11},{14,12},{15,13},{16,18},{17,... | collective-permute-start | bytes 6291464 | tf_op jit(solution)/shard_map/ppermute | solution.py:169
  166.2 1.2 copy-done.2
  167.9 2.1 collective-permute-done.17.refs_3_
  170.1 1.5 collective-permute-done.18.refs_4_
  171.6 15.1 %shard_map.48 = (f32[128,4096]{1,0:T(8,128)S(1)}, f32[128,4096]{1,0:T(8,128)}, f32[128,4096]{1,0:T(8,128)}) custom-call(bf16[384,512]{1,0:T(8,128)(2,1)S(1)} %copy-done, bf16[384,512]{1,0:T(8,128)(2,1)S(1)} %copy-done.1, f32[4096,128]{1,0:T(8,128)} %copy-done.16, f32[4096,128]{1,0:T(8,128)} %copy-done.18, f32[4096,128]{1,0:T(8,128)} %copy-done.12, ...), custom_call_target="tpu_custom_call" | custom-call | tf_op jit(solution)/shard_map/pallas_call | solution.py:111
  186.7 22.5 %collective-permute-done.19.refs_2_ = f32[128,4096]{1,0:T(8,128)} collective-permute-done((f32[128,4096]{1,0:T(8,128)}, f32[128,4096]{1,0:T(8,128)}, u32[]{:S(2)}, u32[]{:S(2)}) %collective-permute-start.19) | collective-permute-done | bytes 2097184 | tf_op jit(solution)/shard_map/ppermute | solution.py:169
  209.1 0.8 collective-permute-start.20
  209.9 1.3 collective-permute-start.14
  211.2 44.6 %collective-permute-done.14.refs_2_ = f32[4096,128]{1,0:T(8,128)S(1)} collective-permute-done((f32[4096,128]{1,0:T(8,128)S(1)}, f32[4096,128]{1,0:T(8,128)S(1)}, u32[]{:S(2)}, u32[]{:S(2)}) %collective-permute-start.14) | collective-permute-done | bytes 2097184 | tf_op jit(solution)/shard_map/ppermute | solution.py:169
  256.6 1.3 collective-permute-start.23
  257.9 0.8 collective-permute-done.21.refs_3_
  258.7 1.5 collective-permute-done.22.refs_4_
  260.2 15.1 %shard_map.49 = (f32[128,4096]{1,0:T(8,128)S(1)}, f32[128,4096]{1,0:T(8,128)}, f32[128,4096]{1,0:T(8,128)}) custom-call(bf16[384,512]{1,0:T(8,128)(2,1)S(1)} %copy-done, bf16[384,512]{1,0:T(8,128)(2,1)S(1)} %copy-done.1, f32[4096,128]{1,0:T(8,128)} %copy-done.15, f32[4096,128]{1,0:T(8,128)} %copy-done.19, f32[4096,128]{1,0:T(8,128)} %copy-done.13, ...), custom_call_target="tpu_custom_call" | custom-call | tf_op jit(solution)/shard_map/pallas_call | solution.py:111
  275.3 1.4 copy-done.8
  279.1 3.0 shard_map.50
  282.1 25.2 %collective-permute-done.23.refs_2_ = f32[128,4096]{1,0:T(8,128)} collective-permute-done((f32[128,4096]{1,0:T(8,128)}, f32[128,4096]{1,0:T(8,128)}, u32[]{:S(2)}, u32[]{:S(2)}) %collective-permute-start.23) | collective-permute-done | bytes 2097184 | tf_op jit(solution)/shard_map/ppermute | solution.py:169
  307.3 1.5 collective-permute-start.25
  308.8 1.0 copy-done.10
  309.8 1.0 copy-done.11
  310.9 20.0 %shard_map.51 = (f32[128,4096]{1,0:T(8,128)S(1)}, f32[128,4096]{1,0:T(8,128)}) custom-call(bf16[256,1024]{1,0:T(8,128)(2,1)S(1)} %copy-done.10, bf16[256,1024]{1,0:T(8,128)(2,1)S(1)} %copy-done.11, f32[4096,128]{1,0:T(8,128)} %get-tuple-element.63.refs_0_, f32[4096,128]{1,0:T(8,128)} %collective-permute-done.26.refs_1_, ...), custom_call_target="tpu_custom_call" | custom-call | tf_op jit(solution)/shard_map/pallas_call | solution.py:111
  330.9 1.3 collective-permute-start.30
  332.2 2.2 collective-permute-start.24
  334.4 3.2 shard_map.52.refs_3_
  337.6 3.2 shard_map.53.refs_2_
  340.8 61.2 %collective-permute-done.30.refs_1_ = f32[128,4096]{1,0:T(8,128)S(1)} collective-permute-done((f32[128,4096]{1,0:T(8,128)}, f32[128,4096]{1,0:T(8,128)S(1)}, u32[]{:S(2)}, u32[]{:S(2)}) %collective-permute-start.30) | collective-permute-done | bytes 2097184 | tf_op jit(solution)/shard_map/ppermute | solution.py:169
  402.0 1.5 shard_map.54.refs_3_
  403.5 1.3 copy-done.21
  404.8 3.8 shard_map.55
  (85 shorter events, 6.9 us)
Async XLA Ops:
  0.0 10.5 %copy-start.22 = (f32[1,32,1024]{2,1,0:T(8,128)S(1)}, f32[1,32,1024]{2,1,0:T(8,128)}, u32[]{:S(2)}) copy-start(f32[1,32,1024]{2,1,0:T(8,128)} %param.4) | copy-start | bytes 393220
  3.9 88.5 %copy-start.14 = (f32[4096,128]{1,0:T(8,128)}, f32[4096,128]{1,0:T(8,128)S(1)}, u32[]{:S(2)}) copy-start(f32[4096,128]{1,0:T(8,128)S(1)} %get-tuple-element.41.refs_0_) | copy-start | bytes 6291460
  3.9 58.4 %collective-permute-start.6 = (f32[4096,128]{1,0:T(8,128)}, f32[4096,128]{1,0:T(8,128)}, u32[]{:S(2)}, u32[]{:S(2)}) collective-permute-start(f32[4096,128]{1,0:T(8,128)} %get-tuple-element.63.refs_0_), channel_id=1, source_target_pairs={{2,4},{3,5},{4,2},{5,3},{10,12},{11,13},{12,10},{13,11},{18,20},{1... | collective-permute-start | bytes 6291464 | tf_op jit(solution)/shard_map/ppermute | solution.py:169
  6.0 56.3 %collective-permute-start.10 = (f32[4096,128]{1,0:T(8,128)S(1)}, f32[4096,128]{1,0:T(8,128)}, u32[]{:S(2)}, u32[]{:S(2)}) collective-permute-start(f32[4096,128]{1,0:T(8,128)S(1)} %get-tuple-element.41.refs_0_), channel_id=1, source_target_pairs={{2,0},{3,1},{0,2},{1,3},{4,6},{5,7},{6,4},{7,5},{10,8},{11,9},{8,1... | collective-permute-start | bytes 6291464 | tf_op jit(solution)/shard_map/ppermute | solution.py:169
  10.5 5.4 %collective-permute-start.1 = (f32[1,32,1024]{2,1,0:T(8,128)S(1)}, f32[1,32,1024]{2,1,0:T(8,128)S(1)}, u32[]{:S(2)}, u32[]{:S(2)}) collective-permute-start(f32[1,32,1024]{2,1,0:T(8,128)S(1)} %copy-done.22), channel_id=1, source_target_pairs={{2,4},{3,5},{4,2},{5,3},{10,12},{11,13},{12,10},{13,11},{18,20},{1... | collective-permute-start | bytes 393224 | tf_op jit(solution)/shard_map/ppermute | solution.py:169
  11.1 48.2 %collective-permute-start.2 = (f32[1,32,1024]{2,1,0:T(8,128)S(1)}, f32[1,32,1024]{2,1,0:T(8,128)S(1)}, u32[]{:S(2)}, u32[]{:S(2)}) collective-permute-start(f32[1,32,1024]{2,1,0:T(8,128)S(1)} %copy-done.22), channel_id=1, source_target_pairs={{0,4},{1,5},{6,2},{7,3},{8,12},{9,13},{14,10},{15,11},{16,20},{17,... | collective-permute-start | bytes 393224 | tf_op jit(solution)/shard_map/ppermute | solution.py:169
  15.8 44.9 %collective-permute-start = (f32[1,32,1024]{2,1,0:T(8,128)S(1)}, f32[1,32,1024]{2,1,0:T(8,128)S(1)}, u32[]{:S(2)}, u32[]{:S(2)}) collective-permute-start(f32[1,32,1024]{2,1,0:T(8,128)S(1)} %copy-done.22), channel_id=1, source_target_pairs={{2,0},{3,1},{0,2},{1,3},{4,6},{5,7},{6,4},{7,5},{10,8},{11,9},{8,1... | collective-permute-start | bytes 393224 | tf_op jit(solution)/shard_map/ppermute | solution.py:169
  60.7 25.1 %copy-start.17 = (f32[4,1,32,1024]{3,2,1,0:T(8,128)}, f32[4,1,32,1024]{3,2,1,0:T(8,128)S(1)}, u32[]{:S(2)}) copy-start(f32[4,1,32,1024]{3,2,1,0:T(8,128)S(1)} %pad_maximum_fusion.refs_0_) | copy-start | bytes 1572868
  60.7 13.5 %collective-permute-start.3 = (f32[4,1,32,1024]{3,2,1,0:T(8,128)S(1)}, f32[4,1,32,1024]{3,2,1,0:T(8,128)S(1)}, u32[]{:S(2)}, u32[]{:S(2)}) collective-permute-start(f32[4,1,32,1024]{3,2,1,0:T(8,128)S(1)} %pad_maximum_fusion.refs_0_), channel_id=1, source_target_pairs={{0,8},{8,16},{16,24},{24,0},{1,9},{9,17},{17,25},{25,1},{2,10},{10... | collective-permute-start | bytes 1572872 | tf_op jit(solution)/shard_map/ppermute | solution.py:222
  62.3 30.1 %collective-permute-start.11 = (f32[4096,128]{1,0:T(8,128)}, f32[4096,128]{1,0:T(8,128)}, u32[]{:S(2)}, u32[]{:S(2)}) collective-permute-start(f32[4096,128]{1,0:T(8,128)} %collective-permute-done.10.refs_2_), channel_id=1, source_target_pairs={{2,3},{3,2},{0,1},{1,0},{4,5},{5,4},{6,7},{7,6},{10,11},{11,10},{8... | collective-permute-start | bytes 6291464 | tf_op jit(solution)/shard_map/ppermute | solution.py:169
  62.3 30.1 %collective-permute-start.9 = (f32[4096,128]{1,0:T(8,128)S(1)}, f32[4096,128]{1,0:T(8,128)}, u32[]{:S(2)}, u32[]{:S(2)}) collective-permute-start(f32[4096,128]{1,0:T(8,128)S(1)} %get-tuple-element.41.refs_0_), channel_id=1, source_target_pairs={{2,3},{3,2},{0,1},{1,0},{4,5},{5,4},{6,7},{7,6},{10,11},{11,10},{8... | collective-permute-start | bytes 6291464 | tf_op jit(solution)/shard_map/ppermute | solution.py:169
  62.8 49.7 %collective-permute-start.8 = (f32[4096,128]{1,0:T(8,128)}, f32[4096,128]{1,0:T(8,128)}, u32[]{:S(2)}, u32[]{:S(2)}) collective-permute-start(f32[4096,128]{1,0:T(8,128)} %get-tuple-element.63.refs_0_), channel_id=1, source_target_pairs={{0,4},{1,5},{6,2},{7,3},{8,12},{9,13},{14,10},{15,11},{16,20},{17,... | collective-permute-start | bytes 6291464 | tf_op jit(solution)/shard_map/ppermute | solution.py:169
  68.4 17.1 %collective-permute-start.4 = (f32[4,1,32,1024]{3,2,1,0:T(8,128)S(1)}, f32[4,1,32,1024]{3,2,1,0:T(8,128)}, u32[]{:S(2)}, u32[]{:S(2)}) collective-permute-start(f32[4,1,32,1024]{3,2,1,0:T(8,128)S(1)} %pad_maximum_fusion.refs_0_), channel_id=1, source_target_pairs={{0,16},{8,24},{16,0},{24,8},{1,17},{9,25},{17,1},{25,9},{2,18},{10... | collective-permute-start | bytes 1572872 | tf_op jit(solution)/shard_map/ppermute | solution.py:222
  74.3 11.6 %copy-start.20 = (f32[4,1,32,1024]{3,2,1,0:T(8,128)}, f32[4,1,32,1024]{3,2,1,0:T(8,128)S(1)}, u32[]{:S(2)}) copy-start(f32[4,1,32,1024]{3,2,1,0:T(8,128)S(1)} %collective-permute-done.3.refs_1_) | copy-start | bytes 1572868
  74.3 11.6 %collective-permute-start.5 = (f32[4,1,32,1024]{3,2,1,0:T(8,128)S(1)}, f32[4,1,32,1024]{3,2,1,0:T(8,128)}, u32[]{:S(2)}, u32[]{:S(2)}) collective-permute-start(f32[4,1,32,1024]{3,2,1,0:T(8,128)S(1)} %pad_maximum_fusion.refs_0_), channel_id=1, source_target_pairs={{0,24},{8,0},{16,8},{24,16},{1,25},{9,1},{17,9},{25,17},{2,26},{10... | collective-permute-start | bytes 1572872 | tf_op jit(solution)/shard_map/ppermute | solution.py:222
  89.8 2.6 copy-start
  89.8 2.6 copy-start.1
  92.4 24.4 %copy-start.16 = (f32[4096,128]{1,0:T(8,128)}, f32[4096,128]{1,0:T(8,128)S(1)}, u32[]{:S(2)}) copy-start(f32[4096,128]{1,0:T(8,128)S(1)} %get-tuple-element.44.refs_0_) | copy-start | bytes 6291460
  92.4 118.8 %copy-start.15 = (f32[4096,128]{1,0:T(8,128)}, f32[4096,128]{1,0:T(8,128)S(1)}, u32[]{:S(2)}) copy-start(f32[4096,128]{1,0:T(8,128)S(1)} %get-tuple-element.46.refs_0_) | copy-start | bytes 6291460
  112.5 48.5 %collective-permute-start.12 = (f32[4096,128]{1,0:T(8,128)S(1)}, f32[4096,128]{1,0:T(8,128)S(1)}, u32[]{:S(2)}, u32[]{:S(2)}) collective-permute-start(f32[4096,128]{1,0:T(8,128)S(1)} %get-tuple-element.44.refs_0_), channel_id=1, source_target_pairs={{2,0},{3,1},{0,2},{1,3},{4,6},{5,7},{6,4},{7,5},{10,8},{11,9},{8,1... | collective-permute-start | bytes 6291464 | tf_op jit(solution)/shard_map/ppermute | solution.py:169
  116.0 50.1 %collective-permute-start.16 = (f32[128,4096]{1,0:T(8,128)S(1)}, f32[128,4096]{1,0:T(8,128)S(1)}, u32[]{:S(2)}, u32[]{:S(2)}) collective-permute-start(f32[128,4096]{1,0:T(8,128)S(1)} %get-tuple-element.47), channel_id=1, source_target_pairs={{2,4},{3,5},{4,2},{5,3},{10,12},{11,13},{12,10},{13,11},{18,20},{1... | collective-permute-start | bytes 6291464 | tf_op jit(solution)/shard_map/ppermute | solution.py:169
  116.8 51.1 %collective-permute-start.15 = (f32[4096,128]{1,0:T(8,128)S(1)}, f32[4096,128]{1,0:T(8,128)S(1)}, u32[]{:S(2)}, u32[]{:S(2)}) collective-permute-start(f32[4096,128]{1,0:T(8,128)S(1)} %get-tuple-element.44.refs_0_), channel_id=1, source_target_pairs={{2,3},{3,2},{0,1},{1,0},{4,5},{5,4},{6,7},{7,6},{10,11},{11,10},{8... | collective-permute-start | bytes 6291464 | tf_op jit(solution)/shard_map/ppermute | solution.py:169
  116.9 92.3 %collective-permute-start.19 = (f32[128,4096]{1,0:T(8,128)}, f32[128,4096]{1,0:T(8,128)}, u32[]{:S(2)}, u32[]{:S(2)}) collective-permute-start(f32[128,4096]{1,0:T(8,128)} %get-tuple-element.51), channel_id=1, source_target_pairs={{2,6},{3,7},{4,0},{5,1},{10,14},{11,15},{12,8},{13,9},{18,22},{19,... | collective-permute-start | bytes 6291464 | tf_op jit(solution)/shard_map/ppermute | solution.py:169
  161.0 5.2 %copy-start.12 = (f32[4096,128]{1,0:T(8,128)}, f32[4096,128]{1,0:T(8,128)S(1)}, u32[]{:S(2)}) copy-start(f32[4096,128]{1,0:T(8,128)S(1)} %collective-permute-done.12.refs_2_) | copy-start | bytes 6291460
  161.0 48.9 %collective-permute-start.13 = (f32[4096,128]{1,0:T(8,128)}, f32[4096,128]{1,0:T(8,128)}, u32[]{:S(2)}, u32[]{:S(2)}) collective-permute-start(f32[4096,128]{1,0:T(8,128)} %get-tuple-element.63.refs_0_), channel_id=1, source_target_pairs={{0,2},{1,3},{6,4},{7,5},{8,10},{9,11},{14,12},{15,13},{16,18},{17,... | collective-permute-start | bytes 6291464 | tf_op jit(solution)/shard_map/ppermute | solution.py:169
  167.4 2.7 collective-permute-start.17
  167.4 4.2 %collective-permute-start.18 = (f32[2048,128]{1,0:T(8,128)S(1)}, f32[2048,128]{1,0:T(8,128)S(1)}, u32[]{:S(2)}, u32[]{:S(2)}) collective-permute-start(f32[2048,128]{1,0:T(8,128)S(1)} %get-tuple-element.75), channel_id=1, source_target_pairs={{2,3},{3,2},{0,1},{1,0},{4,5},{5,4},{6,7},{7,6},{10,11},{11,10},{8... | collective-permute-start | bytes 3145736 | tf_op jit(solution)/shard_map/ppermute | solution.py:169
  186.7 69.3 %copy-start.4 = (f32[128,4096]{1,0:T(8,128)}, f32[128,4096]{1,0:T(8,128)S(1)}, u32[]{:S(2)}) copy-start(f32[128,4096]{1,0:T(8,128)S(1)} %get-tuple-element.49.refs_0_) | copy-start | bytes 6291460
  209.1 2.1 collective-permute-start.20
  209.9 45.9 %collective-permute-start.14 = (f32[4096,128]{1,0:T(8,128)S(1)}, f32[4096,128]{1,0:T(8,128)S(1)}, u32[]{:S(2)}, u32[]{:S(2)}) collective-permute-start(f32[4096,128]{1,0:T(8,128)S(1)} %get-tuple-element.46.refs_0_), channel_id=1, source_target_pairs={{2,0},{3,1},{0,2},{1,3},{4,6},{5,7},{6,4},{7,5},{10,8},{11,9},{8,1... | collective-permute-start | bytes 6291464 | tf_op jit(solution)/shard_map/ppermute | solution.py:169
  211.2 46.7 %collective-permute-start.7 = (f32[4096,128]{1,0:T(8,128)S(1)}, f32[4096,128]{1,0:T(8,128)S(1)}, u32[]{:S(2)}, u32[]{:S(2)}) collective-permute-start(f32[4096,128]{1,0:T(8,128)S(1)} %get-tuple-element.46.refs_0_), channel_id=1, source_target_pairs={{2,3},{3,2},{0,1},{1,0},{4,5},{5,4},{6,7},{7,6},{10,11},{11,10},{8... | collective-permute-start | bytes 6291464 | tf_op jit(solution)/shard_map/ppermute | solution.py:169
  211.2 44.8 %copy-start.6 = (f32[128,4096]{1,0:T(8,128)}, f32[128,4096]{1,0:T(8,128)S(1)}, u32[]{:S(2)}) copy-start(f32[128,4096]{1,0:T(8,128)S(1)} %collective-permute-done.20.refs_1_) | copy-start | bytes 6291460
  255.8 4.4 %copy-start.13 = (f32[4096,128]{1,0:T(8,128)}, f32[4096,128]{1,0:T(8,128)S(1)}, u32[]{:S(2)}) copy-start(f32[4096,128]{1,0:T(8,128)S(1)} %collective-permute-done.14.refs_2_) | copy-start | bytes 6291460
  256.0 2.7 collective-permute-start.21
  256.1 4.1 %collective-permute-start.22 = (f32[2048,128]{1,0:T(8,128)S(1)}, f32[2048,128]{1,0:T(8,128)S(1)}, u32[]{:S(2)}, u32[]{:S(2)}) collective-permute-start(f32[2048,128]{1,0:T(8,128)S(1)} %get-tuple-element.73), channel_id=1, source_target_pairs={{2,3},{3,2},{0,1},{1,0},{4,5},{5,4},{6,7},{7,6},{10,11},{11,10},{8... | collective-permute-start | bytes 3145736 | tf_op jit(solution)/shard_map/ppermute | solution.py:169
  256.6 50.7 %collective-permute-start.23 = (f32[128,4096]{1,0:T(8,128)}, f32[128,4096]{1,0:T(8,128)}, u32[]{:S(2)}, u32[]{:S(2)}) collective-permute-start(f32[128,4096]{1,0:T(8,128)} %get-tuple-element.57), channel_id=1, source_target_pairs={{2,6},{3,7},{4,0},{5,1},{10,14},{11,15},{12,8},{13,9},{18,22},{19,... | collective-permute-start | bytes 6291464 | tf_op jit(solution)/shard_map/ppermute | solution.py:169
  257.9 2.4 copy-start.19
  276.7 32.1 %collective-permute-start.27 = (f32[4096,128]{1,0:T(8,128)}, f32[4096,128]{1,0:T(8,128)}, u32[]{:S(2)}, u32[]{:S(2)}) collective-permute-start(f32[4096,128]{1,0:T(8,128)} %collective-permute-done.13.refs_2_), channel_id=1, source_target_pairs={{2,3},{3,2},{0,1},{1,0},{4,5},{5,4},{6,7},{7,6},{10,11},{11,10},{8... | collective-permute-start | bytes 6291464 | tf_op jit(solution)/shard_map/ppermute | solution.py:169
  276.9 31.9 %collective-permute-start.29 = (f32[4096,128]{1,0:T(8,128)}, f32[4096,128]{1,0:T(8,128)}, u32[]{:S(2)}, u32[]{:S(2)}) collective-permute-start(f32[4096,128]{1,0:T(8,128)} %collective-permute-done.8.refs_6_), channel_id=1, source_target_pairs={{2,3},{3,2},{0,1},{1,0},{4,5},{5,4},{6,7},{7,6},{10,11},{11,10},{8... | collective-permute-start | bytes 6291464 | tf_op jit(solution)/shard_map/ppermute | solution.py:169
  277.2 31.6 %collective-permute-start.28 = (f32[4096,128]{1,0:T(8,128)}, f32[4096,128]{1,0:T(8,128)}, u32[]{:S(2)}, u32[]{:S(2)}) collective-permute-start(f32[4096,128]{1,0:T(8,128)} %collective-permute-done.6.refs_4_), channel_id=1, source_target_pairs={{2,3},{3,2},{0,1},{1,0},{4,5},{5,4},{6,7},{7,6},{10,11},{11,10},{8... | collective-permute-start | bytes 6291464 | tf_op jit(solution)/shard_map/ppermute | solution.py:169
  277.4 31.4 %collective-permute-start.26 = (f32[4096,128]{1,0:T(8,128)}, f32[4096,128]{1,0:T(8,128)}, u32[]{:S(2)}, u32[]{:S(2)}) collective-permute-start(f32[4096,128]{1,0:T(8,128)} %get-tuple-element.63.refs_0_), channel_id=1, source_target_pairs={{2,3},{3,2},{0,1},{1,0},{4,5},{5,4},{6,7},{7,6},{10,11},{11,10},{8... | collective-permute-start | bytes 6291464 | tf_op jit(solution)/shard_map/ppermute | solution.py:169
  307.3 96.2 %collective-permute-start.25 = (f32[128,4096]{1,0:T(8,128)}, f32[128,4096]{1,0:T(8,128)S(1)}, u32[]{:S(2)}, u32[]{:S(2)}) collective-permute-start(f32[128,4096]{1,0:T(8,128)} %get-tuple-element.60), channel_id=1, source_target_pairs={{2,6},{3,7},{4,0},{5,1},{10,14},{11,15},{12,8},{13,9},{18,22},{19,... | collective-permute-start | bytes 6291464 | tf_op jit(solution)/shard_map/ppermute | solution.py:169
  310.9 23.5 %copy-start.3 = (f32[128,4096]{1,0:T(8,128)S(1)}, f32[128,4096]{1,0:T(8,128)}, u32[]{:S(2)}) copy-start(f32[128,4096]{1,0:T(8,128)} %copy-done.2) | copy-start | bytes 6291460
  330.9 71.1 %collective-permute-start.30 = (f32[128,4096]{1,0:T(8,128)}, f32[128,4096]{1,0:T(8,128)S(1)}, u32[]{:S(2)}, u32[]{:S(2)}) collective-permute-start(f32[128,4096]{1,0:T(8,128)} %get-tuple-element.68), channel_id=1, source_target_pairs={{2,0},{3,1},{4,6},{5,7},{10,8},{11,9},{12,14},{13,15},{18,16},{19,... | collective-permute-start | bytes 6291464 | tf_op jit(solution)/shard_map/ppermute | solution.py:169
  332.2 5.5 %copy-start.5 = (f32[128,4096]{1,0:T(8,128)S(1)}, f32[128,4096]{1,0:T(8,128)}, u32[]{:S(2)}) copy-start(f32[128,4096]{1,0:T(8,128)} %copy-done.4) | copy-start | bytes 6291460
  332.2 5.5 %copy-start.7 = (f32[128,4096]{1,0:T(8,128)S(1)}, f32[128,4096]{1,0:T(8,128)}, u32[]{:S(2)}) copy-start(f32[128,4096]{1,0:T(8,128)} %copy-done.6) | copy-start | bytes 6291460
  332.2 71.4 %collective-permute-start.24 = (f32[128,4096]{1,0:T(8,128)}, f32[128,4096]{1,0:T(8,128)}, u32[]{:S(2)}, u32[]{:S(2)}) collective-permute-start(f32[128,4096]{1,0:T(8,128)} %get-tuple-element.58), channel_id=1, source_target_pairs={{2,4},{3,5},{4,2},{5,3},{10,12},{11,13},{12,10},{13,11},{18,20},{1... | collective-permute-start | bytes 6291464 | tf_op jit(solution)/shard_map/ppermute | solution.py:169
  402.0 2.8 copy-start.9
  (6 other events, 8.2 us)
